TPU v7x, 512 devices: a whole 4x8x8 slice. The times are simulated.
512 devices in a mesh: row: 8 (over y), col: 16 (over z_lo, x), layer: 4 (over z_hi, core).
Axes of the slice: x: 4, y: 8, z: 8 (z_hi: 2, z_lo: 4; z = z_hi * 4 + z_lo), core: 2. Of those that a mesh axis runs over, the one named last changes fastest.
Arguments:
- root_values: bfloat16 [128, 4, 6, 128, 128], P('col', 'layer'), may hold values from -0.5 to 0.5
- root_columns: int32 [128, 4, 6], P('col', 'layer'), may hold values from 0 to 127, as said below
- root_counts: int32 [128, 4], P('col', 'layer'), may hold values from 1 to 6, as said below
- fock_values: bfloat16 [128, 4, 6, 128, 128], P('col', 'layer'), may hold values from -0.5 to 0.5
- fock_columns: int32 [128, 4, 6], P('col', 'layer'), may hold values from 0 to 127, as said below
- fock_counts: int32 [128, 4], P('col', 'layer'), may hold values from 1 to 6, as said below
- density_values: bfloat16 [128, 4, 6, 128, 128], P('col', 'layer'), may hold values from -0.5 to 0.5
- density_columns: int32 [128, 4, 6], P('col', 'layer'), may hold values from 0 to 127, as said below
- density_counts: int32 [128, 4], P('col', 'layer'), may hold values from 1 to 6, as said below
Outputs:
- fock_slab: bfloat16 [16384, 2048], P(('col', 'layer'), 'row')
- purified_slab: bfloat16 [16384, 2048], P(('col', 'layer'), 'row')
- energy_slab: bfloat16 [16384, 2048], P(('col', 'layer'), 'row')
Inputs may be any that keep to these rules, and one draw needn't show every extreme that they name: `root_columns`: for each block row i and quarter q the 6 entries are distinct block columns of quarter q; entries at k >= the count are block columns too and their values are ignored. `fock_columns`: for each block row i and quarter q the 6 entries are distinct block columns of quarter q; entries at k >= the count are block columns too and their values are ignored. `density_columns`: for each block row i and quarter q the 6 entries are distinct block columns of quarter q; entries at k >= the count are block columns too and their values are ignored. `root_counts`: some entry equals 6 in every draw. `fock_counts`: some entry equals 6 in every draw. `density_counts`: some entry equals 6 in every draw.
All inputs are finite; a program needn't handle non-finite values.
Results may differ from a plain program's by a relative error of at most 0.018.
Values may be sent and summed in bfloat16 or wider, within the bound.
No kernel may reach another device: no remote copies, remote signals or barrier semaphores. Data moves between devices by JAX's collectives and lax.ppermute only.
A program may use at most 64 MiB of HBM per device.

v0:
```python
import jax
import jax.numpy as jnp
from jax import lax
from jax.sharding import Mesh
from jax.sharding import PartitionSpec as P

WS = 256
COL = ("col_0", "col_1")
COL_LAYER = ("col_0", "col_1", "layer")


def split_up(shard, dim, count):
    before, after = (shard.shape[:dim], shard.shape[dim + 1 :])
    return jnp.moveaxis(shard.reshape(*before, count, -1, *after), dim, 0)


def sent_and_summed(shard, axis, dim):
    pieces = split_up(shard, dim, lax.axis_size(axis))
    arrived = lax.all_to_all(pieces, axis, split_axis=0, concat_axis=0, tiled=True)
    return arrived.astype(jnp.float32).sum(axis=0)


def in_order(pieces, dim):
    shape = list(pieces.shape[1:])
    shape[dim] *= pieces.shape[0]
    return jnp.moveaxis(pieces, 0, dim).reshape(shape)


def gather_in_order(shard, axes, order):
    pieces = shard[None]
    for k in order:
        pieces = lax.all_gather(pieces, axes[k], axis=0, tiled=True)
    held = [lax.axis_size(axes[k]) for k in reversed(order)]
    pieces = pieces.reshape(*held, *shard.shape)
    turned = sorted(range(len(order)), key=lambda place: order[len(order) - 1 - place])
    return pieces.transpose(*turned, *range(len(order), pieces.ndim)).reshape(-1, *shard.shape)


def gathered_by_axis(shard, axes, order, dim):
    return in_order(gather_in_order(shard, axes, order), dim)


def extract_slab(values, columns, counts):
    block_size = values.shape[-1]
    per_device = WS // block_size
    first_block = lax.axis_index("row") * per_device
    slot_ids = jnp.arange(values.shape[2], dtype=jnp.int32)
    usable = slot_ids[None, None, :] < counts[:, :, None]
    targets = first_block + jnp.arange(per_device, dtype=jnp.int32)
    onehot = ((columns[..., None] == targets) & usable[..., None]).astype(jnp.bfloat16)
    pieces = jnp.einsum("rqkt,rqkab->ratb", onehot, values, preferred_element_type=jnp.float32)
    pieces = pieces.reshape(values.shape[0] * block_size, WS)
    return sent_and_summed(pieces.astype(jnp.bfloat16), "layer", 0).astype(jnp.bfloat16)


def layer_total(partial_value):
    return sent_and_summed(partial_value.astype(jnp.bfloat16), "layer", 0)


def sparse_product(values, columns, counts, slab):
    block_size = values.shape[-1]
    row_blocks = values.shape[0]
    slot_count = values.shape[2]
    width = slab.shape[1]
    group_size = row_blocks // lax.axis_size("layer")
    gathered = gathered_by_axis(slab, COL, (0, 1), 0)
    blocks = gathered.reshape(-1, block_size, width)
    local_columns = columns[:, 0, :]
    positions = local_columns // row_blocks * group_size + local_columns % group_size
    usable = jnp.arange(slot_count, dtype=jnp.int32)[None, :] < counts[:, 0][:, None]
    masked_tiles = values[:, 0] * usable[:, :, None, None].astype(jnp.bfloat16)
    picked = jnp.take(blocks, positions, axis=0)
    partial_value = jnp.einsum(
        "rkab,rkbw->raw", masked_tiles, picked, preferred_element_type=jnp.float32
    )
    rounded = partial_value.reshape(row_blocks * block_size, width).astype(jnp.bfloat16)
    return layer_total(rounded.astype(jnp.float32))


def on_device(
    root_values,
    root_columns,
    root_counts,
    fock_values,
    fock_columns,
    fock_counts,
    density_values,
    density_columns,
    density_counts,
):
    root_slab = extract_slab(root_values, root_columns, root_counts)
    fock_inner = sparse_product(fock_values, fock_columns, fock_counts, root_slab).astype(
        jnp.bfloat16
    )
    fock_slab = sparse_product(root_values, root_columns, root_counts, fock_inner).astype(
        jnp.bfloat16
    )
    density_slab = extract_slab(density_values, density_columns, density_counts)
    squared = sparse_product(density_values, density_columns, density_counts, density_slab).astype(
        jnp.bfloat16
    )
    cubed_term = sparse_product(density_values, density_columns, density_counts, squared)
    purified_slab = (3.0 * squared.astype(jnp.float32) - 2.0 * cubed_term).astype(jnp.bfloat16)
    energy_slab = sparse_product(density_values, density_columns, density_counts, fock_slab).astype(
        jnp.bfloat16
    )
    return (fock_slab, purified_slab, energy_slab)


def solution(mesh):
    finer = Mesh(
        mesh.devices.reshape(mesh.shape["row"], 4, 4, mesh.shape["layer"]),
        ("row", "col_0", "col_1", "layer"),
    )
    return jax.shard_map(
        on_device,
        mesh=finer,
        in_specs=(
            P(COL, "layer", None, None, None),
            P(COL, "layer", None),
            P(COL, "layer"),
            P(COL, "layer", None, None, None),
            P(COL, "layer", None),
            P(COL, "layer"),
            P(COL, "layer", None, None, None),
            P(COL, "layer", None),
            P(COL, "layer"),
        ),
        out_specs=(P(COL_LAYER, "row"), P(COL_LAYER, "row"), P(COL_LAYER, "row")),
        check_vma=False,
    )
```

profile of v0, /device:TPU:64, one launch (start us, length us, event | category | flops | bytes accessed | tf_op | source)
XLA Modules:
  0.0 297.5 jit_solution(5055084215396574342)
XLA Ops:
  8.7 2.6 fusion.68
  11.7 27.6 %all_to_all.35 = bf16[4,256,256]{2,1,0:T(8,128)(2,1)S(1)} all-to-all(bf16[4,256,256]{2,1,0:T(8,128)(2,1)S(1)} %convert_element_type.118), channel_id=1, replica_groups=mesh['row'=8,'col_0'=4,'col_1'=4,'layer'=4] {'layer'}, dimensions={0} | all-to-all | bytes 1048576 | tf_op jit(solution)/shard_map/all_to_all | solution.py:19
  39.4 13.8 %all-gather = bf16[1024,256]{1,0:T(8,128)(2,1)} all-gather(bf16[256,256]{1,0:T(8,128)(2,1)S(1)} %reduce_sum.81), channel_id=2, replica_groups=mesh['row'=8,'col_0'=4,'col_1'=4,'layer'=4] {'col_0'}, dimensions={0}, use_global_device_ids=true | all-gather | bytes 655360 | tf_op jit(solution)/shard_map/all_gather | solution.py:32
  55.0 20.7 %all_to_all.36 = bf16[4,256,256]{2,1,0:T(8,128)(2,1)S(1)} all-to-all(bf16[4,256,256]{2,1,0:T(8,128)(2,1)S(1)} %convert_element_type.126), channel_id=1, replica_groups=mesh['row'=8,'col_0'=4,'col_1'=4,'layer'=4] {'layer'}, dimensions={0} | all-to-all | bytes 1048576 | tf_op jit(solution)/shard_map/all_to_all | solution.py:19
  75.8 13.8 %all-gather.2 = bf16[1024,256]{1,0:T(8,128)(2,1)} all-gather(bf16[256,256]{1,0:T(8,128)(2,1)S(1)} %reduce_sum.84), channel_id=4, replica_groups=mesh['row'=8,'col_0'=4,'col_1'=4,'layer'=4] {'col_0'}, dimensions={0}, use_global_device_ids=true | all-gather | bytes 655360 | tf_op jit(solution)/shard_map/all_gather | solution.py:32
  91.8 2.5 gather_fusion
  94.3 3.2 %fusion.56 = bf16[8,128,256]{2,1,0:T(8,128)(2,1)S(1)} fusion(bf16[8,6,128,256]{3,2,1,0:T(8,128)(2,1)} %bitcast.140, pred[8,6]{1,0:T(8,128)(4,1)S(1)} %get-tuple-element.8, bf16[8,1,6,128,128]{4,3,2,1,0:T(8,128)(2,1)} %param.14, bf16[8,6]{1,0:T(8,128)(2,1)S(1)} %get-tuple-element.14), kind=kOutput, calls=%fused_computation.40 | convolution fusion | flops 405274624 | bytes 5243024 | tf_op jit(solution)/shard_map/rkab,rkbw->raw/dot_general | solution.py:73
  97.4 23.3 %all_to_all.37 = bf16[4,256,256]{2,1,0:T(8,128)(2,1)S(1)} all-to-all(bf16[4,256,256]{2,1,0:T(8,128)(2,1)S(1)} %bitcast.157), channel_id=1, replica_groups=mesh['row'=8,'col_0'=4,'col_1'=4,'layer'=4] {'layer'}, dimensions={0} | all-to-all | bytes 1048576 | tf_op jit(solution)/shard_map/all_to_all | solution.py:19
  120.8 13.7 %all-gather.1 = bf16[1024,256]{1,0:T(8,128)(2,1)} all-gather(bf16[256,256]{1,0:T(8,128)(2,1)S(1)} %reduce_sum.82), channel_id=3, replica_groups=mesh['row'=8,'col_0'=4,'col_1'=4,'layer'=4] {'col_0'}, dimensions={0}, use_global_device_ids=true | all-gather | bytes 655360 | tf_op jit(solution)/shard_map/all_gather | solution.py:32
  136.5 2.5 gather_fusion.2
  139.0 3.2 %fusion.48 = bf16[8,128,256]{2,1,0:T(8,128)(2,1)S(1)} fusion(bf16[8,6,128,256]{3,2,1,0:T(8,128)(2,1)} %bitcast.143, pred[8,6]{1,0:T(8,128)(4,1)S(1)} %get-tuple-element.4, bf16[8,6]{1,0:T(8,128)(2,1)S(1)} %get-tuple-element.18, bf16[8,1,6,128,128]{4,3,2,1,0:T(8,128)(2,1)} %param.17), kind=kOutput, calls=%fused_computation.38 | convolution fusion | flops 405274624 | bytes 5243024 | tf_op jit(solution)/shard_map/rkab,rkbw->raw/dot_general | solution.py:73
  142.1 20.7 %all_to_all.38 = bf16[4,256,256]{2,1,0:T(8,128)(2,1)S(1)} all-to-all(bf16[4,256,256]{2,1,0:T(8,128)(2,1)S(1)} %bitcast.159), channel_id=1, replica_groups=mesh['row'=8,'col_0'=4,'col_1'=4,'layer'=4] {'layer'}, dimensions={0} | all-to-all | bytes 1048576 | tf_op jit(solution)/shard_map/all_to_all | solution.py:19
  163.0 13.8 %all-gather.3 = bf16[1024,256]{1,0:T(8,128)(2,1)} all-gather(bf16[256,256]{1,0:T(8,128)(2,1)S(1)} %reduce_sum.85), channel_id=5, replica_groups=mesh['row'=8,'col_0'=4,'col_1'=4,'layer'=4] {'col_0'}, dimensions={0}, use_global_device_ids=true | all-gather | bytes 655360 | tf_op jit(solution)/shard_map/all_gather | solution.py:32
  178.7 2.5 gather_fusion.1
  181.2 3.2 %fusion.51 = bf16[8,128,256]{2,1,0:T(8,128)(2,1)S(1)} fusion(bf16[8,6,128,256]{3,2,1,0:T(8,128)(2,1)} %bitcast.141, pred[8,6]{1,0:T(8,128)(4,1)S(1)} %get-tuple-element.6, bf16[8,6]{1,0:T(8,128)(2,1)S(1)} %get-tuple-element.16, bf16[8,1,6,128,128]{4,3,2,1,0:T(8,128)(2,1)} %param.11), kind=kOutput, calls=%fused_computation.39 | convolution fusion | flops 405274624 | bytes 5243024 | tf_op jit(solution)/shard_map/rkab,rkbw->raw/dot_general | solution.py:73
  184.3 20.7 %all_to_all.39 = bf16[4,256,256]{2,1,0:T(8,128)(2,1)S(1)} all-to-all(bf16[4,256,256]{2,1,0:T(8,128)(2,1)S(1)} %bitcast.158), channel_id=1, replica_groups=mesh['row'=8,'col_0'=4,'col_1'=4,'layer'=4] {'layer'}, dimensions={0} | all-to-all | bytes 1048576 | tf_op jit(solution)/shard_map/all_to_all | solution.py:19
  205.2 14.5 %all-gather.4 = bf16[1024,256]{1,0:T(8,128)(2,1)} all-gather(bf16[256,256]{1,0:T(8,128)(2,1)S(1)} %reduce_sum.83), channel_id=6, replica_groups=mesh['row'=8,'col_0'=4,'col_1'=4,'layer'=4] {'col_0'}, dimensions={0}, use_global_device_ids=true | all-gather | bytes 655360 | tf_op jit(solution)/shard_map/all_gather | solution.py:32
  221.5 2.5 gather_fusion.3
  224.0 4.0 %fusion.45 = bf16[8,128,256]{2,1,0:T(8,128)(2,1)} fusion(bf16[8,6,128,256]{3,2,1,0:T(8,128)(2,1)} %bitcast.144, pred[8,6]{1,0:T(8,128)(4,1)S(1)} %get-tuple-element.4, bf16[8,6]{1,0:T(8,128)(2,1)S(1)} %get-tuple-element.18, bf16[8,1,6,128,128]{4,3,2,1,0:T(8,128)(2,1)} %param.17), kind=kOutput, calls=%fused_computation.37 | convolution fusion | flops 405274624 | bytes 5243024 | tf_op jit(solution)/shard_map/rkab,rkbw->raw/dot_general | solution.py:73
  228.0 3.5 %all-to-all-start.5 = ((bf16[4,256,256]{2,1,0:T(8,128)(2,1)}), bf16[4,256,256]{2,1,0:T(8,128)(2,1)S(1)}, u32[]{:S(2)}, u32[]{:S(2)}) async-start(bf16[4,256,256]{2,1,0:T(8,128)(2,1)} %bitcast.46), calls=%async_computation.5 | async-start | bytes 1048576 | tf_op jit(solution)/shard_map/all_to_all | solution.py:19
  231.5 25.7 %all-gather.19.cloned.1.call-done = bf16[16,256,256]{2,1,0:T(8,128)(2,1)} async-done(((bf16[4,256,256]{2,1,0:T(8,128)(2,1)}), bf16[16,256,256]{2,1,0:T(8,128)(2,1)}) %all-gather.19.cloned.1.call-update) | async-done | bytes 2097168 | tf_op jit(solution)/shard_map/all_gather | solution.py:32
  261.4 4.0 %fusion.42 = bf16[8,128,256]{2,1,0:T(8,128)(2,1)} fusion(bf16[8,6,128,256]{3,2,1,0:T(8,128)(2,1)} %bitcast.142, pred[8,6]{1,0:T(8,128)(4,1)S(1)} %get-tuple-element.4, bf16[8,6]{1,0:T(8,128)(2,1)S(1)} %get-tuple-element.18, bf16[8,1,6,128,128]{4,3,2,1,0:T(8,128)(2,1)} %param.17), kind=kOutput, calls=%fused_computation.36 | convolution fusion | flops 405274624 | bytes 5243024 | tf_op jit(solution)/shard_map/rkab,rkbw->raw/dot_general | solution.py:73
  265.4 6.5 %all-to-all-start.6 = ((bf16[4,256,256]{2,1,0:T(8,128)(2,1)}), bf16[4,256,256]{2,1,0:T(8,128)(2,1)S(1)}, u32[]{:S(2)}, u32[]{:S(2)}) async-start(bf16[4,256,256]{2,1,0:T(8,128)(2,1)} %bitcast.54), calls=%async_computation.6 | async-start | bytes 1048576 | tf_op jit(solution)/shard_map/all_to_all | solution.py:19
  272.6 17.6 %all-to-all-done.6 = bf16[4,256,256]{2,1,0:T(8,128)(2,1)S(1)} async-done(((bf16[4,256,256]{2,1,0:T(8,128)(2,1)}), bf16[4,256,256]{2,1,0:T(8,128)(2,1)S(1)}, u32[]{:S(2)}, u32[]{:S(2)}) %all-to-all-start.6) | async-done | bytes 524320 | tf_op jit(solution)/shard_map/all_to_all | solution.py:19
  (57 shorter events, 17.4 us)
Async XLA Ops:
  7.2 82.9 %all-gather.11.cloned.1.call-start = ((), (), s32[]{:S(2)}) async-start(), calls=%async_computation.7 | async-start | bytes 2621440 | tf_op jit(solution)/shard_map/all_gather | solution.py:32
  11.3 41.9 %copy-start.2 = (s32[8,1,6]{0,1,2:T(1,128)S(1)}, s32[8,1,6]{0,1,2:T(1,128)}, u32[]{:S(2)}) copy-start(s32[8,1,6]{0,1,2:T(1,128)} %param.18) | copy-start | bytes 580
  11.3 42.0 %copy-start.4 = (s32[8,1]{0,1:T(1,128)S(1)}, s32[8,1]{0,1:T(1,128)}, u32[]{:S(2)}) copy-start(s32[8,1]{0,1:T(1,128)} %param.19) | copy-start | bytes 100
  11.4 42.1 %copy-start = (bf16[8,1,6,128,128]{4,3,2,1,0:T(8,128)(2,1)S(1)}, bf16[8,1,6,128,128]{4,3,2,1,0:T(8,128)(2,1)}, u32[]{:S(2)}) copy-start(bf16[8,1,6,128,128]{4,3,2,1,0:T(8,128)(2,1)} %param.17) | copy-start | bytes 4718596
  53.2 81.5 %all-gather.15.cloned.1.call-start = ((), (), s32[]{:S(2)}) async-start(), calls=%async_computation.9 | async-start | bytes 2621440 | tf_op jit(solution)/shard_map/all_gather | solution.py:32
  54.7 35.1 %copy-start.3 = (s32[8,1,6]{0,1,2:T(1,128)S(1)}, s32[8,1,6]{0,1,2:T(1,128)}, u32[]{:S(2)}) copy-start(s32[8,1,6]{0,1,2:T(1,128)} %param.15) | copy-start | bytes 580
  54.7 35.2 %copy-start.5 = (s32[8,1]{0,1:T(1,128)S(1)}, s32[8,1]{0,1:T(1,128)}, u32[]{:S(2)}) copy-start(s32[8,1]{0,1:T(1,128)} %param.16) | copy-start | bytes 100
  89.7 87.2 %all-gather.13.cloned.1.call-start = ((), (), s32[]{:S(2)}) async-start(), calls=%async_computation.8 | async-start | bytes 2621440 | tf_op jit(solution)/shard_map/all_gather | solution.py:32
  134.6 85.2 %all-gather.17.cloned.1.call-start = ((), (), s32[]{:S(2)}) async-start(), calls=%async_computation.10 | async-start | bytes 2621440 | tf_op jit(solution)/shard_map/all_gather | solution.py:32
  176.8 80.4 %all-gather.19.cloned.1.call-start = ((), (), s32[]{:S(2)}) async-start(), calls=%async_computation.11 | async-start | bytes 2621440 | tf_op jit(solution)/shard_map/all_gather | solution.py:32
  205.2 16.3 %copy-start.1 = (bf16[256,256]{1,0:T(8,128)(2,1)}, bf16[256,256]{1,0:T(8,128)(2,1)S(1)}, u32[]{:S(2)}) copy-start(bf16[256,256]{1,0:T(8,128)(2,1)S(1)} %reduce_sum.83) | copy-start | bytes 393220
  228.0 37.4 %all-to-all-start.5 = ((bf16[4,256,256]{2,1,0:T(8,128)(2,1)}), bf16[4,256,256]{2,1,0:T(8,128)(2,1)S(1)}, u32[]{:S(2)}, u32[]{:S(2)}) async-start(bf16[4,256,256]{2,1,0:T(8,128)(2,1)} %bitcast.46), calls=%async_computation.5 | async-start | bytes 1048576 | tf_op jit(solution)/shard_map/all_to_all | solution.py:19
  265.4 24.8 %all-to-all-start.6 = ((bf16[4,256,256]{2,1,0:T(8,128)(2,1)}), bf16[4,256,256]{2,1,0:T(8,128)(2,1)S(1)}, u32[]{:S(2)}, u32[]{:S(2)}) async-start(bf16[4,256,256]{2,1,0:T(8,128)(2,1)} %bitcast.54), calls=%async_computation.6 | async-start | bytes 1048576 | tf_op jit(solution)/shard_map/all_to_all | solution.py:19
Sparse Core Ops, SparseCore 0:
  53.3 35.3 all-gather.10
  90.8 36.1 all-gather.14
  134.7 35.4 all-gather.12
  176.9 36.7 all-gather.16
  219.9 37.2 all-gather.18
where the time goes:
time: 298 us; the launch traced here: 297 us
  blocking collectives  183 us (61%)
  waiting for transfers between devices  43.4 us (15%)
  local copies, waits for them, and re-layouts  23 us (8%)
  matrix products  21.3 us (7%)
  between operations  14 us (5%)
  starting transfers between devices  10.1 us (3%)
    all_to_all x5, blocking collectives, sent_and_summed(): lax.all_to_all(pieces, axis, split_axis=0, concat_axis=0, tiled=True)  113 us
    all_gather x5, blocking collectives, gather_in_order(): pieces = lax.all_gather(pieces, axes[k], axis=0, tiled=True)  69.6 us
    all_gather x5, waiting for transfers between devices, gather_in_order(): pieces = lax.all_gather(pieces, axes[k], axis=0, tiled=True)  25.8 us
    all_to_all x2, waiting for transfers between devices, sent_and_summed(): lax.all_to_all(pieces, axis, split_axis=0, concat_axis=0, tiled=True)  17.6 us
    dot_general x5, matrix products, sparse_product(): jnp.einsum('rkab,rkbw->raw', masked_tiles, picked, preferred_element_type...  17.5 us
    gather x5, local copies, waits for them, and re-layouts, sparse_product(): picked = jnp.take(blocks, positions, axis=0)  12.5 us
    all_to_all x2, starting transfers between devices, sent_and_summed(): lax.all_to_all(pieces, axis, split_axis=0, concat_axis=0, tiled=True)  9.92 us
    transpose x5, local copies, waits for them, and re-layouts, gather_in_order(): pieces.transpose(*turned, *range(len(order), pieces.ndim))  8.64 us
  transfers between devices with their start and end apart: 7, of which 2 were waited for; matrix products, arithmetic and copies ran while one was open for 14% of the time, Pallas kernels for 0%

commit v1 on v0

v1 whole, which is shorter than its diff:
```python
import functools

import jax
import jax.numpy as jnp
from jax import lax
from jax.experimental import pallas as pl
from jax.experimental.pallas import tpu as pltpu
from jax.sharding import Mesh
from jax.sharding import PartitionSpec as P

BS = 128
KQ = 6
RB = 8
HALF = RB // 2
META = KQ + 1
ROOT, FOCK, DENSITY = range(3)
COL = ("zl", "x")
LAYER = ("zh", "c")


def swapped(value, axis):
    return lax.ppermute(value, axis, [(0, 1), (1, 0)])


def extract_kernel(mat, own_meta, other_meta, place, own, other, out):
    row = place[0] + pl.program_id(0)
    start = (mat * RB + row) * META
    out[...] = jnp.zeros_like(out)
    for meta, tiles in ((own_meta, own), (other_meta, other)):
        count = meta[start + KQ]
        for k in range(KQ):

            @pl.when((meta[start + k] == place[1]) & (k < count))
            def _(k=k, tiles=tiles):
                out[0] = tiles[0, k].astype(out.dtype)


def product_kernel(mat, own_meta, other_meta, place, own, other, slab, out):
    row = place[0] + pl.program_id(0)
    start = (mat * RB + row) * META
    left, right = [], []
    for meta, tiles in ((own_meta, own), (other_meta, other)):
        count = meta[start + KQ]
        for k in range(KQ):
            j = meta[start + k]
            at = (((j >> 3) & 3) * 4 + (j >> 5)) * HALF + (j & 3)
            tile = tiles[0, k]
            left.append(jnp.where(k < count, tile, jnp.zeros_like(tile)))
            right.append(slab[at])
    total = jnp.dot(
        jnp.concatenate(left, axis=1),
        jnp.concatenate(right, axis=0),
        preferred_element_type=jnp.float32,
    )
    out[0] = total.astype(out.dtype)


def rows_call(kernel, place, metas, tiles, slab, dtype, count=HALF):
    tile_spec = pl.BlockSpec((1, KQ, BS, BS), lambda r, a, b, p: (p[0] + r, 0, 0, 0))
    slabs = [] if slab is None else [slab]
    return pl.pallas_call(
        kernel,
        out_shape=jax.ShapeDtypeStruct((count, BS, BS), dtype),
        grid_spec=pltpu.PrefetchScalarGridSpec(
            num_scalar_prefetch=3,
            grid=(count,),
            in_specs=[tile_spec, tile_spec]
            + [pl.BlockSpec(memory_space=pltpu.VMEM) for _ in slabs],
            out_specs=pl.BlockSpec((1, BS, BS), lambda r, a, b, p: (r, 0, 0)),
        ),
        cost_estimate=pl.CostEstimate(
            flops=2 * count * 2 * KQ * BS * BS * BS,
            bytes_accessed=count * 2 * KQ * BS * BS * 2,
            transcendentals=0,
        ),
    )(metas[0], metas[1], place, *tiles, *slabs)


def halves_exchanged(rows, places):
    sent = rows(places[1], jnp.bfloat16)
    arrived = swapped(sent, "zh")
    kept = rows(places[0], jnp.float32)
    return kept + arrived.astype(jnp.float32)


def gathered(piece):
    along_z = lax.all_gather(piece, "zl", axis=0, tiled=True)
    copies = jnp.broadcast_to(along_z[None], (4, *along_z.shape))
    return lax.all_to_all(copies, "x", split_axis=0, concat_axis=0, tiled=True).reshape(-1, BS, BS)


def widened(pieces):
    core = lax.axis_index("c")
    split = jnp.stack(pieces).reshape(len(pieces), 2, 2 * BS, BS)
    mine = lax.dynamic_index_in_dim(split, core, 1, keepdims=False)
    other = swapped(lax.dynamic_index_in_dim(split, 1 - core, 1, keepdims=False), "c")
    first = jnp.where(core == 0, mine, other)
    second = jnp.where(core == 0, other, mine)
    return jnp.concatenate([first, second], axis=-1)


def on_device(
    root_values,
    root_columns,
    root_counts,
    fock_values,
    fock_columns,
    fock_counts,
    density_values,
    density_columns,
    density_counts,
):
    row, zh, core = (lax.axis_index(a) for a in ("row", "zh", "c"))
    target = row * 2 + core
    places = [jnp.stack([half * HALF, target]).astype(jnp.int32) for half in (zh, 1 - zh)]
    own_meta = jnp.stack(
        [
            jnp.concatenate([columns[:, 0], counts], axis=1)
            for columns, counts in (
                (root_columns, root_counts),
                (fock_columns, fock_counts),
                (density_columns, density_counts),
            )
        ]
    ).reshape(-1)
    metas = (own_meta, swapped(own_meta, "c"))
    held = []
    for values in (root_values, fock_values, density_values):
        tiles = values[:, 0]
        held.append((tiles, swapped(tiles, "c")))

    def extracted(mat):
        def rows(place, dtype):
            kernel = functools.partial(extract_kernel, mat)
            return rows_call(kernel, place, metas, held[mat], None, dtype)

        return halves_exchanged(rows, places).astype(jnp.bfloat16)

    def product(mat, slab):
        def rows(place, dtype):
            kernel = functools.partial(product_kernel, mat)
            return rows_call(kernel, place, metas, held[mat], slab, dtype)

        return halves_exchanged(rows, places)

    root_slab = extracted(ROOT)
    density_slab = extracted(DENSITY)
    fock_inner = product(FOCK, gathered(root_slab)).astype(jnp.bfloat16)
    squared = product(DENSITY, gathered(density_slab)).astype(jnp.bfloat16)
    fock_slab = product(ROOT, gathered(fock_inner)).astype(jnp.bfloat16)
    cubed_term = product(DENSITY, gathered(squared))
    purified = (3.0 * squared.astype(jnp.float32) - 2.0 * cubed_term).astype(jnp.bfloat16)
    outs = widened([fock_slab, purified])

    all_rows = jnp.stack([jnp.int32(0), target]).astype(jnp.int32)
    partial_value = rows_call(
        functools.partial(product_kernel, DENSITY),
        all_rows,
        metas,
        held[DENSITY],
        gathered(fock_slab),
        jnp.bfloat16,
        RB,
    )
    pieces = partial_value.reshape(4, 2 * BS, BS)
    arrived = lax.all_to_all(pieces, LAYER, split_axis=0, concat_axis=0, tiled=True)
    energy = arrived.reshape(2, 2, 2 * BS, BS).astype(jnp.float32).sum(axis=0)
    energy = jnp.concatenate([energy[0], energy[1]], axis=-1).astype(jnp.bfloat16)
    return outs[0], outs[1], energy


def solution(mesh):
    finer = Mesh(mesh.devices.reshape(mesh.shape["row"], 4, 4, 2, 2), ("row", *COL, *LAYER))
    specs = (P(COL, LAYER, None, None, None), P(COL, LAYER, None), P(COL, LAYER))
    return jax.shard_map(
        on_device,
        mesh=finer,
        in_specs=specs * 3,
        out_specs=(P((*COL, *LAYER), "row"),) * 3,
        check_vma=False,
    )
```

time: 298 us -> 274 us (0.919)
  the two profiles are of different devices: /device:TPU:64 before, /device:TPU:74 now
where the time goes in v1:
time: 274 us; the launch traced here: 271 us
  starting transfers between devices  81.3 us (30%)
  blocking collectives  75.5 us (28%)
  Pallas kernels  67.3 us (25%)
  waiting for transfers between devices  19.9 us (7%)
  local copies, waits for them, and re-layouts  16.9 us (6%)
  other arithmetic  9.41 us (3%)
    all_gather x5, blocking collectives, gathered(): along_z = lax.all_gather(piece, 'zl', axis=0, tiled=True)  75.5 us
    pallas_call x13, Pallas kernels, rows_call(): pl.pallas_call(kernel, out_shape=jax.ShapeDtypeStruct((count, BS, BS), dt...  67.3 us
    ppermute x11, starting transfers between devices, swapped(): return lax.ppermute(value, axis, [(0, 1), (1, 0)])  52.1 us
    all_to_all x5, starting transfers between devices, gathered(): lax.all_to_all(copies, 'x', split_axis=0, concat_axis=0, tiled=True)  24.2 us
    all_to_all x1, waiting for transfers between devices, on_device(): lax.all_to_all(pieces, LAYER, split_axis=0, concat_axis=0, tiled=True)  12 us
    broadcast_in_dim x5, local copies, waits for them, and re-layouts, gathered(): copies = jnp.broadcast_to(along_z[None], (4, *along_z.shape))  9.44 us
    ppermute x11, waiting for transfers between devices, swapped(): return lax.ppermute(value, axis, [(0, 1), (1, 0)])  7.93 us
    unnamed x18, local copies, waits for them, and re-layouts  7.4 us
  transfers between devices with their start and end apart: 17, of which 6 were waited for; matrix products, arithmetic and copies ran while one was open for 6% of the time, Pallas kernels for 25%

profile of v1, /device:TPU:74, one launch (start us, length us, event | category | flops | bytes accessed | tf_op | source)
XLA Modules:
  0.0 271.2 jit_solution(696566157307041286)
XLA Ops:
  18.1 10.0 %collective-permute-start.3 = (bf16[4,128,128]{2,1,0:T(8,128)(2,1)}, bf16[4,128,128]{2,1,0:T(8,128)(2,1)S(1)}, u32[]{:S(2)}, u32[]{:S(2)}) collective-permute-start(bf16[4,128,128]{2,1,0:T(8,128)(2,1)} %shard_map.113), channel_id=1, source_target_pairs={{0,2},{2,0},{1,3},{3,1},{4,6},{6,4},{5,7},{7,5},{8,10},{10,8},{9,1... | collective-permute-start | bytes 393224 | tf_op jit(solution)/shard_map/ppermute | solution.py:22
  36.4 13.2 %all_gather.15 = bf16[16,128,128]{2,1,0:T(8,128)(2,1)S(1)} all-gather(bf16[4,128,128]{2,1,0:T(8,128)(2,1)S(1)} %add_convert_fusion.4), channel_id=1, replica_groups=mesh['row'=8,'zl'=4,'x'=4,'zh'=2,'c'=2] {'zl'}, dimensions={0}, use_global_device_ids=true | all-gather | bytes 655360 | tf_op jit(solution)/shard_map/all_gather | solution.py:87
  51.5 5.0 %all-to-all-start = ((bf16[4,16,128,128]{3,2,1,0:T(8,128)(2,1)}), bf16[4,16,128,128]{3,2,1,0:T(8,128)(2,1)}, u32[]{:S(2)}, u32[]{:S(2)}) async-start(bf16[4,16,128,128]{3,2,1,0:T(8,128)(2,1)} %broadcast_in_dim.10), calls=%async_computation | async-start | bytes 4194304 | tf_op jit(solution)/shard_map/all_to_all | solution.py:89
  63.6 7.1 %collective-permute-start.7 = (bf16[4,128,128]{2,1,0:T(8,128)(2,1)}, bf16[4,128,128]{2,1,0:T(8,128)(2,1)S(1)}, u32[]{:S(2)}, u32[]{:S(2)}) collective-permute-start(bf16[4,128,128]{2,1,0:T(8,128)(2,1)} %shard_map.119), channel_id=1, source_target_pairs={{0,2},{2,0},{1,3},{3,1},{4,6},{6,4},{5,7},{7,5},{8,10},{10,8},{9,1... | collective-permute-start | bytes 393224 | tf_op jit(solution)/shard_map/ppermute | solution.py:22
  79.3 15.4 %all_gather.17 = bf16[16,128,128]{2,1,0:T(8,128)(2,1)S(1)} all-gather(bf16[4,128,128]{2,1,0:T(8,128)(2,1)S(1)} %add_convert_fusion.1), channel_id=1, replica_groups=mesh['row'=8,'zl'=4,'x'=4,'zh'=2,'c'=2] {'zl'}, dimensions={0}, use_global_device_ids=true | all-gather | bytes 655360 | tf_op jit(solution)/shard_map/all_gather | solution.py:87
  96.5 4.8 %all-to-all-start.2 = ((bf16[4,16,128,128]{3,2,1,0:T(8,128)(2,1)}), bf16[4,16,128,128]{3,2,1,0:T(8,128)(2,1)S(1)}, u32[]{:S(2)}, u32[]{:S(2)}) async-start(bf16[4,16,128,128]{3,2,1,0:T(8,128)(2,1)} %broadcast_in_dim.12), calls=%async_computation.2 | async-start | bytes 4194304 | tf_op jit(solution)/shard_map/all_to_all | solution.py:89
  101.3 5.4 %shard_map.115 = bf16[4,128,128]{2,1,0:T(8,128)(2,1)} custom-call(s32[168]{0:T(256)} %copy-done.4, s32[168]{0:T(256)} %copy-done.5, s32[2]{0:T(128)} %pad_add_fusion.2.place, bf16[8,6,128,128]{3,2,1,0:T(8,128)(2,1)} %bitcast.9.own, bf16[8,6,128,128]{3,2,1,0:T(8,128)(2,1)} %collective-permute-done.2.other, bf16[64,128,128]{2,1,0:T(8,128)(2,1)} %bitcast.11.slab), custom_call_target="tpu_custom_call" | custom-call | flops 201326592 | bytes 1572864 | tf_op jit(solution)/shard_map/pallas_call | solution.py:61
  106.7 5.5 %collective-permute-start.4 = (bf16[4,128,128]{2,1,0:T(8,128)(2,1)}, bf16[4,128,128]{2,1,0:T(8,128)(2,1)S(1)}, u32[]{:S(2)}, u32[]{:S(2)}) collective-permute-start(bf16[4,128,128]{2,1,0:T(8,128)(2,1)} %shard_map.115), channel_id=1, source_target_pairs={{0,2},{2,0},{1,3},{3,1},{4,6},{6,4},{5,7},{7,5},{8,10},{10,8},{9,1... | collective-permute-start | bytes 393224 | tf_op jit(solution)/shard_map/ppermute | solution.py:22
  112.1 5.4 %shard_map.114 = f32[4,128,128]{2,1,0:T(8,128)} custom-call(s32[168]{0:T(256)} %copy-done.4, s32[168]{0:T(256)} %copy-done.5, s32[2]{0:T(128)} %pad_add_fusion.1.place, bf16[8,6,128,128]{3,2,1,0:T(8,128)(2,1)} %bitcast.9.own, bf16[8,6,128,128]{3,2,1,0:T(8,128)(2,1)} %collective-permute-done.2.other, bf16[64,128,128]{2,1,0:T(8,128)(2,1)} %bitcast.11.slab), custom_call_target="tpu_custom_call" | custom-call | flops 201326592 | bytes 1572864 | tf_op jit(solution)/shard_map/pallas_call | solution.py:61
  118.7 17.2 %all_gather.16 = bf16[16,128,128]{2,1,0:T(8,128)(2,1)S(1)} all-gather(bf16[4,128,128]{2,1,0:T(8,128)(2,1)S(1)} %add_convert_fusion.3), channel_id=1, replica_groups=mesh['row'=8,'zl'=4,'x'=4,'zh'=2,'c'=2] {'zl'}, dimensions={0}, use_global_device_ids=true | all-gather | bytes 655360 | tf_op jit(solution)/shard_map/all_gather | solution.py:87
  142.7 5.4 %shard_map.121 = bf16[4,128,128]{2,1,0:T(8,128)(2,1)} custom-call(s32[168]{0:T(256)} %copy-done.4, s32[168]{0:T(256)} %copy-done.5, s32[2]{0:T(128)} %pad_add_fusion.2.place, bf16[8,6,128,128]{3,2,1,0:T(8,128)(2,1)} %bitcast.43, bf16[8,6,128,128]{3,2,1,0:T(8,128)(2,1)} %copy-done, bf16[64,128,128]{2,1,0:T(8,128)(2,1)} %bitcast.55), custom_call_target="tpu_custom_call" | custom-call | flops 201326592 | bytes 1572864 | tf_op jit(solution)/shard_map/pallas_call | solution.py:61
  148.0 5.4 %collective-permute-start.8 = (bf16[4,128,128]{2,1,0:T(8,128)(2,1)}, bf16[4,128,128]{2,1,0:T(8,128)(2,1)S(1)}, u32[]{:S(2)}, u32[]{:S(2)}) collective-permute-start(bf16[4,128,128]{2,1,0:T(8,128)(2,1)} %shard_map.121), channel_id=1, source_target_pairs={{0,2},{2,0},{1,3},{3,1},{4,6},{6,4},{5,7},{7,5},{8,10},{10,8},{9,1... | collective-permute-start | bytes 393224 | tf_op jit(solution)/shard_map/ppermute | solution.py:22
  153.5 5.4 %shard_map.120 = f32[4,128,128]{2,1,0:T(8,128)} custom-call(s32[168]{0:T(256)} %copy-done.4, s32[168]{0:T(256)} %copy-done.5, s32[2]{0:T(128)} %pad_add_fusion.1.place, bf16[8,6,128,128]{3,2,1,0:T(8,128)(2,1)} %bitcast.44, bf16[8,6,128,128]{3,2,1,0:T(8,128)(2,1)} %copy-done, bf16[64,128,128]{2,1,0:T(8,128)(2,1)} %bitcast.56), custom_call_target="tpu_custom_call" | custom-call | flops 201326592 | bytes 1572864 | tf_op jit(solution)/shard_map/pallas_call | solution.py:61
  160.2 16.2 %all_gather.18 = bf16[16,128,128]{2,1,0:T(8,128)(2,1)S(1)} all-gather(bf16[4,128,128]{2,1,0:T(8,128)(2,1)S(1)} %add_convert_fusion), channel_id=1, replica_groups=mesh['row'=8,'zl'=4,'x'=4,'zh'=2,'c'=2] {'zl'}, dimensions={0}, use_global_device_ids=true | all-gather | bytes 655360 | tf_op jit(solution)/shard_map/all_gather | solution.py:87
  182.9 5.4 %shard_map.117 = bf16[4,128,128]{2,1,0:T(8,128)(2,1)} custom-call(s32[168]{0:T(256)} %copy-done.4, s32[168]{0:T(256)} %copy-done.5, s32[2]{0:T(128)} %pad_add_fusion.2.place, bf16[8,6,128,128]{3,2,1,0:T(8,128)(2,1)} %bitcast.51, bf16[8,6,128,128]{3,2,1,0:T(8,128)(2,1)} %copy-done.1, bf16[64,128,128]{2,1,0:T(8,128)(2,1)} %bitcast.12.slab), custom_call_target="tpu_custom_call" | custom-call | flops 201326592 | bytes 1572864 | tf_op jit(solution)/shard_map/pallas_call | solution.py:61
  188.3 6.6 %collective-permute-start.5 = (bf16[4,128,128]{2,1,0:T(8,128)(2,1)}, bf16[4,128,128]{2,1,0:T(8,128)(2,1)S(1)}, u32[]{:S(2)}, u32[]{:S(2)}) collective-permute-start(bf16[4,128,128]{2,1,0:T(8,128)(2,1)} %shard_map.117), channel_id=1, source_target_pairs={{0,2},{2,0},{1,3},{3,1},{4,6},{6,4},{5,7},{7,5},{8,10},{10,8},{9,1... | collective-permute-start | bytes 393224 | tf_op jit(solution)/shard_map/ppermute | solution.py:22
  194.9 5.4 %shard_map.116 = f32[4,128,128]{2,1,0:T(8,128)} custom-call(s32[168]{0:T(256)} %copy-done.4, s32[168]{0:T(256)} %copy-done.5, s32[2]{0:T(128)} %pad_add_fusion.1.place, bf16[8,6,128,128]{3,2,1,0:T(8,128)(2,1)} %bitcast.52, bf16[8,6,128,128]{3,2,1,0:T(8,128)(2,1)} %copy-done.1, bf16[64,128,128]{2,1,0:T(8,128)(2,1)} %bitcast.12.slab), custom_call_target="tpu_custom_call" | custom-call | flops 201326592 | bytes 1572864 | tf_op jit(solution)/shard_map/pallas_call | solution.py:61
  202.5 13.7 %all_gather.19 = bf16[16,128,128]{2,1,0:T(8,128)(2,1)S(1)} all-gather(bf16[4,128,128]{2,1,0:T(8,128)(2,1)S(1)} %add_convert_fusion.2), channel_id=1, replica_groups=mesh['row'=8,'zl'=4,'x'=4,'zh'=2,'c'=2] {'zl'}, dimensions={0}, use_global_device_ids=true | all-gather | bytes 655360 | tf_op jit(solution)/shard_map/all_gather | solution.py:87
  222.9 5.4 %shard_map.123 = bf16[4,128,128]{2,1,0:T(8,128)(2,1)} custom-call(s32[168]{0:T(256)} %copy-done.4, s32[168]{0:T(256)} %copy-done.5, s32[2]{0:T(128)} %pad_add_fusion.2.place, bf16[8,6,128,128]{3,2,1,0:T(8,128)(2,1)} %bitcast.45, bf16[8,6,128,128]{3,2,1,0:T(8,128)(2,1)} %copy-done, bf16[64,128,128]{2,1,0:T(8,128)(2,1)} %bitcast.53), custom_call_target="tpu_custom_call" | custom-call | flops 201326592 | bytes 1572864 | tf_op jit(solution)/shard_map/pallas_call | solution.py:61
  228.3 7.4 %collective-permute-start.9 = (bf16[4,128,128]{2,1,0:T(8,128)(2,1)}, bf16[4,128,128]{2,1,0:T(8,128)(2,1)S(1)}, u32[]{:S(2)}, u32[]{:S(2)}) collective-permute-start(bf16[4,128,128]{2,1,0:T(8,128)(2,1)} %shard_map.123), channel_id=1, source_target_pairs={{0,2},{2,0},{1,3},{3,1},{4,6},{6,4},{5,7},{7,5},{8,10},{10,8},{9,1... | collective-permute-start | bytes 393224 | tf_op jit(solution)/shard_map/ppermute | solution.py:22
  235.7 5.4 %shard_map.122 = f32[4,128,128]{2,1,0:T(8,128)} custom-call(s32[168]{0:T(256)} %copy-done.4, s32[168]{0:T(256)} %copy-done.5, s32[2]{0:T(128)} %pad_add_fusion.1.place, bf16[8,6,128,128]{3,2,1,0:T(8,128)(2,1)} %bitcast.46, bf16[8,6,128,128]{3,2,1,0:T(8,128)(2,1)} %copy-done, bf16[64,128,128]{2,1,0:T(8,128)(2,1)} %bitcast.54), custom_call_target="tpu_custom_call" | custom-call | flops 201326592 | bytes 1572864 | tf_op jit(solution)/shard_map/pallas_call | solution.py:61
  244.7 8.1 %shard_map.124 = bf16[8,128,128]{2,1,0:T(8,128)(2,1)} custom-call(s32[168]{0:T(256)} %copy-done.4, s32[168]{0:T(256)} %copy-done.5, s32[2]{0:T(128)} %pad_add_fusion.3.place, bf16[8,6,128,128]{3,2,1,0:T(8,128)(2,1)} %bitcast.47, bf16[8,6,128,128]{3,2,1,0:T(8,128)(2,1)} %copy-done, bf16[64,128,128]{2,1,0:T(8,128)(2,1)} %bitcast.22.slab), custom_call_target="tpu_custom_call" | custom-call | flops 402653184 | bytes 3145728 | tf_op jit(solution)/shard_map/pallas_call | solution.py:61
  252.7 5.0 %all-to-all-start.5 = ((bf16[4,256,128]{2,1,0:T(8,128)(2,1)}), bf16[4,256,128]{2,1,0:T(8,128)(2,1)S(1)}, u32[]{:S(2)}, u32[]{:S(2)}) async-start(bf16[4,256,128]{2,1,0:T(8,128)(2,1)} %bitcast.62), calls=%async_computation.5 | async-start | bytes 524288 | tf_op jit(solution)/shard_map/all_to_all | solution.py:166
  258.5 12.0 %all-to-all-done.5 = bf16[4,256,128]{2,1,0:T(8,128)(2,1)S(1)} async-done(((bf16[4,256,128]{2,1,0:T(8,128)(2,1)}), bf16[4,256,128]{2,1,0:T(8,128)(2,1)S(1)}, u32[]{:S(2)}, u32[]{:S(2)}) %all-to-all-start.5) | async-done | bytes 262176 | tf_op jit(solution)/shard_map/all_to_all | solution.py:166
  (70 shorter events, 75.0 us)
Async XLA Ops:
  0.6 11.7 %collective-permute-start.1 = (bf16[8,6,128,128]{3,2,1,0:T(8,128)(2,1)}, bf16[8,6,128,128]{3,2,1,0:T(8,128)(2,1)S(1)}, u32[]{:S(2)}, u32[]{:S(2)}) collective-permute-start(bf16[8,6,128,128]{3,2,1,0:T(8,128)(2,1)} %bitcast.48), channel_id=1, source_target_pairs={{0,1},{1,0},{2,3},{3,2},{4,5},{5,4},{6,7},{7,6},{8,9},{9,8},{10,11... | collective-permute-start | bytes 4718600 | tf_op jit(solution)/shard_map/ppermute | solution.py:22
  7.3 5.0 %copy-start.4 = (s32[168]{0:T(256)}, s32[168]{0:T(256)S(1)}, u32[]{:S(2)}) copy-start(s32[168]{0:T(256)S(1)} %reshape.40.own_meta) | copy-start | bytes 2020
  7.3 5.0 %collective-permute-start = (s32[168]{0:T(256)S(1)}, s32[168]{0:T(256)S(1)}, u32[]{:S(2)}, u32[]{:S(2)}) collective-permute-start(s32[168]{0:T(256)S(1)} %reshape.40.own_meta), channel_id=1, source_target_pairs={{0,1},{1,0},{2,3},{3,2},{4,5},{5,4},{6,7},{7,6},{8,9},{9,8},{10,11... | collective-permute-start | bytes 2024 | tf_op jit(solution)/shard_map/ppermute | solution.py:22
  9.7 48.7 %collective-permute-start.6 = (bf16[8,6,128,128]{3,2,1,0:T(8,128)(2,1)}, bf16[8,6,128,128]{3,2,1,0:T(8,128)(2,1)S(1)}, u32[]{:S(2)}, u32[]{:S(2)}) collective-permute-start(bf16[8,6,128,128]{3,2,1,0:T(8,128)(2,1)} %bitcast.40), channel_id=1, source_target_pairs={{0,1},{1,0},{2,3},{3,2},{4,5},{5,4},{6,7},{7,6},{8,9},{9,8},{10,11... | collective-permute-start | bytes 4718600 | tf_op jit(solution)/shard_map/ppermute | solution.py:22
  12.3 0.6 copy-start.5
  12.9 1.2 copy-start.1
  18.1 17.3 %collective-permute-start.3 = (bf16[4,128,128]{2,1,0:T(8,128)(2,1)}, bf16[4,128,128]{2,1,0:T(8,128)(2,1)S(1)}, u32[]{:S(2)}, u32[]{:S(2)}) collective-permute-start(bf16[4,128,128]{2,1,0:T(8,128)(2,1)} %shard_map.113), channel_id=1, source_target_pairs={{0,2},{2,0},{1,3},{3,1},{4,6},{6,4},{5,7},{7,5},{8,10},{10,8},{9,1... | collective-permute-start | bytes 393224 | tf_op jit(solution)/shard_map/ppermute | solution.py:22
  51.5 43.2 %all-to-all-start = ((bf16[4,16,128,128]{3,2,1,0:T(8,128)(2,1)}), bf16[4,16,128,128]{3,2,1,0:T(8,128)(2,1)}, u32[]{:S(2)}, u32[]{:S(2)}) async-start(bf16[4,16,128,128]{3,2,1,0:T(8,128)(2,1)} %broadcast_in_dim.10), calls=%async_computation | async-start | bytes 4194304 | tf_op jit(solution)/shard_map/all_to_all | solution.py:89
  56.5 44.8 %collective-permute-start.2 = (bf16[8,6,128,128]{3,2,1,0:T(8,128)(2,1)}, bf16[8,6,128,128]{3,2,1,0:T(8,128)(2,1)}, u32[]{:S(2)}, u32[]{:S(2)}) collective-permute-start(bf16[8,6,128,128]{3,2,1,0:T(8,128)(2,1)} %bitcast.9.own), channel_id=1, source_target_pairs={{0,1},{1,0},{2,3},{3,2},{4,5},{5,4},{6,7},{7,6},{8,9},{9,8},{10,11... | collective-permute-start | bytes 4718600 | tf_op jit(solution)/shard_map/ppermute | solution.py:22
  58.4 1.1 copy-start
  63.6 14.8 %collective-permute-start.7 = (bf16[4,128,128]{2,1,0:T(8,128)(2,1)}, bf16[4,128,128]{2,1,0:T(8,128)(2,1)S(1)}, u32[]{:S(2)}, u32[]{:S(2)}) collective-permute-start(bf16[4,128,128]{2,1,0:T(8,128)(2,1)} %shard_map.119), channel_id=1, source_target_pairs={{0,2},{2,0},{1,3},{3,1},{4,6},{6,4},{5,7},{7,5},{8,10},{10,8},{9,1... | collective-permute-start | bytes 393224 | tf_op jit(solution)/shard_map/ppermute | solution.py:22
  96.5 39.4 %all-to-all-start.2 = ((bf16[4,16,128,128]{3,2,1,0:T(8,128)(2,1)}), bf16[4,16,128,128]{3,2,1,0:T(8,128)(2,1)S(1)}, u32[]{:S(2)}, u32[]{:S(2)}) async-start(bf16[4,16,128,128]{3,2,1,0:T(8,128)(2,1)} %broadcast_in_dim.12), calls=%async_computation.2 | async-start | bytes 4194304 | tf_op jit(solution)/shard_map/all_to_all | solution.py:89
  106.7 11.1 %collective-permute-start.4 = (bf16[4,128,128]{2,1,0:T(8,128)(2,1)}, bf16[4,128,128]{2,1,0:T(8,128)(2,1)S(1)}, u32[]{:S(2)}, u32[]{:S(2)}) collective-permute-start(bf16[4,128,128]{2,1,0:T(8,128)(2,1)} %shard_map.115), channel_id=1, source_target_pairs={{0,2},{2,0},{1,3},{3,1},{4,6},{6,4},{5,7},{7,5},{8,10},{10,8},{9,1... | collective-permute-start | bytes 393224 | tf_op jit(solution)/shard_map/ppermute | solution.py:22
  135.9 2.0 copy-start.3
  137.9 38.4 %all-to-all-start.1 = ((bf16[4,16,128,128]{3,2,1,0:T(8,128)(2,1)}), bf16[4,16,128,128]{3,2,1,0:T(8,128)(2,1)}, u32[]{:S(2)}, u32[]{:S(2)}) async-start(bf16[4,16,128,128]{3,2,1,0:T(8,128)(2,1)} %broadcast_in_dim.11), calls=%async_computation.1 | async-start | bytes 4194304 | tf_op jit(solution)/shard_map/all_to_all | solution.py:89
  148.0 11.1 %collective-permute-start.8 = (bf16[4,128,128]{2,1,0:T(8,128)(2,1)}, bf16[4,128,128]{2,1,0:T(8,128)(2,1)S(1)}, u32[]{:S(2)}, u32[]{:S(2)}) collective-permute-start(bf16[4,128,128]{2,1,0:T(8,128)(2,1)} %shard_map.121), channel_id=1, source_target_pairs={{0,2},{2,0},{1,3},{3,1},{4,6},{6,4},{5,7},{7,5},{8,10},{10,8},{9,1... | collective-permute-start | bytes 393224 | tf_op jit(solution)/shard_map/ppermute | solution.py:22
  178.1 38.0 %all-to-all-start.3 = ((bf16[4,16,128,128]{3,2,1,0:T(8,128)(2,1)}), bf16[4,16,128,128]{3,2,1,0:T(8,128)(2,1)S(1)}, u32[]{:S(2)}, u32[]{:S(2)}) async-start(bf16[4,16,128,128]{3,2,1,0:T(8,128)(2,1)} %broadcast_in_dim.13), calls=%async_computation.3 | async-start | bytes 4194304 | tf_op jit(solution)/shard_map/all_to_all | solution.py:89
  188.3 13.2 %collective-permute-start.5 = (bf16[4,128,128]{2,1,0:T(8,128)(2,1)}, bf16[4,128,128]{2,1,0:T(8,128)(2,1)S(1)}, u32[]{:S(2)}, u32[]{:S(2)}) collective-permute-start(bf16[4,128,128]{2,1,0:T(8,128)(2,1)} %shard_map.117), channel_id=1, source_target_pairs={{0,2},{2,0},{1,3},{3,1},{4,6},{6,4},{5,7},{7,5},{8,10},{10,8},{9,1... | collective-permute-start | bytes 393224 | tf_op jit(solution)/shard_map/ppermute | solution.py:22
  216.2 2.0 copy-start.2
  218.2 26.5 %all-to-all-start.4 = ((bf16[4,16,128,128]{3,2,1,0:T(8,128)(2,1)}), bf16[4,16,128,128]{3,2,1,0:T(8,128)(2,1)}, u32[]{:S(2)}, u32[]{:S(2)}) async-start(bf16[4,16,128,128]{3,2,1,0:T(8,128)(2,1)} %broadcast_in_dim.14), calls=%async_computation.4 | async-start | bytes 4194304 | tf_op jit(solution)/shard_map/all_to_all | solution.py:89
  228.3 12.8 %collective-permute-start.9 = (bf16[4,128,128]{2,1,0:T(8,128)(2,1)}, bf16[4,128,128]{2,1,0:T(8,128)(2,1)S(1)}, u32[]{:S(2)}, u32[]{:S(2)}) collective-permute-start(bf16[4,128,128]{2,1,0:T(8,128)(2,1)} %shard_map.123), channel_id=1, source_target_pairs={{0,2},{2,0},{1,3},{3,1},{4,6},{6,4},{5,7},{7,5},{8,10},{10,8},{9,1... | collective-permute-start | bytes 393224 | tf_op jit(solution)/shard_map/ppermute | solution.py:22
  242.1 15.6 %collective-permute-start.10 = (bf16[2,256,128]{2,1,0:T(8,128)(2,1)S(1)}, bf16[2,256,128]{2,1,0:T(8,128)(2,1)S(1)}, u32[]{:S(2)}, u32[]{:S(2)}) collective-permute-start(bf16[2,256,128]{2,1,0:T(8,128)(2,1)S(1)} %fusion.3), channel_id=1, source_target_pairs={{0,1},{1,0},{2,3},{3,2},{4,5},{5,4},{6,7},{7,6},{8,9},{9,8},{10,11... | collective-permute-start | bytes 393224 | tf_op jit(solution)/shard_map/ppermute | solution.py:22
  252.7 17.8 %all-to-all-start.5 = ((bf16[4,256,128]{2,1,0:T(8,128)(2,1)}), bf16[4,256,128]{2,1,0:T(8,128)(2,1)S(1)}, u32[]{:S(2)}, u32[]{:S(2)}) async-start(bf16[4,256,128]{2,1,0:T(8,128)(2,1)} %bitcast.62), calls=%async_computation.5 | async-start | bytes 524288 | tf_op jit(solution)/shard_map/all_to_all | solution.py:166

commit v2 on v1

v2 whole, which is shorter than its diff:
```python
import functools

import jax
import jax.numpy as jnp
from jax import lax
from jax.experimental import pallas as pl
from jax.experimental.pallas import tpu as pltpu
from jax.sharding import Mesh
from jax.sharding import PartitionSpec as P


BS = 128
KQ = 6
RB = 8
HALF = RB // 2
META = KQ + 1
VMEM = 12 << 20
SMALL = 4 << 20
COL = ("zl", "x")
LAYER = ("zh", "c")


def swapped(value, axis):
    return lax.ppermute(value, axis, [(0, 1), (1, 0)])


def spread(value, axis):
    return lax.all_to_all(value, axis, split_axis=0, concat_axis=0, tiled=True)


def extract_kernel(mat, count, own_meta, other_meta, place, own, other, out, found, sems):
    def slot(meta, row):
        at, hit = jnp.int32(0), jnp.int32(0)
        listed = meta[(mat * META + KQ) * RB + row]
        for k in range(KQ):
            here = (meta[(mat * META + k) * RB + row] == place[1]) & (k < listed)
            at = jnp.where(here, k, at)
            hit = jnp.where(here, 1, hit)
        return at, hit

    copies, hits = [], []
    for r in range(count):
        row = place[0] + r
        for side, (meta, tiles) in enumerate(((own_meta, own), (other_meta, other))):
            at, hit = slot(meta, row)
            copy = pltpu.make_async_copy(tiles.at[row, at], found.at[r, side], sems.at[r, side])
            copy.start()
            copies.append(copy)
            hits.append(hit)
    for r in range(count):
        copies[2 * r].wait()
        copies[2 * r + 1].wait()
        zero = jnp.zeros((BS, BS), found.dtype)
        tile = jnp.where(hits[2 * r] > 0, found[r, 0], zero)
        out[r] = jnp.where(hits[2 * r + 1] > 0, found[r, 1], tile).astype(out.dtype)


def product_kernel(mat, count, own_meta, other_meta, place, own, other, slab, out):
    for r in range(count):
        row = place[0] + r
        left, right = [], []
        for meta, tiles in ((own_meta, own), (other_meta, other)):
            listed = meta[(mat * META + KQ) * RB + row]
            for k in range(KQ):
                j = meta[(mat * META + k) * RB + row]
                tile = tiles[row, k]
                left.append(jnp.where(k < listed, tile, jnp.zeros_like(tile)))
                right.append(slab[(((j >> 3) & 3) * 4 + (j >> 5)) * HALF + (j & 3)])
        total = jnp.dot(
            jnp.concatenate(left, axis=1),
            jnp.concatenate(right, axis=0),
            preferred_element_type=jnp.float32,
        )
        out[r] = total.astype(out.dtype)


def local_call(kernel, place, metas, operands, space, count, dtype, scratch):
    return pl.pallas_call(
        kernel,
        out_shape=jax.ShapeDtypeStruct((count, BS, BS), dtype),
        in_specs=[pl.BlockSpec(memory_space=pltpu.SMEM)] * 3
        + [pl.BlockSpec(memory_space=space) for _ in operands],
        out_specs=pl.BlockSpec(memory_space=pltpu.VMEM),
        scratch_shapes=scratch,
        compiler_params=pltpu.CompilerParams(vmem_limit_bytes=VMEM),
        cost_estimate=pl.CostEstimate(
            flops=2 * count * 2 * KQ * BS * BS * BS,
            bytes_accessed=count * 2 * KQ * BS * BS * 2,
            transcendentals=0,
        ),
    )(*metas, place, *operands)


def extracted(mat, metas, held, place, count, dtype):
    scratch = [pltpu.VMEM((count, 2, BS, BS), jnp.bfloat16), pltpu.SemaphoreType.DMA((count, 2))]
    kernel = functools.partial(extract_kernel, mat, count)
    return local_call(kernel, place, metas, held, pl.ANY, count, dtype, scratch)


def multiplied(mat, slab, metas, held, place, count, dtype):
    kernel = functools.partial(product_kernel, mat, count)
    return local_call(kernel, place, metas, [*held, slab], pltpu.VMEM, count, dtype, [])


def add_kernel(kept, arrived, out):
    out[...] = (kept[...] + arrived[...].astype(jnp.float32)).astype(out.dtype)


def copies_kernel(piece, out, sems):
    copies = [pltpu.make_async_copy(piece, out.at[i], sems.at[i]) for i in range(4)]
    for copy in copies:
        copy.start()
    for copy in copies:
        copy.wait()


def small_call(kernel, operands, shape, space, scratch, dtype=jnp.bfloat16):
    return pl.pallas_call(
        kernel,
        out_shape=jax.ShapeDtypeStruct(shape, dtype),
        in_specs=[pl.BlockSpec(memory_space=pltpu.VMEM) for _ in operands],
        out_specs=pl.BlockSpec(memory_space=space),
        scratch_shapes=scratch,
        compiler_params=pltpu.CompilerParams(vmem_limit_bytes=SMALL),
    )(*operands)


def exchanged(rows, places, dtype=jnp.bfloat16):
    sent = rows(places[1], HALF, jnp.bfloat16)
    arrived = swapped(sent, "zh")
    kept = rows(places[0], HALF, jnp.float32)
    return small_call(add_kernel, [kept, arrived], kept.shape, pltpu.VMEM, [], dtype)


def gathered_z(piece):
    return lax.all_gather(piece, "zl", axis=0, tiled=True)


def gathered_x(along_z):
    sems = [pltpu.SemaphoreType.DMA((4,))]
    copies = small_call(copies_kernel, [along_z], (4, *along_z.shape), pl.ANY, sems)
    return spread(copies, "x").reshape(-1, BS, BS)


def all_columns(pieces):
    core = lax.axis_index("c")
    split = jnp.stack(pieces).reshape(len(pieces), 2, 2 * BS, BS)
    mine = lax.dynamic_index_in_dim(split, core, 1, keepdims=False)
    other = swapped(lax.dynamic_index_in_dim(split, 1 - core, 1, keepdims=False), "c")
    first = jnp.where(core == 0, mine, other)
    second = jnp.where(core == 0, other, mine)
    return jnp.concatenate([first, second], axis=-1)


def summed_over_layer(partial_value):
    arrived = spread(partial_value.reshape(4, 2 * BS, BS), LAYER).reshape(2, 2, 2 * BS, BS)
    total = arrived.astype(jnp.float32).sum(axis=0)
    return jnp.concatenate([total[0], total[1]], axis=-1)


def on_device(
    root_values,
    root_columns,
    root_counts,
    fock_values,
    fock_columns,
    fock_counts,
    density_values,
    density_columns,
    density_counts,
):
    row, zh, core = (lax.axis_index(a) for a in ("row", "zh", "c"))
    target = row * 2 + core
    places = [
        jnp.stack([first, target]).astype(jnp.int32)
        for first in (zh * HALF, (1 - zh) * HALF, jnp.int32(0))
    ]

    def listed(*pairs):
        parts = [part for columns, counts in pairs for part in (columns[:, 0].T, counts.T)]
        own = jnp.concatenate(parts).reshape(-1)
        return own, swapped(own, "c")

    def pair(values):
        tiles = values[:, 0]
        return tiles, swapped(tiles, "c")

    def product(mat, metas, held, slab):
        def rows(place, count, dtype):
            return multiplied(mat, slab, metas, held, place, count, dtype)

        return rows

    def extraction(mat, metas, held):
        def rows(place, count, dtype):
            return extracted(mat, metas, held, place, count, dtype)

        return rows

    root = pair(root_values)
    root_metas = listed((root_columns, root_counts))
    root_slab = exchanged(extraction(0, root_metas, root), places)
    density = pair(density_values)
    fock = pair(fock_values)
    metas = listed((fock_columns, fock_counts), (density_columns, density_counts))
    density_slab = exchanged(extraction(1, metas, density), places)

    slab = gathered_x(gathered_z(root_slab))
    fock_inner = exchanged(product(0, metas, fock, slab), places)
    slab = gathered_x(gathered_z(density_slab))
    squared = exchanged(product(1, metas, density, slab), places)
    slab = gathered_x(gathered_z(fock_inner))
    fock_slab = exchanged(product(0, root_metas, root, slab), places)
    slab = gathered_x(gathered_z(squared))
    cubed_term = exchanged(product(1, metas, density, slab), places, jnp.float32)
    purified = 3.0 * squared.astype(jnp.float32) - 2.0 * cubed_term
    slab = gathered_x(gathered_z(fock_slab))
    outs = all_columns([fock_slab, purified.astype(jnp.bfloat16)])
    rows = product(1, metas, density, slab)
    energy = summed_over_layer(rows(places[2], RB, jnp.bfloat16))
    return outs[0], outs[1], energy.astype(jnp.bfloat16)


def solution(mesh):
    finer = Mesh(mesh.devices.reshape(mesh.shape["row"], 4, 4, 2, 2), ("row", *COL, *LAYER))
    specs = (P(COL, LAYER, None, None, None), P(COL, LAYER, None), P(COL, LAYER))

    return jax.shard_map(
        on_device,
        mesh=finer,
        in_specs=specs * 3,
        out_specs=(P((*COL, *LAYER), "row"),) * 3,
        check_vma=False,
    )
```

time: 274 us -> 249 us (0.909)
  the two profiles are of different devices: /device:TPU:74 before, /device:TPU:66 now
where the time goes in v2:
time: 249 us; the launch traced here: 247 us
  starting transfers between devices  89.9 us (36%)
  blocking collectives  71.9 us (29%)
  waiting for transfers between devices  33.5 us (13%)
  Pallas kernels  28.7 us (12%)
  local copies, waits for them, and re-layouts  18.6 us (7%)
  other arithmetic  3.49 us (1%)
    all_gather x5, blocking collectives, gathered_z(): return lax.all_gather(piece, 'zl', axis=0, tiled=True)  71.9 us
    ppermute x12, starting transfers between devices, swapped(): return lax.ppermute(value, axis, [(0, 1), (1, 0)])  58 us
    all_to_all x6, starting transfers between devices, spread(): return lax.all_to_all(value, axis, split_axis=0, concat_axis=0, tiled=True)  31.9 us
    pallas_call x13, Pallas kernels, local_call(): pl.pallas_call(kernel, out_shape=jax.ShapeDtypeStruct((count, BS, BS), dt...  26.7 us
    ppermute x12, waiting for transfers between devices, swapped(): return lax.ppermute(value, axis, [(0, 1), (1, 0)])  22.5 us
    unnamed x41, local copies, waits for them, and re-layouts  17.4 us
    all_to_all x6, waiting for transfers between devices, spread(): return lax.all_to_all(value, axis, split_axis=0, concat_axis=0, tiled=True)  11.1 us
  transfers between devices with their start and end apart: 18, of which 7 were waited for; matrix products, arithmetic and copies ran while one was open for 2% of the time, Pallas kernels for 12%

profile of v2, /device:TPU:66, one launch (start us, length us, event | category | flops | bytes accessed | tf_op | source)
XLA Modules:
  0.0 247.1 jit_solution(15507906198449402647)
XLA Ops:
  13.9 10.0 %collective-permute-start.4 = (bf16[4,128,128]{2,1,0:T(8,128)(2,1)S(1)}, bf16[4,128,128]{2,1,0:T(8,128)(2,1)S(1)}, u32[]{:S(2)}, u32[]{:S(2)}) collective-permute-start(bf16[4,128,128]{2,1,0:T(8,128)(2,1)S(1)} %shard_map.113), channel_id=1, source_target_pairs={{0,2},{2,0},{1,3},{3,1},{4,6},{6,4},{5,7},{7,5},{8,10},{10,8},{9,1... | collective-permute-start | bytes 393224 | tf_op jit(solution)/shard_map/ppermute | solution.py:24
  26.5 4.4 %collective-permute-done.4.arrived = bf16[4,128,128]{2,1,0:T(8,128)(2,1)S(1)} collective-permute-done((bf16[4,128,128]{2,1,0:T(8,128)(2,1)S(1)}, bf16[4,128,128]{2,1,0:T(8,128)(2,1)S(1)}, u32[]{:S(2)}, u32[]{:S(2)}) %collective-permute-start.4) | collective-permute-done | bytes 131104 | tf_op jit(solution)/shard_map/ppermute | solution.py:24
  31.0 13.2 %all_gather.15.piece = bf16[16,128,128]{2,1,0:T(8,128)(2,1)S(1)} all-gather(bf16[4,128,128]{2,1,0:T(8,128)(2,1)S(1)} %shard_map.114), channel_id=1, replica_groups=mesh['row'=8,'zl'=4,'x'=4,'zh'=2,'c'=2] {'zl'}, dimensions={0}, use_global_device_ids=true | all-gather | bytes 655360 | tf_op jit(solution)/shard_map/all_gather | solution.py:136
  45.8 5.2 %all-to-all-start = ((bf16[4,16,128,128]{3,2,1,0:T(8,128)(2,1)}), bf16[4,16,128,128]{3,2,1,0:T(8,128)(2,1)}, u32[]{:S(2)}, u32[]{:S(2)}) async-start(bf16[4,16,128,128]{3,2,1,0:T(8,128)(2,1)} %copy-done.9), calls=%async_computation | async-start | bytes 4194304 | tf_op jit(solution)/shard_map/all_to_all | solution.py:28
  57.1 7.1 %collective-permute-start.8 = (bf16[4,128,128]{2,1,0:T(8,128)(2,1)S(1)}, bf16[4,128,128]{2,1,0:T(8,128)(2,1)S(1)}, u32[]{:S(2)}, u32[]{:S(2)}) collective-permute-start(bf16[4,128,128]{2,1,0:T(8,128)(2,1)S(1)} %shard_map.124), channel_id=1, source_target_pairs={{0,2},{2,0},{1,3},{3,1},{4,6},{6,4},{5,7},{7,5},{8,10},{10,8},{9,1... | collective-permute-start | bytes 393224 | tf_op jit(solution)/shard_map/ppermute | solution.py:24
  65.3 5.8 %collective-permute-done.8.arrived = bf16[4,128,128]{2,1,0:T(8,128)(2,1)S(1)} collective-permute-done((bf16[4,128,128]{2,1,0:T(8,128)(2,1)S(1)}, bf16[4,128,128]{2,1,0:T(8,128)(2,1)S(1)}, u32[]{:S(2)}, u32[]{:S(2)}) %collective-permute-start.8) | collective-permute-done | bytes 131104 | tf_op jit(solution)/shard_map/ppermute | solution.py:24
  71.2 15.1 %all_gather.17.piece = bf16[16,128,128]{2,1,0:T(8,128)(2,1)S(1)} all-gather(bf16[4,128,128]{2,1,0:T(8,128)(2,1)S(1)} %shard_map.125), channel_id=1, replica_groups=mesh['row'=8,'zl'=4,'x'=4,'zh'=2,'c'=2] {'zl'}, dimensions={0}, use_global_device_ids=true | all-gather | bytes 655360 | tf_op jit(solution)/shard_map/all_gather | solution.py:136
  87.8 4.8 %all-to-all-start.2 = ((bf16[4,16,128,128]{3,2,1,0:T(8,128)(2,1)}), bf16[4,16,128,128]{3,2,1,0:T(8,128)(2,1)}, u32[]{:S(2)}, u32[]{:S(2)}) async-start(bf16[4,16,128,128]{3,2,1,0:T(8,128)(2,1)} %copy-done.11), calls=%async_computation.2 | async-start | bytes 4194304 | tf_op jit(solution)/shard_map/all_to_all | solution.py:28
  96.7 5.3 %collective-permute-start.5 = (bf16[4,128,128]{2,1,0:T(8,128)(2,1)S(1)}, bf16[4,128,128]{2,1,0:T(8,128)(2,1)S(1)}, u32[]{:S(2)}, u32[]{:S(2)}) collective-permute-start(bf16[4,128,128]{2,1,0:T(8,128)(2,1)S(1)} %shard_map.117), channel_id=1, source_target_pairs={{0,2},{2,0},{1,3},{3,1},{4,6},{6,4},{5,7},{7,5},{8,10},{10,8},{9,1... | collective-permute-start | bytes 393224 | tf_op jit(solution)/shard_map/ppermute | solution.py:24
  104.7 2.9 %collective-permute-done.5.arrived = bf16[4,128,128]{2,1,0:T(8,128)(2,1)S(1)} collective-permute-done((bf16[4,128,128]{2,1,0:T(8,128)(2,1)S(1)}, bf16[4,128,128]{2,1,0:T(8,128)(2,1)S(1)}, u32[]{:S(2)}, u32[]{:S(2)}) %collective-permute-start.5) | collective-permute-done | bytes 131104 | tf_op jit(solution)/shard_map/ppermute | solution.py:24
  107.7 16.5 %all_gather.16.piece = bf16[16,128,128]{2,1,0:T(8,128)(2,1)S(1)} all-gather(bf16[4,128,128]{2,1,0:T(8,128)(2,1)S(1)} %shard_map.118), channel_id=1, replica_groups=mesh['row'=8,'zl'=4,'x'=4,'zh'=2,'c'=2] {'zl'}, dimensions={0}, use_global_device_ids=true | all-gather | bytes 655360 | tf_op jit(solution)/shard_map/all_gather | solution.py:136
  125.7 4.8 %all-to-all-start.1 = ((bf16[4,16,128,128]{3,2,1,0:T(8,128)(2,1)}), bf16[4,16,128,128]{3,2,1,0:T(8,128)(2,1)}, u32[]{:S(2)}, u32[]{:S(2)}) async-start(bf16[4,16,128,128]{3,2,1,0:T(8,128)(2,1)} %copy-done.13), calls=%async_computation.1 | async-start | bytes 4194304 | tf_op jit(solution)/shard_map/all_to_all | solution.py:28
  132.7 6.5 %collective-permute-start.9 = (bf16[4,128,128]{2,1,0:T(8,128)(2,1)S(1)}, bf16[4,128,128]{2,1,0:T(8,128)(2,1)S(1)}, u32[]{:S(2)}, u32[]{:S(2)}) collective-permute-start(bf16[4,128,128]{2,1,0:T(8,128)(2,1)S(1)} %shard_map.128), channel_id=1, source_target_pairs={{0,2},{2,0},{1,3},{3,1},{4,6},{6,4},{5,7},{7,5},{8,10},{10,8},{9,1... | collective-permute-start | bytes 393224 | tf_op jit(solution)/shard_map/ppermute | solution.py:24
  141.5 3.7 %collective-permute-done.9.arrived = bf16[4,128,128]{2,1,0:T(8,128)(2,1)S(1)} collective-permute-done((bf16[4,128,128]{2,1,0:T(8,128)(2,1)S(1)}, bf16[4,128,128]{2,1,0:T(8,128)(2,1)S(1)}, u32[]{:S(2)}, u32[]{:S(2)}) %collective-permute-start.9) | collective-permute-done | bytes 131104 | tf_op jit(solution)/shard_map/ppermute | solution.py:24
  145.2 14.2 %all_gather.18.piece = bf16[16,128,128]{2,1,0:T(8,128)(2,1)S(1)} all-gather(bf16[4,128,128]{2,1,0:T(8,128)(2,1)S(1)} %shard_map.129), channel_id=1, replica_groups=mesh['row'=8,'zl'=4,'x'=4,'zh'=2,'c'=2] {'zl'}, dimensions={0}, use_global_device_ids=true | all-gather | bytes 655360 | tf_op jit(solution)/shard_map/all_gather | solution.py:136
  161.1 5.1 %all-to-all-start.3 = ((bf16[4,16,128,128]{3,2,1,0:T(8,128)(2,1)}), bf16[4,16,128,128]{3,2,1,0:T(8,128)(2,1)}, u32[]{:S(2)}, u32[]{:S(2)}) async-start(bf16[4,16,128,128]{3,2,1,0:T(8,128)(2,1)} %copy-done.12), calls=%async_computation.3 | async-start | bytes 4194304 | tf_op jit(solution)/shard_map/all_to_all | solution.py:28
  171.3 7.0 %collective-permute-start.6 = (bf16[4,128,128]{2,1,0:T(8,128)(2,1)S(1)}, bf16[4,128,128]{2,1,0:T(8,128)(2,1)S(1)}, u32[]{:S(2)}, u32[]{:S(2)}) collective-permute-start(bf16[4,128,128]{2,1,0:T(8,128)(2,1)S(1)} %shard_map.121), channel_id=1, source_target_pairs={{0,2},{2,0},{1,3},{3,1},{4,6},{6,4},{5,7},{7,5},{8,10},{10,8},{9,1... | collective-permute-start | bytes 393224 | tf_op jit(solution)/shard_map/ppermute | solution.py:24
  180.5 4.7 %collective-permute-done.6.arrived = bf16[4,128,128]{2,1,0:T(8,128)(2,1)S(1)} collective-permute-done((bf16[4,128,128]{2,1,0:T(8,128)(2,1)S(1)}, bf16[4,128,128]{2,1,0:T(8,128)(2,1)S(1)}, u32[]{:S(2)}, u32[]{:S(2)}) %collective-permute-start.6) | collective-permute-done | bytes 131104 | tf_op jit(solution)/shard_map/ppermute | solution.py:24
  185.3 12.9 %all_gather.19.piece = bf16[16,128,128]{2,1,0:T(8,128)(2,1)S(1)} all-gather(bf16[4,128,128]{2,1,0:T(8,128)(2,1)S(1)} %shard_map.122), channel_id=1, replica_groups=mesh['row'=8,'zl'=4,'x'=4,'zh'=2,'c'=2] {'zl'}, dimensions={0}, use_global_device_ids=true | all-gather | bytes 655360 | tf_op jit(solution)/shard_map/all_gather | solution.py:136
  199.7 4.8 %all-to-all-start.4 = ((bf16[4,16,128,128]{3,2,1,0:T(8,128)(2,1)}), bf16[4,16,128,128]{3,2,1,0:T(8,128)(2,1)}, u32[]{:S(2)}, u32[]{:S(2)}) async-start(bf16[4,16,128,128]{3,2,1,0:T(8,128)(2,1)} %copy-done.10), calls=%async_computation.4 | async-start | bytes 4194304 | tf_op jit(solution)/shard_map/all_to_all | solution.py:28
  206.7 9.6 %collective-permute-start.10 = (bf16[4,128,128]{2,1,0:T(8,128)(2,1)S(1)}, bf16[4,128,128]{2,1,0:T(8,128)(2,1)}, u32[]{:S(2)}, u32[]{:S(2)}) collective-permute-start(bf16[4,128,128]{2,1,0:T(8,128)(2,1)S(1)} %shard_map.132), channel_id=1, source_target_pairs={{0,2},{2,0},{1,3},{3,1},{4,6},{6,4},{5,7},{7,5},{8,10},{10,8},{9,1... | collective-permute-start | bytes 393224 | tf_op jit(solution)/shard_map/ppermute | solution.py:24
  223.0 3.3 %shard_map.135 = bf16[8,128,128]{2,1,0:T(8,128)(2,1)} custom-call(s32[112]{0:T(128)S(1)} %reshape.39.own_meta, s32[112]{0:T(128)S(1)} %collective-permute-done.2.other_meta, s32[2]{0:T(128)S(1)} %pad_add_fusion.4.place, bf16[8,6,128,128]{3,2,1,0:T(8,128)(2,1)S(1)} %bitcast.50, bf16[8,6,128,128]{3,2,1,0:T(8,128)(2,1)S(1)} %collective-permute-done.7.other, ...), custom_call_target="tpu_custom_call" | custom-call | flops 402653184 | bytes 3145728 | tf_op jit(solution)/shard_map/pallas_call | solution.py:78
  226.4 7.3 %all-to-all-start.5 = ((bf16[4,256,128]{2,1,0:T(8,128)(2,1)}), bf16[4,256,128]{2,1,0:T(8,128)(2,1)S(1)}, u32[]{:S(2)}, u32[]{:S(2)}) async-start(bf16[4,256,128]{2,1,0:T(8,128)(2,1)} %bitcast.26), calls=%async_computation.5 | async-start | bytes 524288 | tf_op jit(solution)/shard_map/all_to_all | solution.py:28
  235.3 11.1 %all-to-all-done.5 = bf16[4,256,128]{2,1,0:T(8,128)(2,1)S(1)} async-done(((bf16[4,256,128]{2,1,0:T(8,128)(2,1)}), bf16[4,256,128]{2,1,0:T(8,128)(2,1)S(1)}, u32[]{:S(2)}, u32[]{:S(2)}) %all-to-all-start.5) | async-done | bytes 262176 | tf_op jit(solution)/shard_map/all_to_all | solution.py:28
  (101 shorter events, 60.8 us)
Async XLA Ops:
  0.6 8.1 %collective-permute-start.1 = (bf16[8,6,128,128]{3,2,1,0:T(8,128)(2,1)}, bf16[8,6,128,128]{3,2,1,0:T(8,128)(2,1)S(1)}, u32[]{:S(2)}, u32[]{:S(2)}) collective-permute-start(bf16[8,6,128,128]{3,2,1,0:T(8,128)(2,1)} %bitcast.51), channel_id=1, source_target_pairs={{0,1},{1,0},{2,3},{3,2},{4,5},{5,4},{6,7},{7,6},{8,9},{9,8},{10,11... | collective-permute-start | bytes 4718600 | tf_op jit(solution)/shard_map/ppermute | solution.py:24
  4.3 4.4 %collective-permute-start = (s32[56]{0:T(128)S(1)}, s32[56]{0:T(128)S(1)}, u32[]{:S(2)}, u32[]{:S(2)}) collective-permute-start(s32[56]{0:T(128)S(1)} %reshape.38.own_meta), channel_id=1, source_target_pairs={{0,1},{1,0},{2,3},{3,2},{4,5},{5,4},{6,7},{7,6},{8,9},{9,8},{10,11... | collective-permute-start | bytes 680 | tf_op jit(solution)/shard_map/ppermute | solution.py:24
  6.7 49.2 %collective-permute-start.7 = (bf16[8,6,128,128]{3,2,1,0:T(8,128)(2,1)}, bf16[8,6,128,128]{3,2,1,0:T(8,128)(2,1)S(1)}, u32[]{:S(2)}, u32[]{:S(2)}) collective-permute-start(bf16[8,6,128,128]{3,2,1,0:T(8,128)(2,1)} %bitcast.43), channel_id=1, source_target_pairs={{0,1},{1,0},{2,3},{3,2},{4,5},{5,4},{6,7},{7,6},{8,9},{9,8},{10,11... | collective-permute-start | bytes 4718600 | tf_op jit(solution)/shard_map/ppermute | solution.py:24
  12.7 11.3 %copy-start.2 = (bf16[8,1,6,128,128]{4,3,2,1,0:T(8,128)(2,1)S(1)}, bf16[8,1,6,128,128]{4,3,2,1,0:T(8,128)(2,1)}, u32[]{:S(2)}) copy-start(bf16[8,1,6,128,128]{4,3,2,1,0:T(8,128)(2,1)} %param.9) | copy-start | bytes 4718596
  13.9 17.1 %collective-permute-start.4 = (bf16[4,128,128]{2,1,0:T(8,128)(2,1)S(1)}, bf16[4,128,128]{2,1,0:T(8,128)(2,1)S(1)}, u32[]{:S(2)}, u32[]{:S(2)}) collective-permute-start(bf16[4,128,128]{2,1,0:T(8,128)(2,1)S(1)} %shard_map.113), channel_id=1, source_target_pairs={{0,2},{2,0},{1,3},{3,1},{4,6},{6,4},{5,7},{7,5},{8,10},{10,8},{9,1... | collective-permute-start | bytes 393224 | tf_op jit(solution)/shard_map/ppermute | solution.py:24
  45.7 5.3 %copy-start.16 = (s32[8,1,6]{0,1,2:T(1,128)S(1)}, s32[8,1,6]{0,1,2:T(1,128)}, u32[]{:S(2)}) copy-start(s32[8,1,6]{0,1,2:T(1,128)} %param.13) | copy-start | bytes 580
  45.7 5.4 %copy-start.17 = (s32[8,1]{0,1:T(1,128)S(1)}, s32[8,1]{0,1:T(1,128)}, u32[]{:S(2)}) copy-start(s32[8,1]{0,1:T(1,128)} %param.14) | copy-start | bytes 100
  45.7 5.4 %copy-start.18 = (s32[8,1]{0,1:T(1,128)S(1)}, s32[8,1]{0,1:T(1,128)}, u32[]{:S(2)}) copy-start(s32[8,1]{0,1:T(1,128)} %param.17) | copy-start | bytes 100
  45.7 10.1 %copy-start = (bf16[8,1,6,128,128]{4,3,2,1,0:T(8,128)(2,1)S(1)}, bf16[8,1,6,128,128]{4,3,2,1,0:T(8,128)(2,1)}, u32[]{:S(2)}) copy-start(bf16[8,1,6,128,128]{4,3,2,1,0:T(8,128)(2,1)} %param.15) | copy-start | bytes 4718596
  45.8 42.0 %all-to-all-start = ((bf16[4,16,128,128]{3,2,1,0:T(8,128)(2,1)}), bf16[4,16,128,128]{3,2,1,0:T(8,128)(2,1)}, u32[]{:S(2)}, u32[]{:S(2)}) async-start(bf16[4,16,128,128]{3,2,1,0:T(8,128)(2,1)} %copy-done.9), calls=%async_computation | async-start | bytes 4194304 | tf_op jit(solution)/shard_map/all_to_all | solution.py:28
  51.5 4.3 %collective-permute-start.2 = (s32[112]{0:T(128)S(1)}, s32[112]{0:T(128)S(1)}, u32[]{:S(2)}, u32[]{:S(2)}) collective-permute-start(s32[112]{0:T(128)S(1)} %reshape.39.own_meta), channel_id=1, source_target_pairs={{0,1},{1,0},{2,3},{3,2},{4,5},{5,4},{6,7},{7,6},{8,9},{9,8},{10,11... | collective-permute-start | bytes 1352 | tf_op jit(solution)/shard_map/ppermute | solution.py:24
  53.5 39.1 %collective-permute-start.3 = (bf16[8,6,128,128]{3,2,1,0:T(8,128)(2,1)}, bf16[8,6,128,128]{3,2,1,0:T(8,128)(2,1)}, u32[]{:S(2)}, u32[]{:S(2)}) collective-permute-start(bf16[8,6,128,128]{3,2,1,0:T(8,128)(2,1)} %bitcast.56), channel_id=1, source_target_pairs={{0,1},{1,0},{2,3},{3,2},{4,5},{5,4},{6,7},{7,6},{8,9},{9,8},{10,11... | collective-permute-start | bytes 4718600 | tf_op jit(solution)/shard_map/ppermute | solution.py:24
  57.1 14.1 %collective-permute-start.8 = (bf16[4,128,128]{2,1,0:T(8,128)(2,1)S(1)}, bf16[4,128,128]{2,1,0:T(8,128)(2,1)S(1)}, u32[]{:S(2)}, u32[]{:S(2)}) collective-permute-start(bf16[4,128,128]{2,1,0:T(8,128)(2,1)S(1)} %shard_map.124), channel_id=1, source_target_pairs={{0,2},{2,0},{1,3},{3,1},{4,6},{6,4},{5,7},{7,5},{8,10},{10,8},{9,1... | collective-permute-start | bytes 393224 | tf_op jit(solution)/shard_map/ppermute | solution.py:24
  87.8 38.0 %all-to-all-start.2 = ((bf16[4,16,128,128]{3,2,1,0:T(8,128)(2,1)}), bf16[4,16,128,128]{3,2,1,0:T(8,128)(2,1)}, u32[]{:S(2)}, u32[]{:S(2)}) async-start(bf16[4,16,128,128]{3,2,1,0:T(8,128)(2,1)} %copy-done.11), calls=%async_computation.2 | async-start | bytes 4194304 | tf_op jit(solution)/shard_map/all_to_all | solution.py:28
  96.7 11.0 %collective-permute-start.5 = (bf16[4,128,128]{2,1,0:T(8,128)(2,1)S(1)}, bf16[4,128,128]{2,1,0:T(8,128)(2,1)S(1)}, u32[]{:S(2)}, u32[]{:S(2)}) collective-permute-start(bf16[4,128,128]{2,1,0:T(8,128)(2,1)S(1)} %shard_map.117), channel_id=1, source_target_pairs={{0,2},{2,0},{1,3},{3,1},{4,6},{6,4},{5,7},{7,5},{8,10},{10,8},{9,1... | collective-permute-start | bytes 393224 | tf_op jit(solution)/shard_map/ppermute | solution.py:24
  125.7 35.3 %all-to-all-start.1 = ((bf16[4,16,128,128]{3,2,1,0:T(8,128)(2,1)}), bf16[4,16,128,128]{3,2,1,0:T(8,128)(2,1)}, u32[]{:S(2)}, u32[]{:S(2)}) async-start(bf16[4,16,128,128]{3,2,1,0:T(8,128)(2,1)} %copy-done.13), calls=%async_computation.1 | async-start | bytes 4194304 | tf_op jit(solution)/shard_map/all_to_all | solution.py:28
  132.7 12.5 %collective-permute-start.9 = (bf16[4,128,128]{2,1,0:T(8,128)(2,1)S(1)}, bf16[4,128,128]{2,1,0:T(8,128)(2,1)S(1)}, u32[]{:S(2)}, u32[]{:S(2)}) collective-permute-start(bf16[4,128,128]{2,1,0:T(8,128)(2,1)S(1)} %shard_map.128), channel_id=1, source_target_pairs={{0,2},{2,0},{1,3},{3,1},{4,6},{6,4},{5,7},{7,5},{8,10},{10,8},{9,1... | collective-permute-start | bytes 393224 | tf_op jit(solution)/shard_map/ppermute | solution.py:24
  161.1 38.6 %all-to-all-start.3 = ((bf16[4,16,128,128]{3,2,1,0:T(8,128)(2,1)}), bf16[4,16,128,128]{3,2,1,0:T(8,128)(2,1)}, u32[]{:S(2)}, u32[]{:S(2)}) async-start(bf16[4,16,128,128]{3,2,1,0:T(8,128)(2,1)} %copy-done.12), calls=%async_computation.3 | async-start | bytes 4194304 | tf_op jit(solution)/shard_map/all_to_all | solution.py:28
  169.0 9.3 %copy-start.4 = (bf16[8,1,6,128,128]{4,3,2,1,0:T(8,128)(2,1)S(1)}, bf16[8,1,6,128,128]{4,3,2,1,0:T(8,128)(2,1)}, u32[]{:S(2)}) copy-start(bf16[8,1,6,128,128]{4,3,2,1,0:T(8,128)(2,1)} %param.9) | copy-start | bytes 4718596
  171.3 13.9 %collective-permute-start.6 = (bf16[4,128,128]{2,1,0:T(8,128)(2,1)S(1)}, bf16[4,128,128]{2,1,0:T(8,128)(2,1)S(1)}, u32[]{:S(2)}, u32[]{:S(2)}) collective-permute-start(bf16[4,128,128]{2,1,0:T(8,128)(2,1)S(1)} %shard_map.121), channel_id=1, source_target_pairs={{0,2},{2,0},{1,3},{3,1},{4,6},{6,4},{5,7},{7,5},{8,10},{10,8},{9,1... | collective-permute-start | bytes 393224 | tf_op jit(solution)/shard_map/ppermute | solution.py:24
  199.7 23.3 %all-to-all-start.4 = ((bf16[4,16,128,128]{3,2,1,0:T(8,128)(2,1)}), bf16[4,16,128,128]{3,2,1,0:T(8,128)(2,1)}, u32[]{:S(2)}, u32[]{:S(2)}) async-start(bf16[4,16,128,128]{3,2,1,0:T(8,128)(2,1)} %copy-done.10), calls=%async_computation.4 | async-start | bytes 4194304 | tf_op jit(solution)/shard_map/all_to_all | solution.py:28
  206.7 12.6 %collective-permute-start.10 = (bf16[4,128,128]{2,1,0:T(8,128)(2,1)S(1)}, bf16[4,128,128]{2,1,0:T(8,128)(2,1)}, u32[]{:S(2)}, u32[]{:S(2)}) collective-permute-start(bf16[4,128,128]{2,1,0:T(8,128)(2,1)S(1)} %shard_map.132), channel_id=1, source_target_pairs={{0,2},{2,0},{1,3},{3,1},{4,6},{6,4},{5,7},{7,5},{8,10},{10,8},{9,1... | collective-permute-start | bytes 393224 | tf_op jit(solution)/shard_map/ppermute | solution.py:24
  221.0 12.6 %collective-permute-start.11 = (bf16[2,256,128]{2,1,0:T(8,128)(2,1)}, bf16[2,256,128]{2,1,0:T(8,128)(2,1)}, u32[]{:S(2)}, u32[]{:S(2)}) collective-permute-start(bf16[2,256,128]{2,1,0:T(8,128)(2,1)} %fusion.3), channel_id=1, source_target_pairs={{0,1},{1,0},{2,3},{3,2},{4,5},{5,4},{6,7},{7,6},{8,9},{9,8},{10,11... | collective-permute-start | bytes 393224 | tf_op jit(solution)/shard_map/ppermute | solution.py:24
  226.4 20.0 %all-to-all-start.5 = ((bf16[4,256,128]{2,1,0:T(8,128)(2,1)}), bf16[4,256,128]{2,1,0:T(8,128)(2,1)S(1)}, u32[]{:S(2)}, u32[]{:S(2)}) async-start(bf16[4,256,128]{2,1,0:T(8,128)(2,1)} %bitcast.26), calls=%async_computation.5 | async-start | bytes 524288 | tf_op jit(solution)/shard_map/all_to_all | solution.py:28
  (13 other events, 21.7 us)

commit v3 on v2

--- a/solution.py
+++ b/solution.py
@@ -28,7 +28,7 @@
     return lax.all_to_all(value, axis, split_axis=0, concat_axis=0, tiled=True)
 
 
-def extract_kernel(mat, count, own_meta, other_meta, place, own, other, out, found, sems):
+def extract_kernel(mat, own_meta, other_meta, place, own, other, sent, kept, found, sems):
     def slot(meta, row):
         at, hit = jnp.int32(0), jnp.int32(0)
         listed = meta[(mat * META + KQ) * RB + row]
@@ -39,67 +39,127 @@
         return at, hit
 
     copies, hits = [], []
-    for r in range(count):
-        row = place[0] + r
+    for r in range(RB):
+        row = (place[0] + r) & (RB - 1)
         for side, (meta, tiles) in enumerate(((own_meta, own), (other_meta, other))):
             at, hit = slot(meta, row)
             copy = pltpu.make_async_copy(tiles.at[row, at], found.at[r, side], sems.at[r, side])
             copy.start()
             copies.append(copy)
             hits.append(hit)
-    for r in range(count):
+    for r in range(RB):
         copies[2 * r].wait()
         copies[2 * r + 1].wait()
         zero = jnp.zeros((BS, BS), found.dtype)
         tile = jnp.where(hits[2 * r] > 0, found[r, 0], zero)
-        out[r] = jnp.where(hits[2 * r + 1] > 0, found[r, 1], tile).astype(out.dtype)
+        tile = jnp.where(hits[2 * r + 1] > 0, found[r, 1], tile)
+        out = sent if r < HALF else kept
+        out[r % HALF] = tile.astype(out.dtype)
+
+
+def row_total(mat, row, metas, tiles, slab):
+    left, right = [], []
+    for side, meta in enumerate(metas):
+        listed = meta[(mat * META + KQ) * RB + row]
+        for k in range(KQ):
+            j = meta[(mat * META + k) * RB + row]
+            tile = tiles(side, k)
+            left.append(jnp.where(k < listed, tile, jnp.zeros_like(tile)))
+            right.append(slab[(((j >> 3) & 3) * 4 + (j >> 5)) * HALF + (j & 3)])
+    return jnp.dot(
+        jnp.concatenate(left, axis=1),
+        jnp.concatenate(right, axis=0),
+        preferred_element_type=jnp.float32,
+    )
 
 
 def product_kernel(mat, count, own_meta, other_meta, place, own, other, slab, out):
     for r in range(count):
         row = place[0] + r
-        left, right = [], []
-        for meta, tiles in ((own_meta, own), (other_meta, other)):
-            listed = meta[(mat * META + KQ) * RB + row]
-            for k in range(KQ):
-                j = meta[(mat * META + k) * RB + row]
-                tile = tiles[row, k]
-                left.append(jnp.where(k < listed, tile, jnp.zeros_like(tile)))
-                right.append(slab[(((j >> 3) & 3) * 4 + (j >> 5)) * HALF + (j & 3)])
-        total = jnp.dot(
-            jnp.concatenate(left, axis=1),
-            jnp.concatenate(right, axis=0),
-            preferred_element_type=jnp.float32,
-        )
+
+        def tiles(side, k, row=row):
+            return (own, other)[side][row, k]
+
+        total = row_total(mat, row, (own_meta, other_meta), tiles, slab)
         out[r] = total.astype(out.dtype)
 
 
-def local_call(kernel, place, metas, operands, space, count, dtype, scratch):
+def halves_kernel(mat, own_meta, other_meta, place, own, other, slab, sent, kept, held, near, sems):
+    slab_copy = pltpu.make_async_copy(slab, near, sems.at[2 * RB])
+    slab_copy.start()
+    copies = []
+    for r in range(RB):
+        row = (place[0] + r) & (RB - 1)
+        for side, ref in enumerate((own, other)):
+            to = held.at[r, pl.ds(side * KQ, KQ)]
+            copy = pltpu.make_async_copy(ref.at[row], to, sems.at[2 * r + side])
+            copy.start()
+            copies.append(copy)
+    slab_copy.wait()
+    for r in range(RB):
+        copies[2 * r].wait()
+        copies[2 * r + 1].wait()
+        row = (place[0] + r) & (RB - 1)
+
+        def tiles(side, k, r=r):
+            return held[r, side * KQ + k]
+
+        total = row_total(mat, row, (own_meta, other_meta), tiles, near)
+        out = sent if r < HALF else kept
+        out[r % HALF] = total.astype(out.dtype)
+
+
+def local_call(kernel, place, metas, operands, spaces, outs, scratch):
+    rows = sum(out.shape[0] for out in outs)
     return pl.pallas_call(
         kernel,
-        out_shape=jax.ShapeDtypeStruct((count, BS, BS), dtype),
+        out_shape=outs,
         in_specs=[pl.BlockSpec(memory_space=pltpu.SMEM)] * 3
-        + [pl.BlockSpec(memory_space=space) for _ in operands],
-        out_specs=pl.BlockSpec(memory_space=pltpu.VMEM),
+        + [pl.BlockSpec(memory_space=space) for space in spaces],
+        out_specs=[pl.BlockSpec(memory_space=pltpu.VMEM) for _ in outs],
         scratch_shapes=scratch,
         compiler_params=pltpu.CompilerParams(vmem_limit_bytes=VMEM),
         cost_estimate=pl.CostEstimate(
-            flops=2 * count * 2 * KQ * BS * BS * BS,
-            bytes_accessed=count * 2 * KQ * BS * BS * 2,
+            flops=2 * rows * 2 * KQ * BS * BS * BS,
+            bytes_accessed=rows * 2 * KQ * BS * BS * 2,
             transcendentals=0,
         ),
     )(*metas, place, *operands)
 
 
-def extracted(mat, metas, held, place, count, dtype):
-    scratch = [pltpu.VMEM((count, 2, BS, BS), jnp.bfloat16), pltpu.SemaphoreType.DMA((count, 2))]
-    kernel = functools.partial(extract_kernel, mat, count)
-    return local_call(kernel, place, metas, held, pl.ANY, count, dtype, scratch)
-
-
-def multiplied(mat, slab, metas, held, place, count, dtype):
+def rows_of(count, dtype):
+    return jax.ShapeDtypeStruct((count, BS, BS), dtype)
+
+
+HALVES = (rows_of(HALF, jnp.bfloat16), rows_of(HALF, jnp.float32))
+
+
+def in_hbm(value):
+    return pltpu.with_memory_space_constraint(value, pltpu.HBM)
+
+
+def extracted(mat, metas, held, places):
+    scratch = [pltpu.VMEM((RB, 2, BS, BS), jnp.bfloat16), pltpu.SemaphoreType.DMA((RB, 2))]
+    kernel = functools.partial(extract_kernel, mat)
+    return local_call(kernel, places[1], metas, held, [pl.ANY] * 2, HALVES, scratch)
+
+
+def halves(mat, metas, held, slab, places):
+    scratch = [
+        pltpu.VMEM((RB, 2 * KQ, BS, BS), jnp.bfloat16),
+        pltpu.VMEM((64, BS, BS), jnp.bfloat16),
+        pltpu.SemaphoreType.DMA((2 * RB + 1,)),
+    ]
+    kernel = functools.partial(halves_kernel, mat)
+    operands = [*map(in_hbm, held), slab]
+    spaces = [pltpu.HBM, pltpu.HBM, pl.ANY]
+    return local_call(kernel, places[1], metas, operands, spaces, HALVES, scratch)
+
+
+def multiplied(mat, metas, held, slab, place, count, dtype):
     kernel = functools.partial(product_kernel, mat, count)
-    return local_call(kernel, place, metas, [*held, slab], pltpu.VMEM, count, dtype, [])
+    outs = (rows_of(count, dtype),)
+    return local_call(kernel, place, metas, [*held, slab], [pltpu.VMEM] * 3, outs, [])[0]
 
 
 def add_kernel(kept, arrived, out):
@@ -125,10 +185,9 @@
     )(*operands)
 
 
-def exchanged(rows, places, dtype=jnp.bfloat16):
-    sent = rows(places[1], HALF, jnp.bfloat16)
+def exchanged(sent, kept, dtype=jnp.bfloat16):
     arrived = swapped(sent, "zh")
-    kept = rows(places[0], HALF, jnp.float32)
+    kept = kept()
     return small_call(add_kernel, [kept, arrived], kept.shape, pltpu.VMEM, [], dtype)
 
 
@@ -185,39 +244,37 @@
         tiles = values[:, 0]
         return tiles, swapped(tiles, "c")
 
-    def product(mat, metas, held, slab):
-        def rows(place, count, dtype):
-            return multiplied(mat, slab, metas, held, place, count, dtype)
-
-        return rows
-
-    def extraction(mat, metas, held):
-        def rows(place, count, dtype):
-            return extracted(mat, metas, held, place, count, dtype)
-
-        return rows
+    def at_once(pieces):
+        return exchanged(pieces[0], lambda: pieces[1])
+
+    def in_turn(mat, held, slab, dtype=jnp.bfloat16):
+        sent = multiplied(mat, metas, held, slab, places[1], HALF, jnp.bfloat16)
+        kept = functools.partial(multiplied, mat, metas, held, slab, places[0], HALF, jnp.float32)
+        return exchanged(sent, kept, dtype)
 
     root = pair(root_values)
     root_metas = listed((root_columns, root_counts))
-    root_slab = exchanged(extraction(0, root_metas, root), places)
+    root_slab = at_once(extracted(0, root_metas, [*map(in_hbm, root)], places))
     density = pair(density_values)
     fock = pair(fock_values)
-    metas = listed((fock_columns, fock_counts), (density_columns, density_counts))
-    density_slab = exchanged(extraction(1, metas, density), places)
+    metas = listed(
+        (fock_columns, fock_counts), (density_columns, density_counts), (root_columns, root_counts)
+    )
+    density_slab = at_once(extracted(1, metas, density, places))
 
     slab = gathered_x(gathered_z(root_slab))
-    fock_inner = exchanged(product(0, metas, fock, slab), places)
+    fock_inner = at_once(halves(0, metas, fock, slab, places))
     slab = gathered_x(gathered_z(density_slab))
-    squared = exchanged(product(1, metas, density, slab), places)
+    squared = in_turn(1, density, slab)
     slab = gathered_x(gathered_z(fock_inner))
-    fock_slab = exchanged(product(0, root_metas, root, slab), places)
+    fock_slab = at_once(halves(2, metas, root, slab, places))
     slab = gathered_x(gathered_z(squared))
-    cubed_term = exchanged(product(1, metas, density, slab), places, jnp.float32)
+    cubed_term = in_turn(1, density, slab, jnp.float32)
     purified = 3.0 * squared.astype(jnp.float32) - 2.0 * cubed_term
     slab = gathered_x(gathered_z(fock_slab))
     outs = all_columns([fock_slab, purified.astype(jnp.bfloat16)])
-    rows = product(1, metas, density, slab)
-    energy = summed_over_layer(rows(places[2], RB, jnp.bfloat16))
+    rows = multiplied(1, metas, density, slab, places[2], RB, jnp.bfloat16)
+    energy = summed_over_layer(rows)
     return outs[0], outs[1], energy.astype(jnp.bfloat16)
 
 

time: 249 us -> 246 us (0.988)
  the two profiles are of different devices: /device:TPU:66 before, /device:TPU:98 now
where the time goes in v3:
time: 246 us; the launch traced here: 245 us
  starting transfers between devices  88.8 us (36%)
  blocking collectives  72.8 us (30%)
  waiting for transfers between devices  42.9 us (17%)
  Pallas kernels  26.7 us (11%)
  local copies, waits for them, and re-layouts  9.07 us (4%)
  other arithmetic  3.41 us (1%)
    all_gather x5, blocking collectives, gathered_z(): return lax.all_gather(piece, 'zl', axis=0, tiled=True)  72.8 us
    ppermute x12, starting transfers between devices, swapped(): return lax.ppermute(value, axis, [(0, 1), (1, 0)])  56.7 us
    all_to_all x6, starting transfers between devices, spread(): return lax.all_to_all(value, axis, split_axis=0, concat_axis=0, tiled=True)  32.1 us
    ppermute x12, waiting for transfers between devices, swapped(): return lax.ppermute(value, axis, [(0, 1), (1, 0)])  31.8 us
    pallas_call x9, Pallas kernels, local_call(): pl.pallas_call(kernel, out_shape=outs, in_specs=[pl.BlockSpec(memory_spac...  24.8 us
    all_to_all x6, waiting for transfers between devices, spread(): return lax.all_to_all(value, axis, split_axis=0, concat_axis=0, tiled=True)  11.1 us
    unnamed x23, local copies, waits for them, and re-layouts  7.75 us
  transfers between devices with their start and end apart: 18, of which 7 were waited for; matrix products, arithmetic and copies ran while one was open for 2% of the time, Pallas kernels for 11%

profile of v3, /device:TPU:98, one launch (start us, length us, event | category | flops | bytes accessed | tf_op | source)
XLA Modules:
  0.0 244.7 jit_solution(5626858221367766846)
XLA Ops:
  10.5 10.0 %collective-permute-start.4 = (bf16[4,128,128]{2,1,0:T(8,128)(2,1)S(1)}, bf16[4,128,128]{2,1,0:T(8,128)(2,1)S(1)}, u32[]{:S(2)}, u32[]{:S(2)}) collective-permute-start(bf16[4,128,128]{2,1,0:T(8,128)(2,1)S(1)} %get-tuple-element.12), channel_id=1, source_target_pairs={{0,2},{2,0},{1,3},{3,1},{4,6},{6,4},{5,7},{7,5},{8,10},{10,8},{9,1... | collective-permute-start | bytes 393224 | tf_op jit(solution)/shard_map/ppermute | solution.py:24
  20.5 7.1 %collective-permute-done.4.arrived = bf16[4,128,128]{2,1,0:T(8,128)(2,1)S(1)} collective-permute-done((bf16[4,128,128]{2,1,0:T(8,128)(2,1)S(1)}, bf16[4,128,128]{2,1,0:T(8,128)(2,1)S(1)}, u32[]{:S(2)}, u32[]{:S(2)}) %collective-permute-start.4) | collective-permute-done | bytes 131104 | tf_op jit(solution)/shard_map/ppermute | solution.py:24
  27.6 13.2 %all_gather.15.piece = bf16[16,128,128]{2,1,0:T(8,128)(2,1)S(1)} all-gather(bf16[4,128,128]{2,1,0:T(8,128)(2,1)S(1)} %shard_map.113), channel_id=1, replica_groups=mesh['row'=8,'zl'=4,'x'=4,'zh'=2,'c'=2] {'zl'}, dimensions={0}, use_global_device_ids=true | all-gather | bytes 655360 | tf_op jit(solution)/shard_map/all_gather | solution.py:195
  42.4 5.1 %all-to-all-start = ((bf16[4,16,128,128]{3,2,1,0:T(8,128)(2,1)}), bf16[4,16,128,128]{3,2,1,0:T(8,128)(2,1)}, u32[]{:S(2)}, u32[]{:S(2)}) async-start(bf16[4,16,128,128]{3,2,1,0:T(8,128)(2,1)} %copy-done.1), calls=%async_computation | async-start | bytes 4194304 | tf_op jit(solution)/shard_map/all_to_all | solution.py:28
  54.3 7.1 %collective-permute-start.8 = (bf16[4,128,128]{2,1,0:T(8,128)(2,1)S(1)}, bf16[4,128,128]{2,1,0:T(8,128)(2,1)S(1)}, u32[]{:S(2)}, u32[]{:S(2)}) collective-permute-start(bf16[4,128,128]{2,1,0:T(8,128)(2,1)S(1)} %get-tuple-element.18), channel_id=1, source_target_pairs={{0,2},{2,0},{1,3},{3,1},{4,6},{6,4},{5,7},{7,5},{8,10},{10,8},{9,1... | collective-permute-start | bytes 393224 | tf_op jit(solution)/shard_map/ppermute | solution.py:24
  61.4 7.0 %collective-permute-done.8.arrived = bf16[4,128,128]{2,1,0:T(8,128)(2,1)S(1)} collective-permute-done((bf16[4,128,128]{2,1,0:T(8,128)(2,1)S(1)}, bf16[4,128,128]{2,1,0:T(8,128)(2,1)S(1)}, u32[]{:S(2)}, u32[]{:S(2)}) %collective-permute-start.8) | collective-permute-done | bytes 131104 | tf_op jit(solution)/shard_map/ppermute | solution.py:24
  68.4 15.5 %all_gather.17.piece = bf16[16,128,128]{2,1,0:T(8,128)(2,1)S(1)} all-gather(bf16[4,128,128]{2,1,0:T(8,128)(2,1)S(1)} %shard_map.121), channel_id=1, replica_groups=mesh['row'=8,'zl'=4,'x'=4,'zh'=2,'c'=2] {'zl'}, dimensions={0}, use_global_device_ids=true | all-gather | bytes 655360 | tf_op jit(solution)/shard_map/all_gather | solution.py:195
  85.4 4.8 %all-to-all-start.2 = ((bf16[4,16,128,128]{3,2,1,0:T(8,128)(2,1)}), bf16[4,16,128,128]{3,2,1,0:T(8,128)(2,1)}, u32[]{:S(2)}, u32[]{:S(2)}) async-start(bf16[4,16,128,128]{3,2,1,0:T(8,128)(2,1)} %copy-done.3), calls=%async_computation.2 | async-start | bytes 4194304 | tf_op jit(solution)/shard_map/all_to_all | solution.py:28
  90.2 4.5 %shard_map.115 = (bf16[4,128,128]{2,1,0:T(8,128)(2,1)S(1)}, f32[4,128,128]{2,1,0:T(8,128)S(1)}) custom-call(s32[168]{0:T(256)S(1)} %reshape.38.own_meta, s32[168]{0:T(256)S(1)} %collective-permute-done.other_meta, s32[2]{0:T(128)S(1)} %pad_add_fusion.1.place, bf16[8,6,128,128]{3,2,1,0:T(8,128)(2,1)} %bitcast.56, ...), custom_call_target="tpu_custom_call" | custom-call | flops 402653184 | bytes 3145728 | tf_op jit(solution)/shard_map/pallas_call | solution.py:114
  94.7 4.9 %collective-permute-start.5 = (bf16[4,128,128]{2,1,0:T(8,128)(2,1)S(1)}, bf16[4,128,128]{2,1,0:T(8,128)(2,1)S(1)}, u32[]{:S(2)}, u32[]{:S(2)}) collective-permute-start(bf16[4,128,128]{2,1,0:T(8,128)(2,1)S(1)} %get-tuple-element.14), channel_id=1, source_target_pairs={{0,2},{2,0},{1,3},{3,1},{4,6},{6,4},{5,7},{7,5},{8,10},{10,8},{9,1... | collective-permute-start | bytes 393224 | tf_op jit(solution)/shard_map/ppermute | solution.py:24
  99.6 6.1 %collective-permute-done.5.arrived = bf16[4,128,128]{2,1,0:T(8,128)(2,1)S(1)} collective-permute-done((bf16[4,128,128]{2,1,0:T(8,128)(2,1)S(1)}, bf16[4,128,128]{2,1,0:T(8,128)(2,1)S(1)}, u32[]{:S(2)}, u32[]{:S(2)}) %collective-permute-start.5) | collective-permute-done | bytes 131104 | tf_op jit(solution)/shard_map/ppermute | solution.py:24
  105.7 16.0 %all_gather.16.piece = bf16[16,128,128]{2,1,0:T(8,128)(2,1)S(1)} all-gather(bf16[4,128,128]{2,1,0:T(8,128)(2,1)S(1)} %shard_map.116), channel_id=1, replica_groups=mesh['row'=8,'zl'=4,'x'=4,'zh'=2,'c'=2] {'zl'}, dimensions={0}, use_global_device_ids=true | all-gather | bytes 655360 | tf_op jit(solution)/shard_map/all_gather | solution.py:195
  123.3 5.0 %all-to-all-start.1 = ((bf16[4,16,128,128]{3,2,1,0:T(8,128)(2,1)}), bf16[4,16,128,128]{3,2,1,0:T(8,128)(2,1)}, u32[]{:S(2)}, u32[]{:S(2)}) async-start(bf16[4,16,128,128]{3,2,1,0:T(8,128)(2,1)} %copy-done.4), calls=%async_computation.1 | async-start | bytes 4194304 | tf_op jit(solution)/shard_map/all_to_all | solution.py:28
  130.5 6.4 %collective-permute-start.9 = (bf16[4,128,128]{2,1,0:T(8,128)(2,1)S(1)}, bf16[4,128,128]{2,1,0:T(8,128)(2,1)S(1)}, u32[]{:S(2)}, u32[]{:S(2)}) collective-permute-start(bf16[4,128,128]{2,1,0:T(8,128)(2,1)S(1)} %shard_map.124), channel_id=1, source_target_pairs={{0,2},{2,0},{1,3},{3,1},{4,6},{6,4},{5,7},{7,5},{8,10},{10,8},{9,1... | collective-permute-start | bytes 393224 | tf_op jit(solution)/shard_map/ppermute | solution.py:24
  142.8 15.2 %all_gather.18.piece = bf16[16,128,128]{2,1,0:T(8,128)(2,1)S(1)} all-gather(bf16[4,128,128]{2,1,0:T(8,128)(2,1)S(1)} %shard_map.125), channel_id=1, replica_groups=mesh['row'=8,'zl'=4,'x'=4,'zh'=2,'c'=2] {'zl'}, dimensions={0}, use_global_device_ids=true | all-gather | bytes 655360 | tf_op jit(solution)/shard_map/all_gather | solution.py:195
  159.6 4.8 %all-to-all-start.3 = ((bf16[4,16,128,128]{3,2,1,0:T(8,128)(2,1)}), bf16[4,16,128,128]{3,2,1,0:T(8,128)(2,1)}, u32[]{:S(2)}, u32[]{:S(2)}) async-start(bf16[4,16,128,128]{3,2,1,0:T(8,128)(2,1)} %copy-done.5), calls=%async_computation.3 | async-start | bytes 4194304 | tf_op jit(solution)/shard_map/all_to_all | solution.py:28
  164.4 4.5 %shard_map.118 = (bf16[4,128,128]{2,1,0:T(8,128)(2,1)S(1)}, f32[4,128,128]{2,1,0:T(8,128)S(1)}) custom-call(s32[168]{0:T(256)S(1)} %reshape.38.own_meta, s32[168]{0:T(256)S(1)} %collective-permute-done.other_meta, s32[2]{0:T(128)S(1)} %pad_add_fusion.1.place, bf16[8,6,128,128]{3,2,1,0:T(8,128)(2,1)} %bitcast.54, ...), custom_call_target="tpu_custom_call" | custom-call | flops 402653184 | bytes 3145728 | tf_op jit(solution)/shard_map/pallas_call | solution.py:114
  168.9 6.6 %collective-permute-start.6 = (bf16[4,128,128]{2,1,0:T(8,128)(2,1)S(1)}, bf16[4,128,128]{2,1,0:T(8,128)(2,1)S(1)}, u32[]{:S(2)}, u32[]{:S(2)}) collective-permute-start(bf16[4,128,128]{2,1,0:T(8,128)(2,1)S(1)} %get-tuple-element.16), channel_id=1, source_target_pairs={{0,2},{2,0},{1,3},{3,1},{4,6},{6,4},{5,7},{7,5},{8,10},{10,8},{9,1... | collective-permute-start | bytes 393224 | tf_op jit(solution)/shard_map/ppermute | solution.py:24
  175.5 7.3 %collective-permute-done.6.arrived = bf16[4,128,128]{2,1,0:T(8,128)(2,1)S(1)} collective-permute-done((bf16[4,128,128]{2,1,0:T(8,128)(2,1)S(1)}, bf16[4,128,128]{2,1,0:T(8,128)(2,1)S(1)}, u32[]{:S(2)}, u32[]{:S(2)}) %collective-permute-start.6) | collective-permute-done | bytes 131104 | tf_op jit(solution)/shard_map/ppermute | solution.py:24
  182.8 13.0 %all_gather.19.piece = bf16[16,128,128]{2,1,0:T(8,128)(2,1)S(1)} all-gather(bf16[4,128,128]{2,1,0:T(8,128)(2,1)S(1)} %shard_map.119), channel_id=1, replica_groups=mesh['row'=8,'zl'=4,'x'=4,'zh'=2,'c'=2] {'zl'}, dimensions={0}, use_global_device_ids=true | all-gather | bytes 655360 | tf_op jit(solution)/shard_map/all_gather | solution.py:195
  197.3 5.1 %all-to-all-start.4 = ((bf16[4,16,128,128]{3,2,1,0:T(8,128)(2,1)}), bf16[4,16,128,128]{3,2,1,0:T(8,128)(2,1)}, u32[]{:S(2)}, u32[]{:S(2)}) async-start(bf16[4,16,128,128]{3,2,1,0:T(8,128)(2,1)} %copy-done.2), calls=%async_computation.4 | async-start | bytes 4194304 | tf_op jit(solution)/shard_map/all_to_all | solution.py:28
  204.6 9.2 %collective-permute-start.10 = (bf16[4,128,128]{2,1,0:T(8,128)(2,1)S(1)}, bf16[4,128,128]{2,1,0:T(8,128)(2,1)}, u32[]{:S(2)}, u32[]{:S(2)}) collective-permute-start(bf16[4,128,128]{2,1,0:T(8,128)(2,1)S(1)} %shard_map.128), channel_id=1, source_target_pairs={{0,2},{2,0},{1,3},{3,1},{4,6},{6,4},{5,7},{7,5},{8,10},{10,8},{9,1... | collective-permute-start | bytes 393224 | tf_op jit(solution)/shard_map/ppermute | solution.py:24
  223.9 7.3 %all-to-all-start.5 = ((bf16[4,256,128]{2,1,0:T(8,128)(2,1)}), bf16[4,256,128]{2,1,0:T(8,128)(2,1)S(1)}, u32[]{:S(2)}, u32[]{:S(2)}) async-start(bf16[4,256,128]{2,1,0:T(8,128)(2,1)} %bitcast.27), calls=%async_computation.5 | async-start | bytes 524288 | tf_op jit(solution)/shard_map/all_to_all | solution.py:28
  232.9 11.1 %all-to-all-done.5 = bf16[4,256,128]{2,1,0:T(8,128)(2,1)S(1)} async-done(((bf16[4,256,128]{2,1,0:T(8,128)(2,1)}), bf16[4,256,128]{2,1,0:T(8,128)(2,1)S(1)}, u32[]{:S(2)}, u32[]{:S(2)}) %all-to-all-start.5) | async-done | bytes 262176 | tf_op jit(solution)/shard_map/all_to_all | solution.py:28
  (79 shorter events, 47.1 us)
Async XLA Ops:
  0.6 8.1 %collective-permute-start.1 = (bf16[8,6,128,128]{3,2,1,0:T(8,128)(2,1)}, bf16[8,6,128,128]{3,2,1,0:T(8,128)(2,1)}, u32[]{:S(2)}, u32[]{:S(2)}) collective-permute-start(bf16[8,6,128,128]{3,2,1,0:T(8,128)(2,1)} %bitcast.52), channel_id=1, source_target_pairs={{0,1},{1,0},{2,3},{3,2},{4,5},{5,4},{6,7},{7,6},{8,9},{9,8},{10,11... | collective-permute-start | bytes 4718600 | tf_op jit(solution)/shard_map/ppermute | solution.py:24
  4.3 4.4 %collective-permute-start.3 = (s32[56]{0:T(128)S(1)}, s32[56]{0:T(128)S(1)}, u32[]{:S(2)}, u32[]{:S(2)}) collective-permute-start(s32[56]{0:T(128)S(1)} %reshape.39.own_meta), channel_id=1, source_target_pairs={{0,1},{1,0},{2,3},{3,2},{4,5},{5,4},{6,7},{7,6},{8,9},{9,8},{10,11... | collective-permute-start | bytes 680 | tf_op jit(solution)/shard_map/ppermute | solution.py:24
  6.7 45.7 %collective-permute-start.7 = (bf16[8,6,128,128]{3,2,1,0:T(8,128)(2,1)}, bf16[8,6,128,128]{3,2,1,0:T(8,128)(2,1)S(1)}, u32[]{:S(2)}, u32[]{:S(2)}) collective-permute-start(bf16[8,6,128,128]{3,2,1,0:T(8,128)(2,1)} %bitcast.43), channel_id=1, source_target_pairs={{0,1},{1,0},{2,3},{3,2},{4,5},{5,4},{6,7},{7,6},{8,9},{9,8},{10,11... | collective-permute-start | bytes 4718600 | tf_op jit(solution)/shard_map/ppermute | solution.py:24
  10.5 17.1 %collective-permute-start.4 = (bf16[4,128,128]{2,1,0:T(8,128)(2,1)S(1)}, bf16[4,128,128]{2,1,0:T(8,128)(2,1)S(1)}, u32[]{:S(2)}, u32[]{:S(2)}) collective-permute-start(bf16[4,128,128]{2,1,0:T(8,128)(2,1)S(1)} %get-tuple-element.12), channel_id=1, source_target_pairs={{0,2},{2,0},{1,3},{3,1},{4,6},{6,4},{5,7},{7,5},{8,10},{10,8},{9,1... | collective-permute-start | bytes 393224 | tf_op jit(solution)/shard_map/ppermute | solution.py:24
  42.4 5.1 %copy-start.6 = (s32[8,1,6]{0,1,2:T(1,128)S(1)}, s32[8,1,6]{0,1,2:T(1,128)}, u32[]{:S(2)}) copy-start(s32[8,1,6]{0,1,2:T(1,128)} %param.13) | copy-start | bytes 580
  42.4 5.2 %copy-start.7 = (s32[8,1,6]{0,1,2:T(1,128)S(1)}, s32[8,1,6]{0,1,2:T(1,128)}, u32[]{:S(2)}) copy-start(s32[8,1,6]{0,1,2:T(1,128)} %param.16) | copy-start | bytes 580
  42.4 5.3 %copy-start.8 = (s32[8,1]{0,1:T(1,128)S(1)}, s32[8,1]{0,1:T(1,128)}, u32[]{:S(2)}) copy-start(s32[8,1]{0,1:T(1,128)} %param.14) | copy-start | bytes 100
  42.4 5.4 %copy-start.9 = (s32[8,1]{0,1:T(1,128)S(1)}, s32[8,1]{0,1:T(1,128)}, u32[]{:S(2)}) copy-start(s32[8,1]{0,1:T(1,128)} %param.17) | copy-start | bytes 100
  42.4 10.1 %copy-start = (bf16[8,1,6,128,128]{4,3,2,1,0:T(8,128)(2,1)S(1)}, bf16[8,1,6,128,128]{4,3,2,1,0:T(8,128)(2,1)}, u32[]{:S(2)}) copy-start(bf16[8,1,6,128,128]{4,3,2,1,0:T(8,128)(2,1)} %param.15) | copy-start | bytes 4718596
  42.4 43.0 %all-to-all-start = ((bf16[4,16,128,128]{3,2,1,0:T(8,128)(2,1)}), bf16[4,16,128,128]{3,2,1,0:T(8,128)(2,1)}, u32[]{:S(2)}, u32[]{:S(2)}) async-start(bf16[4,16,128,128]{3,2,1,0:T(8,128)(2,1)} %copy-done.1), calls=%async_computation | async-start | bytes 4194304 | tf_op jit(solution)/shard_map/all_to_all | solution.py:28
  48.1 4.3 %collective-permute-start = (s32[168]{0:T(256)S(1)}, s32[168]{0:T(256)S(1)}, u32[]{:S(2)}, u32[]{:S(2)}) collective-permute-start(s32[168]{0:T(256)S(1)} %reshape.38.own_meta), channel_id=1, source_target_pairs={{0,1},{1,0},{2,3},{3,2},{4,5},{5,4},{6,7},{7,6},{8,9},{9,8},{10,11... | collective-permute-start | bytes 2024 | tf_op jit(solution)/shard_map/ppermute | solution.py:24
  50.0 40.1 %collective-permute-start.2 = (bf16[8,6,128,128]{3,2,1,0:T(8,128)(2,1)}, bf16[8,6,128,128]{3,2,1,0:T(8,128)(2,1)}, u32[]{:S(2)}, u32[]{:S(2)}) collective-permute-start(bf16[8,6,128,128]{3,2,1,0:T(8,128)(2,1)} %bitcast.55), channel_id=1, source_target_pairs={{0,1},{1,0},{2,3},{3,2},{4,5},{5,4},{6,7},{7,6},{8,9},{9,8},{10,11... | collective-permute-start | bytes 4718600 | tf_op jit(solution)/shard_map/ppermute | solution.py:24
  54.3 14.1 %collective-permute-start.8 = (bf16[4,128,128]{2,1,0:T(8,128)(2,1)S(1)}, bf16[4,128,128]{2,1,0:T(8,128)(2,1)S(1)}, u32[]{:S(2)}, u32[]{:S(2)}) collective-permute-start(bf16[4,128,128]{2,1,0:T(8,128)(2,1)S(1)} %get-tuple-element.18), channel_id=1, source_target_pairs={{0,2},{2,0},{1,3},{3,1},{4,6},{6,4},{5,7},{7,5},{8,10},{10,8},{9,1... | collective-permute-start | bytes 393224 | tf_op jit(solution)/shard_map/ppermute | solution.py:24
  85.4 37.9 %all-to-all-start.2 = ((bf16[4,16,128,128]{3,2,1,0:T(8,128)(2,1)}), bf16[4,16,128,128]{3,2,1,0:T(8,128)(2,1)}, u32[]{:S(2)}, u32[]{:S(2)}) async-start(bf16[4,16,128,128]{3,2,1,0:T(8,128)(2,1)} %copy-done.3), calls=%async_computation.2 | async-start | bytes 4194304 | tf_op jit(solution)/shard_map/all_to_all | solution.py:28
  94.7 11.0 %collective-permute-start.5 = (bf16[4,128,128]{2,1,0:T(8,128)(2,1)S(1)}, bf16[4,128,128]{2,1,0:T(8,128)(2,1)S(1)}, u32[]{:S(2)}, u32[]{:S(2)}) collective-permute-start(bf16[4,128,128]{2,1,0:T(8,128)(2,1)S(1)} %get-tuple-element.14), channel_id=1, source_target_pairs={{0,2},{2,0},{1,3},{3,1},{4,6},{6,4},{5,7},{7,5},{8,10},{10,8},{9,1... | collective-permute-start | bytes 393224 | tf_op jit(solution)/shard_map/ppermute | solution.py:24
  123.3 36.3 %all-to-all-start.1 = ((bf16[4,16,128,128]{3,2,1,0:T(8,128)(2,1)}), bf16[4,16,128,128]{3,2,1,0:T(8,128)(2,1)}, u32[]{:S(2)}, u32[]{:S(2)}) async-start(bf16[4,16,128,128]{3,2,1,0:T(8,128)(2,1)} %copy-done.4), calls=%async_computation.1 | async-start | bytes 4194304 | tf_op jit(solution)/shard_map/all_to_all | solution.py:28
  130.5 12.3 %collective-permute-start.9 = (bf16[4,128,128]{2,1,0:T(8,128)(2,1)S(1)}, bf16[4,128,128]{2,1,0:T(8,128)(2,1)S(1)}, u32[]{:S(2)}, u32[]{:S(2)}) collective-permute-start(bf16[4,128,128]{2,1,0:T(8,128)(2,1)S(1)} %shard_map.124), channel_id=1, source_target_pairs={{0,2},{2,0},{1,3},{3,1},{4,6},{6,4},{5,7},{7,5},{8,10},{10,8},{9,1... | collective-permute-start | bytes 393224 | tf_op jit(solution)/shard_map/ppermute | solution.py:24
  158.2 1.4 copy-start.5
  159.6 37.7 %all-to-all-start.3 = ((bf16[4,16,128,128]{3,2,1,0:T(8,128)(2,1)}), bf16[4,16,128,128]{3,2,1,0:T(8,128)(2,1)}, u32[]{:S(2)}, u32[]{:S(2)}) async-start(bf16[4,16,128,128]{3,2,1,0:T(8,128)(2,1)} %copy-done.5), calls=%async_computation.3 | async-start | bytes 4194304 | tf_op jit(solution)/shard_map/all_to_all | solution.py:28
  168.9 13.8 %collective-permute-start.6 = (bf16[4,128,128]{2,1,0:T(8,128)(2,1)S(1)}, bf16[4,128,128]{2,1,0:T(8,128)(2,1)S(1)}, u32[]{:S(2)}, u32[]{:S(2)}) collective-permute-start(bf16[4,128,128]{2,1,0:T(8,128)(2,1)S(1)} %get-tuple-element.16), channel_id=1, source_target_pairs={{0,2},{2,0},{1,3},{3,1},{4,6},{6,4},{5,7},{7,5},{8,10},{10,8},{9,1... | collective-permute-start | bytes 393224 | tf_op jit(solution)/shard_map/ppermute | solution.py:24
  197.3 23.3 %all-to-all-start.4 = ((bf16[4,16,128,128]{3,2,1,0:T(8,128)(2,1)}), bf16[4,16,128,128]{3,2,1,0:T(8,128)(2,1)}, u32[]{:S(2)}, u32[]{:S(2)}) async-start(bf16[4,16,128,128]{3,2,1,0:T(8,128)(2,1)} %copy-done.2), calls=%async_computation.4 | async-start | bytes 4194304 | tf_op jit(solution)/shard_map/all_to_all | solution.py:28
  204.6 12.3 %collective-permute-start.10 = (bf16[4,128,128]{2,1,0:T(8,128)(2,1)S(1)}, bf16[4,128,128]{2,1,0:T(8,128)(2,1)}, u32[]{:S(2)}, u32[]{:S(2)}) collective-permute-start(bf16[4,128,128]{2,1,0:T(8,128)(2,1)S(1)} %shard_map.128), channel_id=1, source_target_pairs={{0,2},{2,0},{1,3},{3,1},{4,6},{6,4},{5,7},{7,5},{8,10},{10,8},{9,1... | collective-permute-start | bytes 393224 | tf_op jit(solution)/shard_map/ppermute | solution.py:24
  218.6 12.6 %collective-permute-start.11 = (bf16[2,256,128]{2,1,0:T(8,128)(2,1)}, bf16[2,256,128]{2,1,0:T(8,128)(2,1)}, u32[]{:S(2)}, u32[]{:S(2)}) collective-permute-start(bf16[2,256,128]{2,1,0:T(8,128)(2,1)} %fusion.3), channel_id=1, source_target_pairs={{0,1},{1,0},{2,3},{3,2},{4,5},{5,4},{6,7},{7,6},{8,9},{9,8},{10,11... | collective-permute-start | bytes 393224 | tf_op jit(solution)/shard_map/ppermute | solution.py:24
  223.9 20.0 %all-to-all-start.5 = ((bf16[4,256,128]{2,1,0:T(8,128)(2,1)}), bf16[4,256,128]{2,1,0:T(8,128)(2,1)S(1)}, u32[]{:S(2)}, u32[]{:S(2)}) async-start(bf16[4,256,128]{2,1,0:T(8,128)(2,1)} %bitcast.27), calls=%async_computation.5 | async-start | bytes 524288 | tf_op jit(solution)/shard_map/all_to_all | solution.py:28
  (4 other events, 5.5 us)

commit v4 on v3

--- a/solution.py
+++ b/solution.py
@@ -31,9 +31,9 @@
 def extract_kernel(mat, own_meta, other_meta, place, own, other, sent, kept, found, sems):
     def slot(meta, row):
         at, hit = jnp.int32(0), jnp.int32(0)
-        listed = meta[(mat * META + KQ) * RB + row]
+        listed = meta[mat * META + KQ, 0, row]
         for k in range(KQ):
-            here = (meta[(mat * META + k) * RB + row] == place[1]) & (k < listed)
+            here = (meta[mat * META + k, 0, row] == place[1]) & (k < listed)
             at = jnp.where(here, k, at)
             hit = jnp.where(here, 1, hit)
         return at, hit
@@ -60,9 +60,9 @@
 def row_total(mat, row, metas, tiles, slab):
     left, right = [], []
     for side, meta in enumerate(metas):
-        listed = meta[(mat * META + KQ) * RB + row]
+        listed = meta[mat * META + KQ, 0, row]
         for k in range(KQ):
-            j = meta[(mat * META + k) * RB + row]
+            j = meta[mat * META + k, 0, row]
             tile = tiles(side, k)
             left.append(jnp.where(k < listed, tile, jnp.zeros_like(tile)))
             right.append(slab[(((j >> 3) & 3) * 4 + (j >> 5)) * HALF + (j & 3)])
@@ -236,8 +236,10 @@
     ]
 
     def listed(*pairs):
-        parts = [part for columns, counts in pairs for part in (columns[:, 0].T, counts.T)]
-        own = jnp.concatenate(parts).reshape(-1)
+        parts = []
+        for columns, counts in pairs:
+            parts += [columns.transpose(2, 1, 0), counts.T[:, None]]
+        own = jnp.concatenate(parts)
         return own, swapped(own, "c")
 
     def pair(values):

time: 246 us -> 243 us (0.988)
  the two profiles are of different devices: /device:TPU:98 before, /device:TPU:74 now
where the time goes in v4:
time: 243 us; the launch traced here: 241 us
  starting transfers between devices  94.3 us (39%)
  blocking collectives  71.1 us (29%)
  waiting for transfers between devices  33.9 us (14%)
  Pallas kernels  28.6 us (12%)
  local copies, waits for them, and re-layouts  8.48 us (3%)
  other arithmetic  4.1 us (2%)
    all_gather x5, blocking collectives, gathered_z(): return lax.all_gather(piece, 'zl', axis=0, tiled=True)  71.1 us
    ppermute x12, starting transfers between devices, swapped(): return lax.ppermute(value, axis, [(0, 1), (1, 0)])  63 us
    all_to_all x6, starting transfers between devices, spread(): return lax.all_to_all(value, axis, split_axis=0, concat_axis=0, tiled=True)  31.4 us
    pallas_call x9, Pallas kernels, local_call(): pl.pallas_call(kernel, out_shape=outs, in_specs=[pl.BlockSpec(memory_spac...  26.6 us
    ppermute x12, waiting for transfers between devices, swapped(): return lax.ppermute(value, axis, [(0, 1), (1, 0)])  22.9 us
    all_to_all x6, waiting for transfers between devices, spread(): return lax.all_to_all(value, axis, split_axis=0, concat_axis=0, tiled=True)  11 us
    unnamed x35, local copies, waits for them, and re-layouts  8.46 us
  transfers between devices with their start and end apart: 18, of which 8 were waited for; matrix products, arithmetic and copies ran while one was open for 1% of the time, Pallas kernels for 11%

profile of v4, /device:TPU:74, one launch (start us, length us, event | category | flops | bytes accessed | tf_op | source)
XLA Modules:
  0.0 241.5 jit_solution(14781886115113557480)
XLA Ops:
  8.5 10.0 %collective-permute-start.4 = (bf16[4,128,128]{2,1,0:T(8,128)(2,1)S(1)}, bf16[4,128,128]{2,1,0:T(8,128)(2,1)S(1)}, u32[]{:S(2)}, u32[]{:S(2)}) collective-permute-start(bf16[4,128,128]{2,1,0:T(8,128)(2,1)S(1)} %get-tuple-element.12), channel_id=1, source_target_pairs={{0,2},{2,0},{1,3},{3,1},{4,6},{6,4},{5,7},{7,5},{8,10},{10,8},{9,1... | collective-permute-start | bytes 393224 | tf_op jit(solution)/shard_map/ppermute | solution.py:24
  20.5 5.0 %collective-permute-done.4.arrived = bf16[4,128,128]{2,1,0:T(8,128)(2,1)S(1)} collective-permute-done((bf16[4,128,128]{2,1,0:T(8,128)(2,1)S(1)}, bf16[4,128,128]{2,1,0:T(8,128)(2,1)S(1)}, u32[]{:S(2)}, u32[]{:S(2)}) %collective-permute-start.4) | collective-permute-done | bytes 131104 | tf_op jit(solution)/shard_map/ppermute | solution.py:24
  25.5 12.9 %all_gather.15.piece = bf16[16,128,128]{2,1,0:T(8,128)(2,1)S(1)} all-gather(bf16[4,128,128]{2,1,0:T(8,128)(2,1)S(1)} %shard_map.113), channel_id=1, replica_groups=mesh['row'=8,'zl'=4,'x'=4,'zh'=2,'c'=2] {'zl'}, dimensions={0}, use_global_device_ids=true | all-gather | bytes 655360 | tf_op jit(solution)/shard_map/all_gather | solution.py:195
  40.0 5.1 %all-to-all-start = ((bf16[4,16,128,128]{3,2,1,0:T(8,128)(2,1)}), bf16[4,16,128,128]{3,2,1,0:T(8,128)(2,1)}, u32[]{:S(2)}, u32[]{:S(2)}) async-start(bf16[4,16,128,128]{3,2,1,0:T(8,128)(2,1)} %copy-done.1), calls=%async_computation | async-start | bytes 4194304 | tf_op jit(solution)/shard_map/all_to_all | solution.py:28
  51.7 7.4 %collective-permute-start.8 = (bf16[4,128,128]{2,1,0:T(8,128)(2,1)S(1)}, bf16[4,128,128]{2,1,0:T(8,128)(2,1)S(1)}, u32[]{:S(2)}, u32[]{:S(2)}) collective-permute-start(bf16[4,128,128]{2,1,0:T(8,128)(2,1)S(1)} %get-tuple-element.18), channel_id=1, source_target_pairs={{0,2},{2,0},{1,3},{3,1},{4,6},{6,4},{5,7},{7,5},{8,10},{10,8},{9,1... | collective-permute-start | bytes 393224 | tf_op jit(solution)/shard_map/ppermute | solution.py:24
  59.1 6.7 %collective-permute-done.8.arrived = bf16[4,128,128]{2,1,0:T(8,128)(2,1)S(1)} collective-permute-done((bf16[4,128,128]{2,1,0:T(8,128)(2,1)S(1)}, bf16[4,128,128]{2,1,0:T(8,128)(2,1)S(1)}, u32[]{:S(2)}, u32[]{:S(2)}) %collective-permute-start.8) | collective-permute-done | bytes 131104 | tf_op jit(solution)/shard_map/ppermute | solution.py:24
  65.8 13.5 %all_gather.17.piece = bf16[16,128,128]{2,1,0:T(8,128)(2,1)S(1)} all-gather(bf16[4,128,128]{2,1,0:T(8,128)(2,1)S(1)} %shard_map.121), channel_id=1, replica_groups=mesh['row'=8,'zl'=4,'x'=4,'zh'=2,'c'=2] {'zl'}, dimensions={0}, use_global_device_ids=true | all-gather | bytes 655360 | tf_op jit(solution)/shard_map/all_gather | solution.py:195
  80.8 4.8 %all-to-all-start.2 = ((bf16[4,16,128,128]{3,2,1,0:T(8,128)(2,1)}), bf16[4,16,128,128]{3,2,1,0:T(8,128)(2,1)}, u32[]{:S(2)}, u32[]{:S(2)}) async-start(bf16[4,16,128,128]{3,2,1,0:T(8,128)(2,1)} %copy-done.3), calls=%async_computation.2 | async-start | bytes 4194304 | tf_op jit(solution)/shard_map/all_to_all | solution.py:28
  85.6 4.8 %shard_map.115 = (bf16[4,128,128]{2,1,0:T(8,128)(2,1)S(1)}, f32[4,128,128]{2,1,0:T(8,128)S(1)}) custom-call(s32[21,1,8]{2,1,0:T(1,128)S(1)} %constant_dynamic-update-slice_fusion.own_meta, s32[21,1,8]{2,1,0:T(1,128)S(1)} %collective-permute-done.other_meta, s32[2]{0:T(128)S(1)} %pad_add_fusion.1.place, bf16[8,6,128,128]{3,2,1,0:T(8,128)(2,1)} %bitcast.56, ...), custom_call_target="tpu_custom_call" | custom-call | flops 402653184 | bytes 3145728 | tf_op jit(solution)/shard_map/pallas_call | solution.py:114
  90.5 7.2 %collective-permute-start.5 = (bf16[4,128,128]{2,1,0:T(8,128)(2,1)S(1)}, bf16[4,128,128]{2,1,0:T(8,128)(2,1)S(1)}, u32[]{:S(2)}, u32[]{:S(2)}) collective-permute-start(bf16[4,128,128]{2,1,0:T(8,128)(2,1)S(1)} %get-tuple-element.14), channel_id=1, source_target_pairs={{0,2},{2,0},{1,3},{3,1},{4,6},{6,4},{5,7},{7,5},{8,10},{10,8},{9,1... | collective-permute-start | bytes 393224 | tf_op jit(solution)/shard_map/ppermute | solution.py:24
  97.6 3.6 %collective-permute-done.5.arrived = bf16[4,128,128]{2,1,0:T(8,128)(2,1)S(1)} collective-permute-done((bf16[4,128,128]{2,1,0:T(8,128)(2,1)S(1)}, bf16[4,128,128]{2,1,0:T(8,128)(2,1)S(1)}, u32[]{:S(2)}, u32[]{:S(2)}) %collective-permute-start.5) | collective-permute-done | bytes 131104 | tf_op jit(solution)/shard_map/ppermute | solution.py:24
  101.3 15.9 %all_gather.16.piece = bf16[16,128,128]{2,1,0:T(8,128)(2,1)S(1)} all-gather(bf16[4,128,128]{2,1,0:T(8,128)(2,1)S(1)} %shard_map.116), channel_id=1, replica_groups=mesh['row'=8,'zl'=4,'x'=4,'zh'=2,'c'=2] {'zl'}, dimensions={0}, use_global_device_ids=true | all-gather | bytes 655360 | tf_op jit(solution)/shard_map/all_gather | solution.py:195
  118.8 4.6 %all-to-all-start.1 = ((bf16[4,16,128,128]{3,2,1,0:T(8,128)(2,1)}), bf16[4,16,128,128]{3,2,1,0:T(8,128)(2,1)}, u32[]{:S(2)}, u32[]{:S(2)}) async-start(bf16[4,16,128,128]{3,2,1,0:T(8,128)(2,1)} %copy-done.4), calls=%async_computation.1 | async-start | bytes 4194304 | tf_op jit(solution)/shard_map/all_to_all | solution.py:28
  125.6 9.3 %collective-permute-start.9 = (bf16[4,128,128]{2,1,0:T(8,128)(2,1)S(1)}, bf16[4,128,128]{2,1,0:T(8,128)(2,1)S(1)}, u32[]{:S(2)}, u32[]{:S(2)}) collective-permute-start(bf16[4,128,128]{2,1,0:T(8,128)(2,1)S(1)} %shard_map.124), channel_id=1, source_target_pairs={{0,2},{2,0},{1,3},{3,1},{4,6},{6,4},{5,7},{7,5},{8,10},{10,8},{9,1... | collective-permute-start | bytes 393224 | tf_op jit(solution)/shard_map/ppermute | solution.py:24
  139.5 15.0 %all_gather.18.piece = bf16[16,128,128]{2,1,0:T(8,128)(2,1)S(1)} all-gather(bf16[4,128,128]{2,1,0:T(8,128)(2,1)S(1)} %shard_map.125), channel_id=1, replica_groups=mesh['row'=8,'zl'=4,'x'=4,'zh'=2,'c'=2] {'zl'}, dimensions={0}, use_global_device_ids=true | all-gather | bytes 655360 | tf_op jit(solution)/shard_map/all_gather | solution.py:195
  156.1 4.8 %all-to-all-start.3 = ((bf16[4,16,128,128]{3,2,1,0:T(8,128)(2,1)}), bf16[4,16,128,128]{3,2,1,0:T(8,128)(2,1)}, u32[]{:S(2)}, u32[]{:S(2)}) async-start(bf16[4,16,128,128]{3,2,1,0:T(8,128)(2,1)} %copy-done.5), calls=%async_computation.3 | async-start | bytes 4194304 | tf_op jit(solution)/shard_map/all_to_all | solution.py:28
  160.9 4.9 %shard_map.118 = (bf16[4,128,128]{2,1,0:T(8,128)(2,1)S(1)}, f32[4,128,128]{2,1,0:T(8,128)S(1)}) custom-call(s32[21,1,8]{2,1,0:T(1,128)S(1)} %constant_dynamic-update-slice_fusion.own_meta, s32[21,1,8]{2,1,0:T(1,128)S(1)} %collective-permute-done.other_meta, s32[2]{0:T(128)S(1)} %pad_add_fusion.1.place, bf16[8,6,128,128]{3,2,1,0:T(8,128)(2,1)} %bitcast.54, ...), custom_call_target="tpu_custom_call" | custom-call | flops 402653184 | bytes 3145728 | tf_op jit(solution)/shard_map/pallas_call | solution.py:114
  165.8 8.3 %collective-permute-start.6 = (bf16[4,128,128]{2,1,0:T(8,128)(2,1)S(1)}, bf16[4,128,128]{2,1,0:T(8,128)(2,1)S(1)}, u32[]{:S(2)}, u32[]{:S(2)}) collective-permute-start(bf16[4,128,128]{2,1,0:T(8,128)(2,1)S(1)} %get-tuple-element.16), channel_id=1, source_target_pairs={{0,2},{2,0},{1,3},{3,1},{4,6},{6,4},{5,7},{7,5},{8,10},{10,8},{9,1... | collective-permute-start | bytes 393224 | tf_op jit(solution)/shard_map/ppermute | solution.py:24
  174.1 5.1 %collective-permute-done.6.arrived = bf16[4,128,128]{2,1,0:T(8,128)(2,1)S(1)} collective-permute-done((bf16[4,128,128]{2,1,0:T(8,128)(2,1)S(1)}, bf16[4,128,128]{2,1,0:T(8,128)(2,1)S(1)}, u32[]{:S(2)}, u32[]{:S(2)}) %collective-permute-start.6) | collective-permute-done | bytes 131104 | tf_op jit(solution)/shard_map/ppermute | solution.py:24
  179.2 13.8 %all_gather.19.piece = bf16[16,128,128]{2,1,0:T(8,128)(2,1)S(1)} all-gather(bf16[4,128,128]{2,1,0:T(8,128)(2,1)S(1)} %shard_map.119), channel_id=1, replica_groups=mesh['row'=8,'zl'=4,'x'=4,'zh'=2,'c'=2] {'zl'}, dimensions={0}, use_global_device_ids=true | all-gather | bytes 655360 | tf_op jit(solution)/shard_map/all_gather | solution.py:195
  194.5 4.8 %all-to-all-start.4 = ((bf16[4,16,128,128]{3,2,1,0:T(8,128)(2,1)}), bf16[4,16,128,128]{3,2,1,0:T(8,128)(2,1)}, u32[]{:S(2)}, u32[]{:S(2)}) async-start(bf16[4,16,128,128]{3,2,1,0:T(8,128)(2,1)} %copy-done.2), calls=%async_computation.4 | async-start | bytes 4194304 | tf_op jit(solution)/shard_map/all_to_all | solution.py:28
  202.2 8.2 %collective-permute-start.10 = (bf16[4,128,128]{2,1,0:T(8,128)(2,1)}, bf16[4,128,128]{2,1,0:T(8,128)(2,1)}, u32[]{:S(2)}, u32[]{:S(2)}) collective-permute-start(bf16[4,128,128]{2,1,0:T(8,128)(2,1)} %shard_map.128), channel_id=1, source_target_pairs={{0,2},{2,0},{1,3},{3,1},{4,6},{6,4},{5,7},{7,5},{8,10},{10,8},{9,1... | collective-permute-start | bytes 393224 | tf_op jit(solution)/shard_map/ppermute | solution.py:24
  220.7 7.3 %all-to-all-start.5 = ((bf16[4,256,128]{2,1,0:T(8,128)(2,1)}), bf16[4,256,128]{2,1,0:T(8,128)(2,1)S(1)}, u32[]{:S(2)}, u32[]{:S(2)}) async-start(bf16[4,256,128]{2,1,0:T(8,128)(2,1)} %bitcast.23), calls=%async_computation.5 | async-start | bytes 524288 | tf_op jit(solution)/shard_map/all_to_all | solution.py:28
  229.7 11.0 %all-to-all-done.5 = bf16[4,256,128]{2,1,0:T(8,128)(2,1)S(1)} async-done(((bf16[4,256,128]{2,1,0:T(8,128)(2,1)}), bf16[4,256,128]{2,1,0:T(8,128)(2,1)S(1)}, u32[]{:S(2)}, u32[]{:S(2)}) %all-to-all-start.5) | async-done | bytes 262176 | tf_op jit(solution)/shard_map/all_to_all | solution.py:28
  (84 shorter events, 46.6 us)
Async XLA Ops:
  0.6 17.9 %copy-start = (bf16[8,1,6,128,128]{4,3,2,1,0:T(8,128)(2,1)S(1)}, bf16[8,1,6,128,128]{4,3,2,1,0:T(8,128)(2,1)}, u32[]{:S(2)}) copy-start(bf16[8,1,6,128,128]{4,3,2,1,0:T(8,128)(2,1)} %param.15) | copy-start | bytes 4718596
  0.6 6.0 %collective-permute-start.1 = (bf16[8,6,128,128]{3,2,1,0:T(8,128)(2,1)}, bf16[8,6,128,128]{3,2,1,0:T(8,128)(2,1)}, u32[]{:S(2)}, u32[]{:S(2)}) collective-permute-start(bf16[8,6,128,128]{3,2,1,0:T(8,128)(2,1)} %bitcast.52), channel_id=1, source_target_pairs={{0,1},{1,0},{2,3},{3,2},{4,5},{5,4},{6,7},{7,6},{8,9},{9,8},{10,11... | collective-permute-start | bytes 4718600 | tf_op jit(solution)/shard_map/ppermute | solution.py:24
  3.4 3.2 %collective-permute-start.3 = (s32[7,1,8]{2,1,0:T(1,128)S(1)}, s32[7,1,8]{2,1,0:T(1,128)S(1)}, u32[]{:S(2)}, u32[]{:S(2)}) collective-permute-start(s32[7,1,8]{2,1,0:T(1,128)S(1)} %pad_add_fusion.own_meta), channel_id=1, source_target_pairs={{0,1},{1,0},{2,3},{3,2},{4,5},{5,4},{6,7},{7,6},{8,9},{9,8},{10,11... | collective-permute-start | bytes 680 | tf_op jit(solution)/shard_map/ppermute | solution.py:24
  8.5 17.0 %collective-permute-start.4 = (bf16[4,128,128]{2,1,0:T(8,128)(2,1)S(1)}, bf16[4,128,128]{2,1,0:T(8,128)(2,1)S(1)}, u32[]{:S(2)}, u32[]{:S(2)}) collective-permute-start(bf16[4,128,128]{2,1,0:T(8,128)(2,1)S(1)} %get-tuple-element.12), channel_id=1, source_target_pairs={{0,2},{2,0},{1,3},{3,1},{4,6},{6,4},{5,7},{7,5},{8,10},{10,8},{9,1... | collective-permute-start | bytes 393224 | tf_op jit(solution)/shard_map/ppermute | solution.py:24
  18.5 31.0 %collective-permute-start.7 = (bf16[8,6,128,128]{3,2,1,0:T(8,128)(2,1)S(1)}, bf16[8,6,128,128]{3,2,1,0:T(8,128)(2,1)S(1)}, u32[]{:S(2)}, u32[]{:S(2)}) collective-permute-start(bf16[8,6,128,128]{3,2,1,0:T(8,128)(2,1)S(1)} %bitcast.43), channel_id=1, source_target_pairs={{0,1},{1,0},{2,3},{3,2},{4,5},{5,4},{6,7},{7,6},{8,9},{9,8},{10,11... | collective-permute-start | bytes 4718600 | tf_op jit(solution)/shard_map/ppermute | solution.py:24
  40.0 5.1 %copy-start.13 = (s32[8,1]{0,1:T(1,128)S(1)}, s32[8,1]{0,1:T(1,128)}, u32[]{:S(2)}) copy-start(s32[8,1]{0,1:T(1,128)} %param.14) | copy-start | bytes 100
  40.0 5.1 %copy-start.11 = (s32[8,1,6]{0,1,2:T(1,128)S(1)}, s32[8,1,6]{0,1,2:T(1,128)}, u32[]{:S(2)}) copy-start(s32[8,1,6]{0,1,2:T(1,128)} %param.16) | copy-start | bytes 580
  40.0 5.2 %copy-start.14 = (s32[8,1]{0,1:T(1,128)S(1)}, s32[8,1]{0,1:T(1,128)}, u32[]{:S(2)}) copy-start(s32[8,1]{0,1:T(1,128)} %param.17) | copy-start | bytes 100
  40.0 5.2 %copy-start.9 = (s32[8,1,6]{0,1,2:T(1,128)S(1)}, s32[8,1,6]{0,1,2:T(1,128)}, u32[]{:S(2)}) copy-start(s32[8,1,6]{0,1,2:T(1,128)} %param.10) | copy-start | bytes 580
  40.0 5.2 %copy-start.12 = (s32[8,1]{0,1:T(1,128)S(1)}, s32[8,1]{0,1:T(1,128)}, u32[]{:S(2)}) copy-start(s32[8,1]{0,1:T(1,128)} %param.11) | copy-start | bytes 100
  40.0 40.8 %all-to-all-start = ((bf16[4,16,128,128]{3,2,1,0:T(8,128)(2,1)}), bf16[4,16,128,128]{3,2,1,0:T(8,128)(2,1)}, u32[]{:S(2)}, u32[]{:S(2)}) async-start(bf16[4,16,128,128]{3,2,1,0:T(8,128)(2,1)} %copy-done.1), calls=%async_computation | async-start | bytes 4194304 | tf_op jit(solution)/shard_map/all_to_all | solution.py:28
  45.2 4.3 %collective-permute-start = (s32[21,1,8]{2,1,0:T(1,128)S(1)}, s32[21,1,8]{2,1,0:T(1,128)S(1)}, u32[]{:S(2)}, u32[]{:S(2)}) collective-permute-start(s32[21,1,8]{2,1,0:T(1,128)S(1)} %constant_dynamic-update-slice_fusion.own_meta), channel_id=1, source_target_pairs={{0,1},{1,0},{2,3},{3,2},{4,5},{5,4},{6,7},{7,6},{8,9},{9,8},{10,11... | collective-permute-start | bytes 2024 | tf_op jit(solution)/shard_map/ppermute | solution.py:24
  47.1 38.5 %collective-permute-start.2 = (bf16[8,6,128,128]{3,2,1,0:T(8,128)(2,1)}, bf16[8,6,128,128]{3,2,1,0:T(8,128)(2,1)}, u32[]{:S(2)}, u32[]{:S(2)}) collective-permute-start(bf16[8,6,128,128]{3,2,1,0:T(8,128)(2,1)} %bitcast.55), channel_id=1, source_target_pairs={{0,1},{1,0},{2,3},{3,2},{4,5},{5,4},{6,7},{7,6},{8,9},{9,8},{10,11... | collective-permute-start | bytes 4718600 | tf_op jit(solution)/shard_map/ppermute | solution.py:24
  51.7 14.1 %collective-permute-start.8 = (bf16[4,128,128]{2,1,0:T(8,128)(2,1)S(1)}, bf16[4,128,128]{2,1,0:T(8,128)(2,1)S(1)}, u32[]{:S(2)}, u32[]{:S(2)}) collective-permute-start(bf16[4,128,128]{2,1,0:T(8,128)(2,1)S(1)} %get-tuple-element.18), channel_id=1, source_target_pairs={{0,2},{2,0},{1,3},{3,1},{4,6},{6,4},{5,7},{7,5},{8,10},{10,8},{9,1... | collective-permute-start | bytes 393224 | tf_op jit(solution)/shard_map/ppermute | solution.py:24
  80.8 38.0 %all-to-all-start.2 = ((bf16[4,16,128,128]{3,2,1,0:T(8,128)(2,1)}), bf16[4,16,128,128]{3,2,1,0:T(8,128)(2,1)}, u32[]{:S(2)}, u32[]{:S(2)}) async-start(bf16[4,16,128,128]{3,2,1,0:T(8,128)(2,1)} %copy-done.3), calls=%async_computation.2 | async-start | bytes 4194304 | tf_op jit(solution)/shard_map/all_to_all | solution.py:28
  90.5 10.8 %collective-permute-start.5 = (bf16[4,128,128]{2,1,0:T(8,128)(2,1)S(1)}, bf16[4,128,128]{2,1,0:T(8,128)(2,1)S(1)}, u32[]{:S(2)}, u32[]{:S(2)}) collective-permute-start(bf16[4,128,128]{2,1,0:T(8,128)(2,1)S(1)} %get-tuple-element.14), channel_id=1, source_target_pairs={{0,2},{2,0},{1,3},{3,1},{4,6},{6,4},{5,7},{7,5},{8,10},{10,8},{9,1... | collective-permute-start | bytes 393224 | tf_op jit(solution)/shard_map/ppermute | solution.py:24
  118.8 37.4 %all-to-all-start.1 = ((bf16[4,16,128,128]{3,2,1,0:T(8,128)(2,1)}), bf16[4,16,128,128]{3,2,1,0:T(8,128)(2,1)}, u32[]{:S(2)}, u32[]{:S(2)}) async-start(bf16[4,16,128,128]{3,2,1,0:T(8,128)(2,1)} %copy-done.4), calls=%async_computation.1 | async-start | bytes 4194304 | tf_op jit(solution)/shard_map/all_to_all | solution.py:28
  125.6 12.3 %collective-permute-start.9 = (bf16[4,128,128]{2,1,0:T(8,128)(2,1)S(1)}, bf16[4,128,128]{2,1,0:T(8,128)(2,1)S(1)}, u32[]{:S(2)}, u32[]{:S(2)}) collective-permute-start(bf16[4,128,128]{2,1,0:T(8,128)(2,1)S(1)} %shard_map.124), channel_id=1, source_target_pairs={{0,2},{2,0},{1,3},{3,1},{4,6},{6,4},{5,7},{7,5},{8,10},{10,8},{9,1... | collective-permute-start | bytes 393224 | tf_op jit(solution)/shard_map/ppermute | solution.py:24
  156.1 38.4 %all-to-all-start.3 = ((bf16[4,16,128,128]{3,2,1,0:T(8,128)(2,1)}), bf16[4,16,128,128]{3,2,1,0:T(8,128)(2,1)}, u32[]{:S(2)}, u32[]{:S(2)}) async-start(bf16[4,16,128,128]{3,2,1,0:T(8,128)(2,1)} %copy-done.5), calls=%async_computation.3 | async-start | bytes 4194304 | tf_op jit(solution)/shard_map/all_to_all | solution.py:28
  165.8 13.4 %collective-permute-start.6 = (bf16[4,128,128]{2,1,0:T(8,128)(2,1)S(1)}, bf16[4,128,128]{2,1,0:T(8,128)(2,1)S(1)}, u32[]{:S(2)}, u32[]{:S(2)}) collective-permute-start(bf16[4,128,128]{2,1,0:T(8,128)(2,1)S(1)} %get-tuple-element.16), channel_id=1, source_target_pairs={{0,2},{2,0},{1,3},{3,1},{4,6},{6,4},{5,7},{7,5},{8,10},{10,8},{9,1... | collective-permute-start | bytes 393224 | tf_op jit(solution)/shard_map/ppermute | solution.py:24
  194.5 22.8 %all-to-all-start.4 = ((bf16[4,16,128,128]{3,2,1,0:T(8,128)(2,1)}), bf16[4,16,128,128]{3,2,1,0:T(8,128)(2,1)}, u32[]{:S(2)}, u32[]{:S(2)}) async-start(bf16[4,16,128,128]{3,2,1,0:T(8,128)(2,1)} %copy-done.2), calls=%async_computation.4 | async-start | bytes 4194304 | tf_op jit(solution)/shard_map/all_to_all | solution.py:28
  202.2 11.5 %collective-permute-start.10 = (bf16[4,128,128]{2,1,0:T(8,128)(2,1)}, bf16[4,128,128]{2,1,0:T(8,128)(2,1)}, u32[]{:S(2)}, u32[]{:S(2)}) collective-permute-start(bf16[4,128,128]{2,1,0:T(8,128)(2,1)} %shard_map.128), channel_id=1, source_target_pairs={{0,2},{2,0},{1,3},{3,1},{4,6},{6,4},{5,7},{7,5},{8,10},{10,8},{9,1... | collective-permute-start | bytes 393224 | tf_op jit(solution)/shard_map/ppermute | solution.py:24
  215.4 12.7 %collective-permute-start.11 = (bf16[2,256,128]{2,1,0:T(8,128)(2,1)}, bf16[2,256,128]{2,1,0:T(8,128)(2,1)}, u32[]{:S(2)}, u32[]{:S(2)}) collective-permute-start(bf16[2,256,128]{2,1,0:T(8,128)(2,1)} %fusion.3), channel_id=1, source_target_pairs={{0,1},{1,0},{2,3},{3,2},{4,5},{5,4},{6,7},{7,6},{8,9},{9,8},{10,11... | collective-permute-start | bytes 393224 | tf_op jit(solution)/shard_map/ppermute | solution.py:24
  220.7 20.0 %all-to-all-start.5 = ((bf16[4,256,128]{2,1,0:T(8,128)(2,1)}), bf16[4,256,128]{2,1,0:T(8,128)(2,1)S(1)}, u32[]{:S(2)}, u32[]{:S(2)}) async-start(bf16[4,256,128]{2,1,0:T(8,128)(2,1)} %bitcast.23), calls=%async_computation.5 | async-start | bytes 524288 | tf_op jit(solution)/shard_map/all_to_all | solution.py:28
  (9 other events, 14.2 us)

commit v5 on v4

--- a/solution.py
+++ b/solution.py
@@ -84,29 +84,26 @@
         out[r] = total.astype(out.dtype)
 
 
-def halves_kernel(mat, own_meta, other_meta, place, own, other, slab, sent, kept, held, near, sems):
-    slab_copy = pltpu.make_async_copy(slab, near, sems.at[2 * RB])
+def fetched_kernel(mat, own_meta, other_meta, place, own, other, slab, out, held, near, sems):
+    slab_copy = pltpu.make_async_copy(slab, near, sems.at[2 * HALF])
     slab_copy.start()
     copies = []
-    for r in range(RB):
-        row = (place[0] + r) & (RB - 1)
+    for r in range(HALF):
         for side, ref in enumerate((own, other)):
             to = held.at[r, pl.ds(side * KQ, KQ)]
-            copy = pltpu.make_async_copy(ref.at[row], to, sems.at[2 * r + side])
+            copy = pltpu.make_async_copy(ref.at[place[0] + r], to, sems.at[2 * r + side])
             copy.start()
             copies.append(copy)
     slab_copy.wait()
-    for r in range(RB):
+    for r in range(HALF):
         copies[2 * r].wait()
         copies[2 * r + 1].wait()
-        row = (place[0] + r) & (RB - 1)
 
         def tiles(side, k, r=r):
             return held[r, side * KQ + k]
 
-        total = row_total(mat, row, (own_meta, other_meta), tiles, near)
-        out = sent if r < HALF else kept
-        out[r % HALF] = total.astype(out.dtype)
+        total = row_total(mat, place[0] + r, (own_meta, other_meta), tiles, near)
+        out[r] = total.astype(out.dtype)
 
 
 def local_call(kernel, place, metas, operands, spaces, outs, scratch):
@@ -131,7 +128,7 @@
     return jax.ShapeDtypeStruct((count, BS, BS), dtype)
 
 
-HALVES = (rows_of(HALF, jnp.bfloat16), rows_of(HALF, jnp.float32))
+HALVES = (rows_of(HALF, jnp.bfloat16),) * 2
 
 
 def in_hbm(value):
@@ -144,16 +141,16 @@
     return local_call(kernel, places[1], metas, held, [pl.ANY] * 2, HALVES, scratch)
 
 
-def halves(mat, metas, held, slab, places):
+def fetched(mat, metas, held, slab, place, count, dtype):
     scratch = [
-        pltpu.VMEM((RB, 2 * KQ, BS, BS), jnp.bfloat16),
+        pltpu.VMEM((count, 2 * KQ, BS, BS), jnp.bfloat16),
         pltpu.VMEM((64, BS, BS), jnp.bfloat16),
-        pltpu.SemaphoreType.DMA((2 * RB + 1,)),
+        pltpu.SemaphoreType.DMA((2 * count + 1,)),
     ]
-    kernel = functools.partial(halves_kernel, mat)
+    kernel = functools.partial(fetched_kernel, mat)
     operands = [*map(in_hbm, held), slab]
     spaces = [pltpu.HBM, pltpu.HBM, pl.ANY]
-    return local_call(kernel, places[1], metas, operands, spaces, HALVES, scratch)
+    return local_call(kernel, place, metas, operands, spaces, (rows_of(count, dtype),), scratch)[0]
 
 
 def multiplied(mat, metas, held, slab, place, count, dtype):
@@ -249,9 +246,9 @@
     def at_once(pieces):
         return exchanged(pieces[0], lambda: pieces[1])
 
-    def in_turn(mat, held, slab, dtype=jnp.bfloat16):
-        sent = multiplied(mat, metas, held, slab, places[1], HALF, jnp.bfloat16)
-        kept = functools.partial(multiplied, mat, metas, held, slab, places[0], HALF, jnp.float32)
+    def in_turn(rows, mat, held, slab, dtype=jnp.bfloat16):
+        sent = rows(mat, metas, held, slab, places[1], HALF, jnp.bfloat16)
+        kept = functools.partial(rows, mat, metas, held, slab, places[0], HALF, jnp.float32)
         return exchanged(sent, kept, dtype)
 
     root = pair(root_values)
@@ -265,13 +262,13 @@
     density_slab = at_once(extracted(1, metas, density, places))
 
     slab = gathered_x(gathered_z(root_slab))
-    fock_inner = at_once(halves(0, metas, fock, slab, places))
+    fock_inner = in_turn(fetched, 0, fock, slab)
     slab = gathered_x(gathered_z(density_slab))
-    squared = in_turn(1, density, slab)
+    squared = in_turn(multiplied, 1, density, slab)
     slab = gathered_x(gathered_z(fock_inner))
-    fock_slab = at_once(halves(2, metas, root, slab, places))
+    fock_slab = in_turn(fetched, 2, root, slab)
     slab = gathered_x(gathered_z(squared))
-    cubed_term = in_turn(1, density, slab, jnp.float32)
+    cubed_term = in_turn(multiplied, 1, density, slab, jnp.float32)
     purified = 3.0 * squared.astype(jnp.float32) - 2.0 * cubed_term
     slab = gathered_x(gathered_z(fock_slab))
     outs = all_columns([fock_slab, purified.astype(jnp.bfloat16)])

time: 243 us -> 242 us (level)
  the two profiles are of different devices: /device:TPU:74 before, /device:TPU:10 now
where the time goes in v5:
time: 242 us; the launch traced here: 240 us
  starting transfers between devices  92.3 us (38%)
  blocking collectives  80.8 us (33%)
  Pallas kernels  34.4 us (14%)
  waiting for transfers between devices  19 us (8%)
  local copies, waits for them, and re-layouts  8.73 us (4%)
  other arithmetic  4.1 us (2%)
    all_gather x5, blocking collectives, gathered_z(): return lax.all_gather(piece, 'zl', axis=0, tiled=True)  80.8 us
    ppermute x12, starting transfers between devices, swapped(): return lax.ppermute(value, axis, [(0, 1), (1, 0)])  60.9 us
    pallas_call x11, Pallas kernels, local_call(): pl.pallas_call(kernel, out_shape=outs, in_specs=[pl.BlockSpec(memory_spac...  31.5 us
    all_to_all x6, starting transfers between devices, spread(): return lax.all_to_all(value, axis, split_axis=0, concat_axis=0, tiled=True)  31.4 us
    ppermute x12, waiting for transfers between devices, swapped(): return lax.ppermute(value, axis, [(0, 1), (1, 0)])  10.7 us
    unnamed x35, local copies, waits for them, and re-layouts  8.71 us
    all_to_all x6, waiting for transfers between devices, spread(): return lax.all_to_all(value, axis, split_axis=0, concat_axis=0, tiled=True)  8.32 us
  transfers between devices with their start and end apart: 18, of which 6 were waited for; matrix products, arithmetic and copies ran while one was open for 1% of the time, Pallas kernels for 14%

profile of v5, /device:TPU:10, one launch (start us, length us, event | category | flops | bytes accessed | tf_op | source)
XLA Modules:
  0.0 240.5 jit_solution(15040506808658960906)
XLA Ops:
  9.6 10.9 %collective-permute-start.4 = (bf16[4,128,128]{2,1,0:T(8,128)(2,1)S(1)}, bf16[4,128,128]{2,1,0:T(8,128)(2,1)S(1)}, u32[]{:S(2)}, u32[]{:S(2)}) collective-permute-start(bf16[4,128,128]{2,1,0:T(8,128)(2,1)S(1)} %get-tuple-element.8), channel_id=1, source_target_pairs={{0,2},{2,0},{1,3},{3,1},{4,6},{6,4},{5,7},{7,5},{8,10},{10,8},{9,1... | collective-permute-start | bytes 393224 | tf_op jit(solution)/shard_map/ppermute | solution.py:24
  24.7 18.8 %all_gather.15.piece = bf16[16,128,128]{2,1,0:T(8,128)(2,1)S(1)} all-gather(bf16[4,128,128]{2,1,0:T(8,128)(2,1)S(1)} %shard_map.113), channel_id=1, replica_groups=mesh['row'=8,'zl'=4,'x'=4,'zh'=2,'c'=2] {'zl'}, dimensions={0}, use_global_device_ids=true | all-gather | bytes 655360 | tf_op jit(solution)/shard_map/all_gather | solution.py:192
  45.1 5.1 %all-to-all-start = ((bf16[4,16,128,128]{3,2,1,0:T(8,128)(2,1)}), bf16[4,16,128,128]{3,2,1,0:T(8,128)(2,1)}, u32[]{:S(2)}, u32[]{:S(2)}) async-start(bf16[4,16,128,128]{3,2,1,0:T(8,128)(2,1)} %copy-done.1), calls=%async_computation | async-start | bytes 4194304 | tf_op jit(solution)/shard_map/all_to_all | solution.py:28
  56.8 7.3 %collective-permute-start.8 = (bf16[4,128,128]{2,1,0:T(8,128)(2,1)S(1)}, bf16[4,128,128]{2,1,0:T(8,128)(2,1)S(1)}, u32[]{:S(2)}, u32[]{:S(2)}) collective-permute-start(bf16[4,128,128]{2,1,0:T(8,128)(2,1)S(1)} %get-tuple-element.10), channel_id=1, source_target_pairs={{0,2},{2,0},{1,3},{3,1},{4,6},{6,4},{5,7},{7,5},{8,10},{10,8},{9,1... | collective-permute-start | bytes 393224 | tf_op jit(solution)/shard_map/ppermute | solution.py:24
  64.1 4.0 %collective-permute-done.8.arrived = bf16[4,128,128]{2,1,0:T(8,128)(2,1)S(1)} collective-permute-done((bf16[4,128,128]{2,1,0:T(8,128)(2,1)S(1)}, bf16[4,128,128]{2,1,0:T(8,128)(2,1)S(1)}, u32[]{:S(2)}, u32[]{:S(2)}) %collective-permute-start.8) | collective-permute-done | bytes 131104 | tf_op jit(solution)/shard_map/ppermute | solution.py:24
  68.1 16.9 %all_gather.17.piece = bf16[16,128,128]{2,1,0:T(8,128)(2,1)S(1)} all-gather(bf16[4,128,128]{2,1,0:T(8,128)(2,1)S(1)} %shard_map.123), channel_id=1, replica_groups=mesh['row'=8,'zl'=4,'x'=4,'zh'=2,'c'=2] {'zl'}, dimensions={0}, use_global_device_ids=true | all-gather | bytes 655360 | tf_op jit(solution)/shard_map/all_gather | solution.py:192
  86.6 4.6 %all-to-all-start.2 = ((bf16[4,16,128,128]{3,2,1,0:T(8,128)(2,1)}), bf16[4,16,128,128]{3,2,1,0:T(8,128)(2,1)}, u32[]{:S(2)}, u32[]{:S(2)}) async-start(bf16[4,16,128,128]{3,2,1,0:T(8,128)(2,1)} %copy-done.3), calls=%async_computation.2 | async-start | bytes 4194304 | tf_op jit(solution)/shard_map/all_to_all | solution.py:28
  91.2 4.3 %shard_map.116 = bf16[4,128,128]{2,1,0:T(8,128)(2,1)} custom-call(s32[21,1,8]{2,1,0:T(1,128)S(1)} %constant_dynamic-update-slice_fusion.own_meta, s32[21,1,8]{2,1,0:T(1,128)S(1)} %collective-permute-done.other_meta, s32[2]{0:T(128)S(1)} %pad_add_fusion.2.place, bf16[8,6,128,128]{3,2,1,0:T(8,128)(2,1)} %bitcast.58, ...), custom_call_target="tpu_custom_call" | custom-call | flops 201326592 | bytes 1572864 | tf_op jit(solution)/shard_map/pallas_call | solution.py:111
  95.6 7.3 %collective-permute-start.5 = (bf16[4,128,128]{2,1,0:T(8,128)(2,1)}, bf16[4,128,128]{2,1,0:T(8,128)(2,1)}, u32[]{:S(2)}, u32[]{:S(2)}) collective-permute-start(bf16[4,128,128]{2,1,0:T(8,128)(2,1)} %shard_map.116), channel_id=1, source_target_pairs={{0,2},{2,0},{1,3},{3,1},{4,6},{6,4},{5,7},{7,5},{8,10},{10,8},{9,1... | collective-permute-start | bytes 393224 | tf_op jit(solution)/shard_map/ppermute | solution.py:24
  103.0 3.7 %shard_map.115.kept = f32[4,128,128]{2,1,0:T(8,128)S(1)} custom-call(s32[21,1,8]{2,1,0:T(1,128)S(1)} %constant_dynamic-update-slice_fusion.own_meta, s32[21,1,8]{2,1,0:T(1,128)S(1)} %collective-permute-done.other_meta, s32[2]{0:T(128)S(1)} %pad_add_fusion.1.place, bf16[8,6,128,128]{3,2,1,0:T(8,128)(2,1)} %bitcast.59, ...), custom_call_target="tpu_custom_call" | custom-call | flops 201326592 | bytes 1572864 | tf_op jit(solution)/shard_map/pallas_call | solution.py:111
  107.6 15.7 %all_gather.16.piece = bf16[16,128,128]{2,1,0:T(8,128)(2,1)S(1)} all-gather(bf16[4,128,128]{2,1,0:T(8,128)(2,1)S(1)} %shard_map.117), channel_id=1, replica_groups=mesh['row'=8,'zl'=4,'x'=4,'zh'=2,'c'=2] {'zl'}, dimensions={0}, use_global_device_ids=true | all-gather | bytes 655360 | tf_op jit(solution)/shard_map/all_gather | solution.py:192
  124.9 4.8 %all-to-all-start.1 = ((bf16[4,16,128,128]{3,2,1,0:T(8,128)(2,1)}), bf16[4,16,128,128]{3,2,1,0:T(8,128)(2,1)}, u32[]{:S(2)}, u32[]{:S(2)}) async-start(bf16[4,16,128,128]{3,2,1,0:T(8,128)(2,1)} %copy-done.5), calls=%async_computation.1 | async-start | bytes 4194304 | tf_op jit(solution)/shard_map/all_to_all | solution.py:28
  131.9 7.0 %collective-permute-start.9 = (bf16[4,128,128]{2,1,0:T(8,128)(2,1)S(1)}, bf16[4,128,128]{2,1,0:T(8,128)(2,1)S(1)}, u32[]{:S(2)}, u32[]{:S(2)}) collective-permute-start(bf16[4,128,128]{2,1,0:T(8,128)(2,1)S(1)} %shard_map.126), channel_id=1, source_target_pairs={{0,2},{2,0},{1,3},{3,1},{4,6},{6,4},{5,7},{7,5},{8,10},{10,8},{9,1... | collective-permute-start | bytes 393224 | tf_op jit(solution)/shard_map/ppermute | solution.py:24
  141.1 2.9 %collective-permute-done.9.arrived = bf16[4,128,128]{2,1,0:T(8,128)(2,1)S(1)} collective-permute-done((bf16[4,128,128]{2,1,0:T(8,128)(2,1)S(1)}, bf16[4,128,128]{2,1,0:T(8,128)(2,1)S(1)}, u32[]{:S(2)}, u32[]{:S(2)}) %collective-permute-start.9) | collective-permute-done | bytes 131104 | tf_op jit(solution)/shard_map/ppermute | solution.py:24
  144.0 14.8 %all_gather.18.piece = bf16[16,128,128]{2,1,0:T(8,128)(2,1)S(1)} all-gather(bf16[4,128,128]{2,1,0:T(8,128)(2,1)S(1)} %shard_map.127), channel_id=1, replica_groups=mesh['row'=8,'zl'=4,'x'=4,'zh'=2,'c'=2] {'zl'}, dimensions={0}, use_global_device_ids=true | all-gather | bytes 655360 | tf_op jit(solution)/shard_map/all_gather | solution.py:192
  160.4 4.8 %all-to-all-start.3 = ((bf16[4,16,128,128]{3,2,1,0:T(8,128)(2,1)}), bf16[4,16,128,128]{3,2,1,0:T(8,128)(2,1)}, u32[]{:S(2)}, u32[]{:S(2)}) async-start(bf16[4,16,128,128]{3,2,1,0:T(8,128)(2,1)} %copy-done.4), calls=%async_computation.3 | async-start | bytes 4194304 | tf_op jit(solution)/shard_map/all_to_all | solution.py:28
  165.2 3.7 %shard_map.120 = bf16[4,128,128]{2,1,0:T(8,128)(2,1)S(1)} custom-call(s32[21,1,8]{2,1,0:T(1,128)S(1)} %constant_dynamic-update-slice_fusion.own_meta, s32[21,1,8]{2,1,0:T(1,128)S(1)} %collective-permute-done.other_meta, s32[2]{0:T(128)S(1)} %pad_add_fusion.2.place, bf16[8,6,128,128]{3,2,1,0:T(8,128)(2,1)} %bitcast.55, bf16[8,6,128,128]{3,2,1,0:T(8,128)(2,1)} %copy-done.7, ...), custom_call_target="tpu_custom_call" | custom-call | flops 201326592 | bytes 1572864 | tf_op jit(solution)/shard_map/pallas_call | solution.py:111
  168.9 7.5 %collective-permute-start.6 = (bf16[4,128,128]{2,1,0:T(8,128)(2,1)S(1)}, bf16[4,128,128]{2,1,0:T(8,128)(2,1)S(1)}, u32[]{:S(2)}, u32[]{:S(2)}) collective-permute-start(bf16[4,128,128]{2,1,0:T(8,128)(2,1)S(1)} %shard_map.120), channel_id=1, source_target_pairs={{0,2},{2,0},{1,3},{3,1},{4,6},{6,4},{5,7},{7,5},{8,10},{10,8},{9,1... | collective-permute-start | bytes 393224 | tf_op jit(solution)/shard_map/ppermute | solution.py:24
  176.3 3.7 %shard_map.119.kept = f32[4,128,128]{2,1,0:T(8,128)S(1)} custom-call(s32[21,1,8]{2,1,0:T(1,128)S(1)} %constant_dynamic-update-slice_fusion.own_meta, s32[21,1,8]{2,1,0:T(1,128)S(1)} %collective-permute-done.other_meta, s32[2]{0:T(128)S(1)} %pad_add_fusion.1.place, bf16[8,6,128,128]{3,2,1,0:T(8,128)(2,1)} %bitcast.56, bf16[8,6,128,128]{3,2,1,0:T(8,128)(2,1)} %copy-done.7, ...), custom_call_target="tpu_custom_call" | custom-call | flops 201326592 | bytes 1572864 | tf_op jit(solution)/shard_map/pallas_call | solution.py:111
  180.1 14.7 %all_gather.19.piece = bf16[16,128,128]{2,1,0:T(8,128)(2,1)S(1)} all-gather(bf16[4,128,128]{2,1,0:T(8,128)(2,1)S(1)} %shard_map.121), channel_id=1, replica_groups=mesh['row'=8,'zl'=4,'x'=4,'zh'=2,'c'=2] {'zl'}, dimensions={0}, use_global_device_ids=true | all-gather | bytes 655360 | tf_op jit(solution)/shard_map/all_gather | solution.py:192
  196.3 4.8 %all-to-all-start.4 = ((bf16[4,16,128,128]{3,2,1,0:T(8,128)(2,1)}), bf16[4,16,128,128]{3,2,1,0:T(8,128)(2,1)}, u32[]{:S(2)}, u32[]{:S(2)}) async-start(bf16[4,16,128,128]{3,2,1,0:T(8,128)(2,1)} %copy-done.2), calls=%async_computation.4 | async-start | bytes 4194304 | tf_op jit(solution)/shard_map/all_to_all | solution.py:28
  204.0 8.2 %collective-permute-start.10 = (bf16[4,128,128]{2,1,0:T(8,128)(2,1)}, bf16[4,128,128]{2,1,0:T(8,128)(2,1)}, u32[]{:S(2)}, u32[]{:S(2)}) collective-permute-start(bf16[4,128,128]{2,1,0:T(8,128)(2,1)} %shard_map.130), channel_id=1, source_target_pairs={{0,2},{2,0},{1,3},{3,1},{4,6},{6,4},{5,7},{7,5},{8,10},{10,8},{9,1... | collective-permute-start | bytes 393224 | tf_op jit(solution)/shard_map/ppermute | solution.py:24
  222.4 7.3 %all-to-all-start.5 = ((bf16[4,256,128]{2,1,0:T(8,128)(2,1)}), bf16[4,256,128]{2,1,0:T(8,128)(2,1)S(1)}, u32[]{:S(2)}, u32[]{:S(2)}) async-start(bf16[4,256,128]{2,1,0:T(8,128)(2,1)} %bitcast.52), calls=%async_computation.5 | async-start | bytes 524288 | tf_op jit(solution)/shard_map/all_to_all | solution.py:28
  231.4 8.3 %all-to-all-done.5 = bf16[4,256,128]{2,1,0:T(8,128)(2,1)S(1)} async-done(((bf16[4,256,128]{2,1,0:T(8,128)(2,1)}), bf16[4,256,128]{2,1,0:T(8,128)(2,1)S(1)}, u32[]{:S(2)}, u32[]{:S(2)}) %all-to-all-start.5) | async-done | bytes 262176 | tf_op jit(solution)/shard_map/all_to_all | solution.py:28
  (86 shorter events, 48.4 us)
Async XLA Ops:
  0.6 19.9 %copy-start = (bf16[8,1,6,128,128]{4,3,2,1,0:T(8,128)(2,1)S(1)}, bf16[8,1,6,128,128]{4,3,2,1,0:T(8,128)(2,1)}, u32[]{:S(2)}) copy-start(bf16[8,1,6,128,128]{4,3,2,1,0:T(8,128)(2,1)} %param.15) | copy-start | bytes 4718596
  0.6 6.0 %collective-permute-start.1 = (bf16[8,6,128,128]{3,2,1,0:T(8,128)(2,1)}, bf16[8,6,128,128]{3,2,1,0:T(8,128)(2,1)S(1)}, u32[]{:S(2)}, u32[]{:S(2)}) collective-permute-start(bf16[8,6,128,128]{3,2,1,0:T(8,128)(2,1)} %bitcast.53), channel_id=1, source_target_pairs={{0,1},{1,0},{2,3},{3,2},{4,5},{5,4},{6,7},{7,6},{8,9},{9,8},{10,11... | collective-permute-start | bytes 4718600 | tf_op jit(solution)/shard_map/ppermute | solution.py:24
  3.4 3.2 %collective-permute-start.3 = (s32[7,1,8]{2,1,0:T(1,128)S(1)}, s32[7,1,8]{2,1,0:T(1,128)S(1)}, u32[]{:S(2)}, u32[]{:S(2)}) collective-permute-start(s32[7,1,8]{2,1,0:T(1,128)S(1)} %pad_add_fusion.own_meta), channel_id=1, source_target_pairs={{0,1},{1,0},{2,3},{3,2},{4,5},{5,4},{6,7},{7,6},{8,9},{9,8},{10,11... | collective-permute-start | bytes 680 | tf_op jit(solution)/shard_map/ppermute | solution.py:24
  9.6 15.0 %collective-permute-start.4 = (bf16[4,128,128]{2,1,0:T(8,128)(2,1)S(1)}, bf16[4,128,128]{2,1,0:T(8,128)(2,1)S(1)}, u32[]{:S(2)}, u32[]{:S(2)}) collective-permute-start(bf16[4,128,128]{2,1,0:T(8,128)(2,1)S(1)} %get-tuple-element.8), channel_id=1, source_target_pairs={{0,2},{2,0},{1,3},{3,1},{4,6},{6,4},{5,7},{7,5},{8,10},{10,8},{9,1... | collective-permute-start | bytes 393224 | tf_op jit(solution)/shard_map/ppermute | solution.py:24
  20.6 34.1 %collective-permute-start.7 = (bf16[8,6,128,128]{3,2,1,0:T(8,128)(2,1)S(1)}, bf16[8,6,128,128]{3,2,1,0:T(8,128)(2,1)S(1)}, u32[]{:S(2)}, u32[]{:S(2)}) collective-permute-start(bf16[8,6,128,128]{3,2,1,0:T(8,128)(2,1)S(1)} %bitcast.43), channel_id=1, source_target_pairs={{0,1},{1,0},{2,3},{3,2},{4,5},{5,4},{6,7},{7,6},{8,9},{9,8},{10,11... | collective-permute-start | bytes 4718600 | tf_op jit(solution)/shard_map/ppermute | solution.py:24
  45.1 5.1 %copy-start.13 = (s32[8,1]{0,1:T(1,128)S(1)}, s32[8,1]{0,1:T(1,128)}, u32[]{:S(2)}) copy-start(s32[8,1]{0,1:T(1,128)} %param.14) | copy-start | bytes 100
  45.1 5.1 %copy-start.11 = (s32[8,1,6]{0,1,2:T(1,128)S(1)}, s32[8,1,6]{0,1,2:T(1,128)}, u32[]{:S(2)}) copy-start(s32[8,1,6]{0,1,2:T(1,128)} %param.16) | copy-start | bytes 580
  45.1 5.2 %copy-start.14 = (s32[8,1]{0,1:T(1,128)S(1)}, s32[8,1]{0,1:T(1,128)}, u32[]{:S(2)}) copy-start(s32[8,1]{0,1:T(1,128)} %param.17) | copy-start | bytes 100
  45.1 5.2 %copy-start.9 = (s32[8,1,6]{0,1,2:T(1,128)S(1)}, s32[8,1,6]{0,1,2:T(1,128)}, u32[]{:S(2)}) copy-start(s32[8,1,6]{0,1,2:T(1,128)} %param.10) | copy-start | bytes 580
  45.1 5.2 %copy-start.12 = (s32[8,1]{0,1:T(1,128)S(1)}, s32[8,1]{0,1:T(1,128)}, u32[]{:S(2)}) copy-start(s32[8,1]{0,1:T(1,128)} %param.11) | copy-start | bytes 100
  45.1 41.5 %all-to-all-start = ((bf16[4,16,128,128]{3,2,1,0:T(8,128)(2,1)}), bf16[4,16,128,128]{3,2,1,0:T(8,128)(2,1)}, u32[]{:S(2)}, u32[]{:S(2)}) async-start(bf16[4,16,128,128]{3,2,1,0:T(8,128)(2,1)} %copy-done.1), calls=%async_computation | async-start | bytes 4194304 | tf_op jit(solution)/shard_map/all_to_all | solution.py:28
  50.3 4.3 %collective-permute-start = (s32[21,1,8]{2,1,0:T(1,128)S(1)}, s32[21,1,8]{2,1,0:T(1,128)S(1)}, u32[]{:S(2)}, u32[]{:S(2)}) collective-permute-start(s32[21,1,8]{2,1,0:T(1,128)S(1)} %constant_dynamic-update-slice_fusion.own_meta), channel_id=1, source_target_pairs={{0,1},{1,0},{2,3},{3,2},{4,5},{5,4},{6,7},{7,6},{8,9},{9,8},{10,11... | collective-permute-start | bytes 2024 | tf_op jit(solution)/shard_map/ppermute | solution.py:24
  52.2 39.0 %collective-permute-start.2 = (bf16[8,6,128,128]{3,2,1,0:T(8,128)(2,1)}, bf16[8,6,128,128]{3,2,1,0:T(8,128)(2,1)}, u32[]{:S(2)}, u32[]{:S(2)}) collective-permute-start(bf16[8,6,128,128]{3,2,1,0:T(8,128)(2,1)} %bitcast.57), channel_id=1, source_target_pairs={{0,1},{1,0},{2,3},{3,2},{4,5},{5,4},{6,7},{7,6},{8,9},{9,8},{10,11... | collective-permute-start | bytes 4718600 | tf_op jit(solution)/shard_map/ppermute | solution.py:24
  56.8 11.3 %collective-permute-start.8 = (bf16[4,128,128]{2,1,0:T(8,128)(2,1)S(1)}, bf16[4,128,128]{2,1,0:T(8,128)(2,1)S(1)}, u32[]{:S(2)}, u32[]{:S(2)}) collective-permute-start(bf16[4,128,128]{2,1,0:T(8,128)(2,1)S(1)} %get-tuple-element.10), channel_id=1, source_target_pairs={{0,2},{2,0},{1,3},{3,1},{4,6},{6,4},{5,7},{7,5},{8,10},{10,8},{9,1... | collective-permute-start | bytes 393224 | tf_op jit(solution)/shard_map/ppermute | solution.py:24
  86.6 38.3 %all-to-all-start.2 = ((bf16[4,16,128,128]{3,2,1,0:T(8,128)(2,1)}), bf16[4,16,128,128]{3,2,1,0:T(8,128)(2,1)}, u32[]{:S(2)}, u32[]{:S(2)}) async-start(bf16[4,16,128,128]{3,2,1,0:T(8,128)(2,1)} %copy-done.3), calls=%async_computation.2 | async-start | bytes 4194304 | tf_op jit(solution)/shard_map/all_to_all | solution.py:28
  95.6 11.1 %collective-permute-start.5 = (bf16[4,128,128]{2,1,0:T(8,128)(2,1)}, bf16[4,128,128]{2,1,0:T(8,128)(2,1)}, u32[]{:S(2)}, u32[]{:S(2)}) collective-permute-start(bf16[4,128,128]{2,1,0:T(8,128)(2,1)} %shard_map.116), channel_id=1, source_target_pairs={{0,2},{2,0},{1,3},{3,1},{4,6},{6,4},{5,7},{7,5},{8,10},{10,8},{9,1... | collective-permute-start | bytes 393224 | tf_op jit(solution)/shard_map/ppermute | solution.py:24
  124.9 35.5 %all-to-all-start.1 = ((bf16[4,16,128,128]{3,2,1,0:T(8,128)(2,1)}), bf16[4,16,128,128]{3,2,1,0:T(8,128)(2,1)}, u32[]{:S(2)}, u32[]{:S(2)}) async-start(bf16[4,16,128,128]{3,2,1,0:T(8,128)(2,1)} %copy-done.5), calls=%async_computation.1 | async-start | bytes 4194304 | tf_op jit(solution)/shard_map/all_to_all | solution.py:28
  131.9 12.1 %collective-permute-start.9 = (bf16[4,128,128]{2,1,0:T(8,128)(2,1)S(1)}, bf16[4,128,128]{2,1,0:T(8,128)(2,1)S(1)}, u32[]{:S(2)}, u32[]{:S(2)}) collective-permute-start(bf16[4,128,128]{2,1,0:T(8,128)(2,1)S(1)} %shard_map.126), channel_id=1, source_target_pairs={{0,2},{2,0},{1,3},{3,1},{4,6},{6,4},{5,7},{7,5},{8,10},{10,8},{9,1... | collective-permute-start | bytes 393224 | tf_op jit(solution)/shard_map/ppermute | solution.py:24
  160.4 35.9 %all-to-all-start.3 = ((bf16[4,16,128,128]{3,2,1,0:T(8,128)(2,1)}), bf16[4,16,128,128]{3,2,1,0:T(8,128)(2,1)}, u32[]{:S(2)}, u32[]{:S(2)}) async-start(bf16[4,16,128,128]{3,2,1,0:T(8,128)(2,1)} %copy-done.4), calls=%async_computation.3 | async-start | bytes 4194304 | tf_op jit(solution)/shard_map/all_to_all | solution.py:28
  168.9 11.2 %collective-permute-start.6 = (bf16[4,128,128]{2,1,0:T(8,128)(2,1)S(1)}, bf16[4,128,128]{2,1,0:T(8,128)(2,1)S(1)}, u32[]{:S(2)}, u32[]{:S(2)}) collective-permute-start(bf16[4,128,128]{2,1,0:T(8,128)(2,1)S(1)} %shard_map.120), channel_id=1, source_target_pairs={{0,2},{2,0},{1,3},{3,1},{4,6},{6,4},{5,7},{7,5},{8,10},{10,8},{9,1... | collective-permute-start | bytes 393224 | tf_op jit(solution)/shard_map/ppermute | solution.py:24
  196.3 22.8 %all-to-all-start.4 = ((bf16[4,16,128,128]{3,2,1,0:T(8,128)(2,1)}), bf16[4,16,128,128]{3,2,1,0:T(8,128)(2,1)}, u32[]{:S(2)}, u32[]{:S(2)}) async-start(bf16[4,16,128,128]{3,2,1,0:T(8,128)(2,1)} %copy-done.2), calls=%async_computation.4 | async-start | bytes 4194304 | tf_op jit(solution)/shard_map/all_to_all | solution.py:28
  204.0 11.4 %collective-permute-start.10 = (bf16[4,128,128]{2,1,0:T(8,128)(2,1)}, bf16[4,128,128]{2,1,0:T(8,128)(2,1)}, u32[]{:S(2)}, u32[]{:S(2)}) collective-permute-start(bf16[4,128,128]{2,1,0:T(8,128)(2,1)} %shard_map.130), channel_id=1, source_target_pairs={{0,2},{2,0},{1,3},{3,1},{4,6},{6,4},{5,7},{7,5},{8,10},{10,8},{9,1... | collective-permute-start | bytes 393224 | tf_op jit(solution)/shard_map/ppermute | solution.py:24
  217.1 12.7 %collective-permute-start.11 = (bf16[2,256,128]{2,1,0:T(8,128)(2,1)}, bf16[2,256,128]{2,1,0:T(8,128)(2,1)}, u32[]{:S(2)}, u32[]{:S(2)}) collective-permute-start(bf16[2,256,128]{2,1,0:T(8,128)(2,1)} %fusion.3), channel_id=1, source_target_pairs={{0,1},{1,0},{2,3},{3,2},{4,5},{5,4},{6,7},{7,6},{8,9},{9,8},{10,11... | collective-permute-start | bytes 393224 | tf_op jit(solution)/shard_map/ppermute | solution.py:24
  222.4 17.3 %all-to-all-start.5 = ((bf16[4,256,128]{2,1,0:T(8,128)(2,1)}), bf16[4,256,128]{2,1,0:T(8,128)(2,1)S(1)}, u32[]{:S(2)}, u32[]{:S(2)}) async-start(bf16[4,256,128]{2,1,0:T(8,128)(2,1)} %bitcast.52), calls=%async_computation.5 | async-start | bytes 524288 | tf_op jit(solution)/shard_map/all_to_all | solution.py:28
  (9 other events, 14.5 us)

commit v6 on v5

--- a/solution.py
+++ b/solution.py
@@ -28,7 +28,7 @@
     return lax.all_to_all(value, axis, split_axis=0, concat_axis=0, tiled=True)
 
 
-def extract_kernel(mat, own_meta, other_meta, place, own, other, sent, kept, found, sems):
+def extract_kernel(mat, own_meta, other_meta, place, own, other, out, found, sems):
     def slot(meta, row):
         at, hit = jnp.int32(0), jnp.int32(0)
         listed = meta[mat * META + KQ, 0, row]
@@ -39,22 +39,20 @@
         return at, hit
 
     copies, hits = [], []
-    for r in range(RB):
-        row = (place[0] + r) & (RB - 1)
+    for r in range(HALF):
+        row = place[0] + r
         for side, (meta, tiles) in enumerate(((own_meta, own), (other_meta, other))):
             at, hit = slot(meta, row)
             copy = pltpu.make_async_copy(tiles.at[row, at], found.at[r, side], sems.at[r, side])
             copy.start()
             copies.append(copy)
             hits.append(hit)
-    for r in range(RB):
+    for r in range(HALF):
         copies[2 * r].wait()
         copies[2 * r + 1].wait()
         zero = jnp.zeros((BS, BS), found.dtype)
         tile = jnp.where(hits[2 * r] > 0, found[r, 0], zero)
-        tile = jnp.where(hits[2 * r + 1] > 0, found[r, 1], tile)
-        out = sent if r < HALF else kept
-        out[r % HALF] = tile.astype(out.dtype)
+        out[r] = jnp.where(hits[2 * r + 1] > 0, found[r, 1], tile)
 
 
 def row_total(mat, row, metas, tiles, slab):
@@ -128,17 +126,15 @@
     return jax.ShapeDtypeStruct((count, BS, BS), dtype)
 
 
-HALVES = (rows_of(HALF, jnp.bfloat16),) * 2
-
-
 def in_hbm(value):
     return pltpu.with_memory_space_constraint(value, pltpu.HBM)
 
 
-def extracted(mat, metas, held, places):
-    scratch = [pltpu.VMEM((RB, 2, BS, BS), jnp.bfloat16), pltpu.SemaphoreType.DMA((RB, 2))]
+def extracted(mat, metas, held, place):
+    scratch = [pltpu.VMEM((HALF, 2, BS, BS), jnp.bfloat16), pltpu.SemaphoreType.DMA((HALF, 2))]
     kernel = functools.partial(extract_kernel, mat)
-    return local_call(kernel, places[1], metas, held, [pl.ANY] * 2, HALVES, scratch)
+    outs = (rows_of(HALF, jnp.bfloat16),)
+    return local_call(kernel, place, metas, held, [pl.ANY] * 2, outs, scratch)[0]
 
 
 def fetched(mat, metas, held, slab, place, count, dtype):
@@ -243,8 +239,9 @@
         tiles = values[:, 0]
         return tiles, swapped(tiles, "c")
 
-    def at_once(pieces):
-        return exchanged(pieces[0], lambda: pieces[1])
+    def extraction(mat, metas, held):
+        sent = extracted(mat, metas, held, places[1])
+        return exchanged(sent, lambda: extracted(mat, metas, held, places[0]))
 
     def in_turn(rows, mat, held, slab, dtype=jnp.bfloat16):
         sent = rows(mat, metas, held, slab, places[1], HALF, jnp.bfloat16)
@@ -253,13 +250,13 @@
 
     root = pair(root_values)
     root_metas = listed((root_columns, root_counts))
-    root_slab = at_once(extracted(0, root_metas, [*map(in_hbm, root)], places))
+    root_slab = extraction(0, root_metas, [*map(in_hbm, root)])
     density = pair(density_values)
     fock = pair(fock_values)
     metas = listed(
         (fock_columns, fock_counts), (density_columns, density_counts), (root_columns, root_counts)
     )
-    density_slab = at_once(extracted(1, metas, density, places))
+    density_slab = extraction(1, metas, density)
 
     slab = gathered_x(gathered_z(root_slab))
     fock_inner = in_turn(fetched, 0, fock, slab)

time: 242 us -> 239 us (0.988)
  the two profiles are of different devices: /device:TPU:10 before, /device:TPU:114 now
where the time goes in v6:
time: 239 us; the launch traced here: 238 us
  starting transfers between devices  93.8 us (39%)
  blocking collectives  68.8 us (29%)
  Pallas kernels  35.2 us (15%)
  waiting for transfers between devices  26.1 us (11%)
  local copies, waits for them, and re-layouts  8.76 us (4%)
  other arithmetic  4.06 us (2%)
    all_gather x5, blocking collectives, gathered_z(): return lax.all_gather(piece, 'zl', axis=0, tiled=True)  68.8 us
    ppermute x12, starting transfers between devices, swapped(): return lax.ppermute(value, axis, [(0, 1), (1, 0)])  62.3 us
    pallas_call x13, Pallas kernels, local_call(): pl.pallas_call(kernel, out_shape=outs, in_specs=[pl.BlockSpec(memory_spac...  33.2 us
    all_to_all x6, starting transfers between devices, spread(): return lax.all_to_all(value, axis, split_axis=0, concat_axis=0, tiled=True)  31.5 us
    ppermute x12, waiting for transfers between devices, swapped(): return lax.ppermute(value, axis, [(0, 1), (1, 0)])  15.1 us
    all_to_all x6, waiting for transfers between devices, spread(): return lax.all_to_all(value, axis, split_axis=0, concat_axis=0, tiled=True)  11.1 us
    unnamed x37, local copies, waits for them, and re-layouts  8.74 us
  transfers between devices with their start and end apart: 18, of which 7 were waited for; matrix products, arithmetic and copies ran while one was open for 1% of the time, Pallas kernels for 14%

profile of v6, /device:TPU:114, one launch (start us, length us, event | category | flops | bytes accessed | tf_op | source)
XLA Modules:
  0.0 237.8 jit_solution(1592781248785880358)
XLA Ops:
  9.4 10.0 %collective-permute-start.4 = (bf16[4,128,128]{2,1,0:T(8,128)(2,1)S(1)}, bf16[4,128,128]{2,1,0:T(8,128)(2,1)S(1)}, u32[]{:S(2)}, u32[]{:S(2)}) collective-permute-start(bf16[4,128,128]{2,1,0:T(8,128)(2,1)S(1)} %shard_map.113), channel_id=1, source_target_pairs={{0,2},{2,0},{1,3},{3,1},{4,6},{6,4},{5,7},{7,5},{8,10},{10,8},{9,1... | collective-permute-start | bytes 393224 | tf_op jit(solution)/shard_map/ppermute | solution.py:24
  26.4 12.9 %all_gather.15.piece = bf16[16,128,128]{2,1,0:T(8,128)(2,1)S(1)} all-gather(bf16[4,128,128]{2,1,0:T(8,128)(2,1)S(1)} %shard_map.114), channel_id=1, replica_groups=mesh['row'=8,'zl'=4,'x'=4,'zh'=2,'c'=2] {'zl'}, dimensions={0}, use_global_device_ids=true | all-gather | bytes 655360 | tf_op jit(solution)/shard_map/all_gather | solution.py:188
  41.0 5.1 %all-to-all-start = ((bf16[4,16,128,128]{3,2,1,0:T(8,128)(2,1)}), bf16[4,16,128,128]{3,2,1,0:T(8,128)(2,1)}, u32[]{:S(2)}, u32[]{:S(2)}) async-start(bf16[4,16,128,128]{3,2,1,0:T(8,128)(2,1)} %copy-done.1), calls=%async_computation | async-start | bytes 4194304 | tf_op jit(solution)/shard_map/all_to_all | solution.py:28
  52.0 7.4 %collective-permute-start.8 = (bf16[4,128,128]{2,1,0:T(8,128)(2,1)S(1)}, bf16[4,128,128]{2,1,0:T(8,128)(2,1)S(1)}, u32[]{:S(2)}, u32[]{:S(2)}) collective-permute-start(bf16[4,128,128]{2,1,0:T(8,128)(2,1)S(1)} %shard_map.124), channel_id=1, source_target_pairs={{0,2},{2,0},{1,3},{3,1},{4,6},{6,4},{5,7},{7,5},{8,10},{10,8},{9,1... | collective-permute-start | bytes 393224 | tf_op jit(solution)/shard_map/ppermute | solution.py:24
  60.9 5.2 %collective-permute-done.8.arrived = bf16[4,128,128]{2,1,0:T(8,128)(2,1)S(1)} collective-permute-done((bf16[4,128,128]{2,1,0:T(8,128)(2,1)S(1)}, bf16[4,128,128]{2,1,0:T(8,128)(2,1)S(1)}, u32[]{:S(2)}, u32[]{:S(2)}) %collective-permute-start.8) | collective-permute-done | bytes 131104 | tf_op jit(solution)/shard_map/ppermute | solution.py:24
  66.2 13.4 %all_gather.17.piece = bf16[16,128,128]{2,1,0:T(8,128)(2,1)S(1)} all-gather(bf16[4,128,128]{2,1,0:T(8,128)(2,1)S(1)} %shard_map.125), channel_id=1, replica_groups=mesh['row'=8,'zl'=4,'x'=4,'zh'=2,'c'=2] {'zl'}, dimensions={0}, use_global_device_ids=true | all-gather | bytes 655360 | tf_op jit(solution)/shard_map/all_gather | solution.py:188
  81.1 4.7 %all-to-all-start.2 = ((bf16[4,16,128,128]{3,2,1,0:T(8,128)(2,1)}), bf16[4,16,128,128]{3,2,1,0:T(8,128)(2,1)}, u32[]{:S(2)}, u32[]{:S(2)}) async-start(bf16[4,16,128,128]{3,2,1,0:T(8,128)(2,1)} %copy-done.3), calls=%async_computation.2 | async-start | bytes 4194304 | tf_op jit(solution)/shard_map/all_to_all | solution.py:28
  85.8 3.7 %shard_map.117 = bf16[4,128,128]{2,1,0:T(8,128)(2,1)S(1)} custom-call(s32[21,1,8]{2,1,0:T(1,128)S(1)} %constant_dynamic-update-slice_fusion.own_meta, s32[21,1,8]{2,1,0:T(1,128)S(1)} %collective-permute-done.other_meta, s32[2]{0:T(128)S(1)} %pad_add_fusion.2.place, bf16[8,6,128,128]{3,2,1,0:T(8,128)(2,1)} %bitcast.60, ...), custom_call_target="tpu_custom_call" | custom-call | flops 201326592 | bytes 1572864 | tf_op jit(solution)/shard_map/pallas_call | solution.py:109
  89.5 7.3 %collective-permute-start.5 = (bf16[4,128,128]{2,1,0:T(8,128)(2,1)S(1)}, bf16[4,128,128]{2,1,0:T(8,128)(2,1)S(1)}, u32[]{:S(2)}, u32[]{:S(2)}) collective-permute-start(bf16[4,128,128]{2,1,0:T(8,128)(2,1)S(1)} %shard_map.117), channel_id=1, source_target_pairs={{0,2},{2,0},{1,3},{3,1},{4,6},{6,4},{5,7},{7,5},{8,10},{10,8},{9,1... | collective-permute-start | bytes 393224 | tf_op jit(solution)/shard_map/ppermute | solution.py:24
  96.8 3.7 %shard_map.116.kept = f32[4,128,128]{2,1,0:T(8,128)S(1)} custom-call(s32[21,1,8]{2,1,0:T(1,128)S(1)} %constant_dynamic-update-slice_fusion.own_meta, s32[21,1,8]{2,1,0:T(1,128)S(1)} %collective-permute-done.other_meta, s32[2]{0:T(128)S(1)} %pad_add_fusion.1.place, bf16[8,6,128,128]{3,2,1,0:T(8,128)(2,1)} %bitcast.61, ...), custom_call_target="tpu_custom_call" | custom-call | flops 201326592 | bytes 1572864 | tf_op jit(solution)/shard_map/pallas_call | solution.py:109
  100.5 15.7 %all_gather.16.piece = bf16[16,128,128]{2,1,0:T(8,128)(2,1)S(1)} all-gather(bf16[4,128,128]{2,1,0:T(8,128)(2,1)S(1)} %shard_map.118), channel_id=1, replica_groups=mesh['row'=8,'zl'=4,'x'=4,'zh'=2,'c'=2] {'zl'}, dimensions={0}, use_global_device_ids=true | all-gather | bytes 655360 | tf_op jit(solution)/shard_map/all_gather | solution.py:188
  117.8 4.9 %all-to-all-start.1 = ((bf16[4,16,128,128]{3,2,1,0:T(8,128)(2,1)}), bf16[4,16,128,128]{3,2,1,0:T(8,128)(2,1)}, u32[]{:S(2)}, u32[]{:S(2)}) async-start(bf16[4,16,128,128]{3,2,1,0:T(8,128)(2,1)} %copy-done.5), calls=%async_computation.1 | async-start | bytes 4194304 | tf_op jit(solution)/shard_map/all_to_all | solution.py:28
  124.9 8.9 %collective-permute-start.9 = (bf16[4,128,128]{2,1,0:T(8,128)(2,1)S(1)}, bf16[4,128,128]{2,1,0:T(8,128)(2,1)S(1)}, u32[]{:S(2)}, u32[]{:S(2)}) collective-permute-start(bf16[4,128,128]{2,1,0:T(8,128)(2,1)S(1)} %shard_map.128), channel_id=1, source_target_pairs={{0,2},{2,0},{1,3},{3,1},{4,6},{6,4},{5,7},{7,5},{8,10},{10,8},{9,1... | collective-permute-start | bytes 393224 | tf_op jit(solution)/shard_map/ppermute | solution.py:24
  136.0 3.4 %collective-permute-done.9.arrived = bf16[4,128,128]{2,1,0:T(8,128)(2,1)S(1)} collective-permute-done((bf16[4,128,128]{2,1,0:T(8,128)(2,1)S(1)}, bf16[4,128,128]{2,1,0:T(8,128)(2,1)S(1)}, u32[]{:S(2)}, u32[]{:S(2)}) %collective-permute-start.9) | collective-permute-done | bytes 131104 | tf_op jit(solution)/shard_map/ppermute | solution.py:24
  139.4 13.1 %all_gather.18.piece = bf16[16,128,128]{2,1,0:T(8,128)(2,1)S(1)} all-gather(bf16[4,128,128]{2,1,0:T(8,128)(2,1)S(1)} %shard_map.129), channel_id=1, replica_groups=mesh['row'=8,'zl'=4,'x'=4,'zh'=2,'c'=2] {'zl'}, dimensions={0}, use_global_device_ids=true | all-gather | bytes 655360 | tf_op jit(solution)/shard_map/all_gather | solution.py:188
  154.1 4.8 %all-to-all-start.3 = ((bf16[4,16,128,128]{3,2,1,0:T(8,128)(2,1)}), bf16[4,16,128,128]{3,2,1,0:T(8,128)(2,1)}, u32[]{:S(2)}, u32[]{:S(2)}) async-start(bf16[4,16,128,128]{3,2,1,0:T(8,128)(2,1)} %copy-done.4), calls=%async_computation.3 | async-start | bytes 4194304 | tf_op jit(solution)/shard_map/all_to_all | solution.py:28
  158.9 3.7 %shard_map.121 = bf16[4,128,128]{2,1,0:T(8,128)(2,1)S(1)} custom-call(s32[21,1,8]{2,1,0:T(1,128)S(1)} %constant_dynamic-update-slice_fusion.own_meta, s32[21,1,8]{2,1,0:T(1,128)S(1)} %collective-permute-done.other_meta, s32[2]{0:T(128)S(1)} %pad_add_fusion.2.place, bf16[8,6,128,128]{3,2,1,0:T(8,128)(2,1)} %bitcast.57, bf16[8,6,128,128]{3,2,1,0:T(8,128)(2,1)} %copy-done.7, ...), custom_call_target="tpu_custom_call" | custom-call | flops 201326592 | bytes 1572864 | tf_op jit(solution)/shard_map/pallas_call | solution.py:109
  162.6 8.2 %collective-permute-start.6 = (bf16[4,128,128]{2,1,0:T(8,128)(2,1)S(1)}, bf16[4,128,128]{2,1,0:T(8,128)(2,1)S(1)}, u32[]{:S(2)}, u32[]{:S(2)}) collective-permute-start(bf16[4,128,128]{2,1,0:T(8,128)(2,1)S(1)} %shard_map.121), channel_id=1, source_target_pairs={{0,2},{2,0},{1,3},{3,1},{4,6},{6,4},{5,7},{7,5},{8,10},{10,8},{9,1... | collective-permute-start | bytes 393224 | tf_op jit(solution)/shard_map/ppermute | solution.py:24
  170.8 3.7 %shard_map.120.kept = f32[4,128,128]{2,1,0:T(8,128)S(1)} custom-call(s32[21,1,8]{2,1,0:T(1,128)S(1)} %constant_dynamic-update-slice_fusion.own_meta, s32[21,1,8]{2,1,0:T(1,128)S(1)} %collective-permute-done.other_meta, s32[2]{0:T(128)S(1)} %pad_add_fusion.1.place, bf16[8,6,128,128]{3,2,1,0:T(8,128)(2,1)} %bitcast.58, bf16[8,6,128,128]{3,2,1,0:T(8,128)(2,1)} %copy-done.7, ...), custom_call_target="tpu_custom_call" | custom-call | flops 201326592 | bytes 1572864 | tf_op jit(solution)/shard_map/pallas_call | solution.py:109
  176.0 13.6 %all_gather.19.piece = bf16[16,128,128]{2,1,0:T(8,128)(2,1)S(1)} all-gather(bf16[4,128,128]{2,1,0:T(8,128)(2,1)S(1)} %shard_map.122), channel_id=1, replica_groups=mesh['row'=8,'zl'=4,'x'=4,'zh'=2,'c'=2] {'zl'}, dimensions={0}, use_global_device_ids=true | all-gather | bytes 655360 | tf_op jit(solution)/shard_map/all_gather | solution.py:188
  191.2 4.8 %all-to-all-start.4 = ((bf16[4,16,128,128]{3,2,1,0:T(8,128)(2,1)}), bf16[4,16,128,128]{3,2,1,0:T(8,128)(2,1)}, u32[]{:S(2)}, u32[]{:S(2)}) async-start(bf16[4,16,128,128]{3,2,1,0:T(8,128)(2,1)} %copy-done.2), calls=%async_computation.4 | async-start | bytes 4194304 | tf_op jit(solution)/shard_map/all_to_all | solution.py:28
  198.8 7.9 %collective-permute-start.10 = (bf16[4,128,128]{2,1,0:T(8,128)(2,1)}, bf16[4,128,128]{2,1,0:T(8,128)(2,1)}, u32[]{:S(2)}, u32[]{:S(2)}) collective-permute-start(bf16[4,128,128]{2,1,0:T(8,128)(2,1)} %shard_map.132), channel_id=1, source_target_pairs={{0,2},{2,0},{1,3},{3,1},{4,6},{6,4},{5,7},{7,5},{8,10},{10,8},{9,1... | collective-permute-start | bytes 393224 | tf_op jit(solution)/shard_map/ppermute | solution.py:24
  217.1 7.3 %all-to-all-start.5 = ((bf16[4,256,128]{2,1,0:T(8,128)(2,1)}), bf16[4,256,128]{2,1,0:T(8,128)(2,1)S(1)}, u32[]{:S(2)}, u32[]{:S(2)}) async-start(bf16[4,256,128]{2,1,0:T(8,128)(2,1)} %bitcast.53), calls=%async_computation.5 | async-start | bytes 524288 | tf_op jit(solution)/shard_map/all_to_all | solution.py:28
  226.1 11.0 %all-to-all-done.5 = bf16[4,256,128]{2,1,0:T(8,128)(2,1)S(1)} async-done(((bf16[4,256,128]{2,1,0:T(8,128)(2,1)}), bf16[4,256,128]{2,1,0:T(8,128)(2,1)S(1)}, u32[]{:S(2)}, u32[]{:S(2)}) %all-to-all-start.5) | async-done | bytes 262176 | tf_op jit(solution)/shard_map/all_to_all | solution.py:28
  (90 shorter events, 52.5 us)
Async XLA Ops:
  0.6 18.8 %copy-start = (bf16[8,1,6,128,128]{4,3,2,1,0:T(8,128)(2,1)S(1)}, bf16[8,1,6,128,128]{4,3,2,1,0:T(8,128)(2,1)}, u32[]{:S(2)}) copy-start(bf16[8,1,6,128,128]{4,3,2,1,0:T(8,128)(2,1)} %param.15) | copy-start | bytes 4718596
  0.6 6.0 %collective-permute-start.1 = (bf16[8,6,128,128]{3,2,1,0:T(8,128)(2,1)}, bf16[8,6,128,128]{3,2,1,0:T(8,128)(2,1)S(1)}, u32[]{:S(2)}, u32[]{:S(2)}) collective-permute-start(bf16[8,6,128,128]{3,2,1,0:T(8,128)(2,1)} %bitcast.54), channel_id=1, source_target_pairs={{0,1},{1,0},{2,3},{3,2},{4,5},{5,4},{6,7},{7,6},{8,9},{9,8},{10,11... | collective-permute-start | bytes 4718600 | tf_op jit(solution)/shard_map/ppermute | solution.py:24
  3.4 3.2 %collective-permute-start.3 = (s32[7,1,8]{2,1,0:T(1,128)S(1)}, s32[7,1,8]{2,1,0:T(1,128)S(1)}, u32[]{:S(2)}, u32[]{:S(2)}) collective-permute-start(s32[7,1,8]{2,1,0:T(1,128)S(1)} %pad_add_fusion.own_meta), channel_id=1, source_target_pairs={{0,1},{1,0},{2,3},{3,2},{4,5},{5,4},{6,7},{7,6},{8,9},{9,8},{10,11... | collective-permute-start | bytes 680 | tf_op jit(solution)/shard_map/ppermute | solution.py:24
  9.4 17.0 %collective-permute-start.4 = (bf16[4,128,128]{2,1,0:T(8,128)(2,1)S(1)}, bf16[4,128,128]{2,1,0:T(8,128)(2,1)S(1)}, u32[]{:S(2)}, u32[]{:S(2)}) collective-permute-start(bf16[4,128,128]{2,1,0:T(8,128)(2,1)S(1)} %shard_map.113), channel_id=1, source_target_pairs={{0,2},{2,0},{1,3},{3,1},{4,6},{6,4},{5,7},{7,5},{8,10},{10,8},{9,1... | collective-permute-start | bytes 393224 | tf_op jit(solution)/shard_map/ppermute | solution.py:24
  19.5 31.0 %collective-permute-start.7 = (bf16[8,6,128,128]{3,2,1,0:T(8,128)(2,1)S(1)}, bf16[8,6,128,128]{3,2,1,0:T(8,128)(2,1)S(1)}, u32[]{:S(2)}, u32[]{:S(2)}) collective-permute-start(bf16[8,6,128,128]{3,2,1,0:T(8,128)(2,1)S(1)} %bitcast.43), channel_id=1, source_target_pairs={{0,1},{1,0},{2,3},{3,2},{4,5},{5,4},{6,7},{7,6},{8,9},{9,8},{10,11... | collective-permute-start | bytes 4718600 | tf_op jit(solution)/shard_map/ppermute | solution.py:24
  40.9 5.1 %copy-start.12 = (s32[8,1,6]{0,1,2:T(1,128)S(1)}, s32[8,1,6]{0,1,2:T(1,128)}, u32[]{:S(2)}) copy-start(s32[8,1,6]{0,1,2:T(1,128)} %param.16) | copy-start | bytes 580
  40.9 5.2 %copy-start.15 = (s32[8,1]{0,1:T(1,128)S(1)}, s32[8,1]{0,1:T(1,128)}, u32[]{:S(2)}) copy-start(s32[8,1]{0,1:T(1,128)} %param.17) | copy-start | bytes 100
  40.9 5.2 %copy-start.10 = (s32[8,1,6]{0,1,2:T(1,128)S(1)}, s32[8,1,6]{0,1,2:T(1,128)}, u32[]{:S(2)}) copy-start(s32[8,1,6]{0,1,2:T(1,128)} %param.10) | copy-start | bytes 580
  41.0 5.2 %copy-start.13 = (s32[8,1]{0,1:T(1,128)S(1)}, s32[8,1]{0,1:T(1,128)}, u32[]{:S(2)}) copy-start(s32[8,1]{0,1:T(1,128)} %param.11) | copy-start | bytes 100
  41.0 40.2 %all-to-all-start = ((bf16[4,16,128,128]{3,2,1,0:T(8,128)(2,1)}), bf16[4,16,128,128]{3,2,1,0:T(8,128)(2,1)}, u32[]{:S(2)}, u32[]{:S(2)}) async-start(bf16[4,16,128,128]{3,2,1,0:T(8,128)(2,1)} %copy-done.1), calls=%async_computation | async-start | bytes 4194304 | tf_op jit(solution)/shard_map/all_to_all | solution.py:28
  46.2 4.3 %collective-permute-start = (s32[21,1,8]{2,1,0:T(1,128)S(1)}, s32[21,1,8]{2,1,0:T(1,128)S(1)}, u32[]{:S(2)}, u32[]{:S(2)}) collective-permute-start(s32[21,1,8]{2,1,0:T(1,128)S(1)} %constant_dynamic-update-slice_fusion.own_meta), channel_id=1, source_target_pairs={{0,1},{1,0},{2,3},{3,2},{4,5},{5,4},{6,7},{7,6},{8,9},{9,8},{10,11... | collective-permute-start | bytes 2024 | tf_op jit(solution)/shard_map/ppermute | solution.py:24
  48.1 37.7 %collective-permute-start.2 = (bf16[8,6,128,128]{3,2,1,0:T(8,128)(2,1)}, bf16[8,6,128,128]{3,2,1,0:T(8,128)(2,1)}, u32[]{:S(2)}, u32[]{:S(2)}) collective-permute-start(bf16[8,6,128,128]{3,2,1,0:T(8,128)(2,1)} %bitcast.59), channel_id=1, source_target_pairs={{0,1},{1,0},{2,3},{3,2},{4,5},{5,4},{6,7},{7,6},{8,9},{9,8},{10,11... | collective-permute-start | bytes 4718600 | tf_op jit(solution)/shard_map/ppermute | solution.py:24
  52.0 14.1 %collective-permute-start.8 = (bf16[4,128,128]{2,1,0:T(8,128)(2,1)S(1)}, bf16[4,128,128]{2,1,0:T(8,128)(2,1)S(1)}, u32[]{:S(2)}, u32[]{:S(2)}) collective-permute-start(bf16[4,128,128]{2,1,0:T(8,128)(2,1)S(1)} %shard_map.124), channel_id=1, source_target_pairs={{0,2},{2,0},{1,3},{3,1},{4,6},{6,4},{5,7},{7,5},{8,10},{10,8},{9,1... | collective-permute-start | bytes 393224 | tf_op jit(solution)/shard_map/ppermute | solution.py:24
  81.1 36.7 %all-to-all-start.2 = ((bf16[4,16,128,128]{3,2,1,0:T(8,128)(2,1)}), bf16[4,16,128,128]{3,2,1,0:T(8,128)(2,1)}, u32[]{:S(2)}, u32[]{:S(2)}) async-start(bf16[4,16,128,128]{3,2,1,0:T(8,128)(2,1)} %copy-done.3), calls=%async_computation.2 | async-start | bytes 4194304 | tf_op jit(solution)/shard_map/all_to_all | solution.py:28
  89.5 11.0 %collective-permute-start.5 = (bf16[4,128,128]{2,1,0:T(8,128)(2,1)S(1)}, bf16[4,128,128]{2,1,0:T(8,128)(2,1)S(1)}, u32[]{:S(2)}, u32[]{:S(2)}) collective-permute-start(bf16[4,128,128]{2,1,0:T(8,128)(2,1)S(1)} %shard_map.117), channel_id=1, source_target_pairs={{0,2},{2,0},{1,3},{3,1},{4,6},{6,4},{5,7},{7,5},{8,10},{10,8},{9,1... | collective-permute-start | bytes 393224 | tf_op jit(solution)/shard_map/ppermute | solution.py:24
  117.8 36.3 %all-to-all-start.1 = ((bf16[4,16,128,128]{3,2,1,0:T(8,128)(2,1)}), bf16[4,16,128,128]{3,2,1,0:T(8,128)(2,1)}, u32[]{:S(2)}, u32[]{:S(2)}) async-start(bf16[4,16,128,128]{3,2,1,0:T(8,128)(2,1)} %copy-done.5), calls=%async_computation.1 | async-start | bytes 4194304 | tf_op jit(solution)/shard_map/all_to_all | solution.py:28
  124.9 14.5 %collective-permute-start.9 = (bf16[4,128,128]{2,1,0:T(8,128)(2,1)S(1)}, bf16[4,128,128]{2,1,0:T(8,128)(2,1)S(1)}, u32[]{:S(2)}, u32[]{:S(2)}) collective-permute-start(bf16[4,128,128]{2,1,0:T(8,128)(2,1)S(1)} %shard_map.128), channel_id=1, source_target_pairs={{0,2},{2,0},{1,3},{3,1},{4,6},{6,4},{5,7},{7,5},{8,10},{10,8},{9,1... | collective-permute-start | bytes 393224 | tf_op jit(solution)/shard_map/ppermute | solution.py:24
  154.1 37.1 %all-to-all-start.3 = ((bf16[4,16,128,128]{3,2,1,0:T(8,128)(2,1)}), bf16[4,16,128,128]{3,2,1,0:T(8,128)(2,1)}, u32[]{:S(2)}, u32[]{:S(2)}) async-start(bf16[4,16,128,128]{3,2,1,0:T(8,128)(2,1)} %copy-done.4), calls=%async_computation.3 | async-start | bytes 4194304 | tf_op jit(solution)/shard_map/all_to_all | solution.py:28
  162.6 13.4 %collective-permute-start.6 = (bf16[4,128,128]{2,1,0:T(8,128)(2,1)S(1)}, bf16[4,128,128]{2,1,0:T(8,128)(2,1)S(1)}, u32[]{:S(2)}, u32[]{:S(2)}) collective-permute-start(bf16[4,128,128]{2,1,0:T(8,128)(2,1)S(1)} %shard_map.121), channel_id=1, source_target_pairs={{0,2},{2,0},{1,3},{3,1},{4,6},{6,4},{5,7},{7,5},{8,10},{10,8},{9,1... | collective-permute-start | bytes 393224 | tf_op jit(solution)/shard_map/ppermute | solution.py:24
  191.2 22.5 %all-to-all-start.4 = ((bf16[4,16,128,128]{3,2,1,0:T(8,128)(2,1)}), bf16[4,16,128,128]{3,2,1,0:T(8,128)(2,1)}, u32[]{:S(2)}, u32[]{:S(2)}) async-start(bf16[4,16,128,128]{3,2,1,0:T(8,128)(2,1)} %copy-done.2), calls=%async_computation.4 | async-start | bytes 4194304 | tf_op jit(solution)/shard_map/all_to_all | solution.py:28
  198.8 11.1 %collective-permute-start.10 = (bf16[4,128,128]{2,1,0:T(8,128)(2,1)}, bf16[4,128,128]{2,1,0:T(8,128)(2,1)}, u32[]{:S(2)}, u32[]{:S(2)}) collective-permute-start(bf16[4,128,128]{2,1,0:T(8,128)(2,1)} %shard_map.132), channel_id=1, source_target_pairs={{0,2},{2,0},{1,3},{3,1},{4,6},{6,4},{5,7},{7,5},{8,10},{10,8},{9,1... | collective-permute-start | bytes 393224 | tf_op jit(solution)/shard_map/ppermute | solution.py:24
  211.7 12.7 %collective-permute-start.11 = (bf16[2,256,128]{2,1,0:T(8,128)(2,1)}, bf16[2,256,128]{2,1,0:T(8,128)(2,1)}, u32[]{:S(2)}, u32[]{:S(2)}) collective-permute-start(bf16[2,256,128]{2,1,0:T(8,128)(2,1)} %fusion.3), channel_id=1, source_target_pairs={{0,1},{1,0},{2,3},{3,2},{4,5},{5,4},{6,7},{7,6},{8,9},{9,8},{10,11... | collective-permute-start | bytes 393224 | tf_op jit(solution)/shard_map/ppermute | solution.py:24
  213.7 10.7 %copy-start.9 = (bf16[4,128,128]{2,1,0:T(8,128)(2,1)S(1)}, bf16[4,128,128]{2,1,0:T(8,128)(2,1)}, u32[]{:S(2)}) copy-start(bf16[4,128,128]{2,1,0:T(8,128)(2,1)} %copy-done.8) | copy-start | bytes 393220
  217.1 20.0 %all-to-all-start.5 = ((bf16[4,256,128]{2,1,0:T(8,128)(2,1)}), bf16[4,256,128]{2,1,0:T(8,128)(2,1)S(1)}, u32[]{:S(2)}, u32[]{:S(2)}) async-start(bf16[4,256,128]{2,1,0:T(8,128)(2,1)} %bitcast.53), calls=%async_computation.5 | async-start | bytes 524288 | tf_op jit(solution)/shard_map/all_to_all | solution.py:28
  (10 other events, 19.6 us)
